TPU v7x, 32 devices: a whole 2x2x4 slice. The times are simulated.
32 devices in a mesh: zx: 2 (over x), zy: 16 (over z, y, core).
Axes of the slice: x: 2, y: 2, z: 4, core: 2. Of those that a mesh axis runs over, the one named last changes fastest.
Arguments:
- frac: float32 [8, 128, 4096], P(None, 'zx', 'zy'), may hold values from 0 to 1, as said below
- density: float32 [8, 128, 4096], P(None, 'zx', 'zy'), may hold values from 0.5 to 4
- energy: float32 [8, 128, 4096], P(None, 'zx', 'zy'), may hold values from 0.5 to 2
- node_shift: float32 [2, 128, 4096], P(None, 'zx', 'zy'), may hold values from -0.15 to 0.15
- node_speed: float32 [2, 128, 4096], P(None, 'zx', 'zy'), may hold values from -1 to 1
- dest_tile: int32 [2, 16, 256, 1], P('zx', 'zy'), may hold values from 0 to 31; in each aligned block of 256 rows (0 to 255, 256 to 511, ..., all dimensions but the last counted through in order) at most 16 rows name the same one
- src_block: int32 [2, 16, 256], P('zx', 'zy'), may hold values from 0 to 127
- dest_block: int32 [2, 16, 256], P('zx', 'zy'), may hold values from 0 to 127
- crossing: float32 [2, 16, 256], P('zx', 'zy'), may hold values from 0.1 to 0.6
- keep: float32 [2, 16, 128], P('zx', 'zy'), may hold values from 0.3 to 0.9
Outputs:
- remapped: float32 [3, 8, 128, 4096], P(None, None, 'zx', 'zy')
- speed_after: float32 [2, 128, 4096], P(None, 'zx', 'zy')
- shift_after: float32 [2, 128, 4096], P(None, 'zx', 'zy')
Inputs may be any that keep to these rules, and one draw needn't show every extreme that they name: `frac`: at each zone the 8 fractions are positive and sum to one. `dest_tile`: devices are numbered a 16 + b; among the entries of one device at most 16 name the same destination device.
All inputs are finite; a program needn't handle non-finite values.
Results may differ from a plain program's by a relative error of at most 0.00002.
Values sent between devices are 32-bit elements; how exact they have to be, the bound alone decides.
No kernel may reach another device: no remote copies, remote signals or barrier semaphores. Data moves between devices by JAX's collectives and lax.ppermute only.
A program may use at most 64 MiB of HBM per device.

v0:
```python
import jax
import jax.numpy as jnp
from jax import lax
from jax.sharding import PartitionSpec as P

TIME_STEP = 0.02
VISC_COEF = 0.25


def shifted(value, axis, by):
    peers = lax.axis_size(axis)
    return lax.ppermute(value, axis, [(i, (i + by) % peers) for i in range(peers)])


def corner_geometry(corners):
    corner_one, corner_two, corner_three, corner_four = corners
    rise_x = 1.0 + corner_three[0] - corner_one[0]
    rise_y = 1.0 + corner_three[1] - corner_one[1]
    cross_x = -1.0 + corner_four[0] - corner_two[0]
    cross_y = 1.0 + corner_four[1] - corner_two[1]
    return (rise_x, rise_y, cross_x, cross_y)


def zone_area(corners):
    rise_x, rise_y, cross_x, cross_y = corner_geometry(corners)
    return 0.5 * (rise_x * cross_y - cross_x * rise_y)


def zone_phase(frac, density, energy, shifts, speeds):
    rise_x, rise_y, cross_x, cross_y = corner_geometry(shifts)
    area_now = 0.5 * (rise_x * cross_y - cross_x * rise_y)
    speed_one, speed_two, speed_three, speed_four = speeds
    area_rate = 0.5 * (
        (speed_three[0] - speed_one[0]) * cross_y
        + rise_x * (speed_four[1] - speed_two[1])
        - (speed_four[0] - speed_two[0]) * rise_y
        - cross_x * (speed_three[1] - speed_one[1])
    )
    squeeze = jnp.minimum(area_rate / area_now, 0.0)
    gammas = (1.3 + 0.05 * jnp.arange(frac.shape[0], dtype=jnp.int32).astype(jnp.float32))[
        :, None, None
    ]
    mat_pressure = (gammas - 1.0) * density * energy
    zone_density = jnp.sum(frac * density, axis=0)
    viscous = VISC_COEF * zone_density * area_now * squeeze * squeeze
    total_pressure = jnp.sum(frac * mat_pressure, axis=0) + viscous
    half_press = 0.5 * total_pressure
    quarter_mass = 0.25 * zone_density * area_now
    term_one = jnp.stack([-half_press * cross_y, half_press * cross_x, quarter_mass])
    term_two = jnp.stack([half_press * rise_y, -half_press * rise_x, quarter_mass])
    term_three = jnp.stack([half_press * cross_y, -half_press * cross_x, quarter_mass])
    term_four = jnp.stack([-half_press * rise_y, half_press * rise_x, quarter_mass])
    return (area_now, mat_pressure, viscous, (term_one, term_two, term_three, term_four))


def node_update(totals, node_shift, node_speed):
    accel_xy = totals[0:2] / totals[2:3]
    speed_after = node_speed + TIME_STEP * accel_xy
    shift_after = node_shift + TIME_STEP * speed_after
    return (speed_after, shift_after)


def material_state(frac, density, energy, area_now, area_after, mat_pressure, viscous):
    energy_after = energy - (mat_pressure + viscous) * (area_after - area_now) / (
        density * area_now
    )
    volume = frac * area_after
    mass_now = frac * density * area_now
    return jnp.stack([volume, mass_now, mass_now * energy_after])


def upper_along_x(values):
    received = shifted(values[:, 0:1, :], "zx", -1)
    return jnp.concatenate([values, received], axis=1)


def upper_along_y(values):
    received = shifted(values[:, :, 0:1], "zy", -1)
    return jnp.concatenate([values, received], axis=2)


def upper_rim(values):
    return upper_along_y(upper_along_x(values))


def spill_along_x(values):
    received = shifted(values[:, -1:, :], "zx", 1)
    return jnp.concatenate([values[:, 0:1, :] + received, values[:, 1:-1, :]], axis=1)


def spill_along_y(values):
    received = shifted(values[:, :, -1:], "zy", 1)
    return jnp.concatenate([values[:, :, 0:1] + received, values[:, :, 1:-1]], axis=2)


def spill_rim(values):
    return spill_along_y(spill_along_x(values))


def slice_corners(extended):
    return (extended[:, :-1, :-1], extended[:, 1:, :-1], extended[:, 1:, 1:], extended[:, :-1, 1:])


def local(
    frac, density, energy, node_shift, node_speed, dest_tile, src_block, dest_block, crossing, keep
):
    materials, rows_x, rows_y = frac.shape
    node_fields = jnp.concatenate([node_shift, node_speed], axis=0)
    extended = upper_rim(node_fields)
    area_now, mat_pressure, viscous, terms = zone_phase(
        frac, density, energy, slice_corners(extended[0:2]), slice_corners(extended[2:4])
    )
    term_one, term_two, term_three, term_four = terms
    gathered = (
        jnp.pad(term_one, ((0, 0), (0, 1), (0, 1)))
        + jnp.pad(term_two, ((0, 0), (1, 0), (0, 1)))
        + jnp.pad(term_three, ((0, 0), (1, 0), (1, 0)))
        + jnp.pad(term_four, ((0, 0), (0, 1), (1, 0)))
    )
    totals = spill_rim(gathered)
    speed_after, shift_after = node_update(totals, node_shift, node_speed)
    moved_rim = upper_rim(shift_after)
    area_after = zone_area(slice_corners(moved_rim))
    conserved = material_state(frac, density, energy, area_now, area_after, mat_pressure, viscous)
    nblocks = keep.shape[2]
    block_len = rows_x * rows_y // nblocks
    fields = 3 * materials
    blocks = conserved.reshape(fields, nblocks, block_len)
    size_x = lax.axis_size("zx")
    size_y = lax.axis_size("zy")
    devices = size_x * size_y
    targets = dest_tile[0, 0, :, 0]
    sources = src_block[0, 0]
    places = dest_block[0, 0]
    weights = crossing[0, 0]
    entry_count = targets.shape[0]
    capacity = max(2, 2 * entry_count // devices)
    member = (targets[:, None] == jnp.arange(devices, dtype=jnp.int32)[None, :]).astype(jnp.int32)
    before = jnp.cumsum(member, axis=0) - member
    slot_rank = jnp.sum(before * member, axis=1)
    slot_index = targets * capacity + slot_rank
    slot_total = devices * capacity
    matches = slot_index[:, None] == jnp.arange(slot_total, dtype=jnp.int32)[None, :]
    filled = jnp.any(matches, axis=0)
    owners = jnp.sum(
        jnp.where(matches, jnp.arange(entry_count, dtype=jnp.int32)[:, None], 0), axis=0
    )
    slot_weight = jnp.where(filled, weights[owners], 0.0)
    slot_place = jnp.where(filled, places[owners], nblocks)
    payload = blocks[:, sources[owners], :] * slot_weight[None, :, None]
    payload = payload.reshape(fields, size_x, size_y, capacity, block_len)
    place_ids = slot_place.reshape(1, size_x, size_y, capacity)
    arrived, arrived_ids = (
        lax.all_to_all(
            lax.all_to_all(payload, "zx", split_axis=1, concat_axis=1, tiled=True),
            "zy",
            split_axis=2,
            concat_axis=2,
            tiled=True,
        ),
        lax.all_to_all(
            lax.all_to_all(place_ids, "zx", split_axis=1, concat_axis=1, tiled=True),
            "zy",
            split_axis=2,
            concat_axis=2,
            tiled=True,
        ),
    )
    arrived = arrived.reshape(fields, slot_total, block_len)
    arrived_ids = arrived_ids.reshape(slot_total)
    landed = (
        jnp.zeros((fields, nblocks + 1, block_len), jnp.float32).at[:, arrived_ids, :].add(arrived)
    )
    result = blocks * keep[0, 0][None, :, None] + landed[:, :nblocks, :]
    remapped = result.reshape(3, materials, rows_x, rows_y)
    return (remapped, speed_after, shift_after)


def solution(mesh):
    in_specs = (
        P(None, "zx", "zy"),
        P(None, "zx", "zy"),
        P(None, "zx", "zy"),
        P(None, "zx", "zy"),
        P(None, "zx", "zy"),
        P("zx", "zy", None, None),
        P("zx", "zy", None),
        P("zx", "zy", None),
        P("zx", "zy", None),
        P("zx", "zy", None),
    )
    out_specs = (P(None, None, "zx", "zy"), P(None, "zx", "zy"), P(None, "zx", "zy"))
    return jax.shard_map(local, mesh=mesh, in_specs=in_specs, out_specs=out_specs, check_vma=False)
```

profile of v0, /device:TPU:13, one launch (start us, length us, event | category | flops | bytes accessed | tf_op | source)
XLA Modules:
  0.0 337.5 jit_solution(17800876172664507886)
XLA Ops:
  0.7 1.0 constant_dynamic-update-slice_fusion.1
  1.7 0.9 constant_dynamic-update-slice_fusion
  2.6 1.3 collective-permute-start
  3.9 0.7 fusion.38
  5.4 0.8 fusion.37
  7.2 3.5 %gather_fusion = s32[512]{0:T(512)S(1)} fusion(s32[256]{0:T(256)S(1)} %bitcast.65, s32[1024]{0:T(1024)S(1)} %pad_clamp_fusion.1), kind=kCustom, calls=%fused_computation | custom fusion | bytes 6144 | tf_op jit(solution)/shard_map/gather | solution.py:149
  11.5 3.2 all-to-all-start
  14.8 1.0 collective-permute-start.1
  16.0 3.5 %gather_fusion.3 = f32[512]{0:T(512)S(1)} fusion(f32[256]{0:T(256)S(1)} %bitcast.66, s32[1024]{0:T(1024)S(1)} %pad_clamp_fusion.1), kind=kCustom, calls=%fused_computation.3 | custom fusion | bytes 6144 | tf_op jit(solution)/shard_map/gather | solution.py:148
  19.5 0.8 collective-permute-done.1
  20.8 1.5 collective-permute-start.2
  22.5 0.9 collective-permute-done.2
  23.5 2.1 collective-permute-start.3
  25.6 3.5 %gather_fusion.1 = s32[512]{0:T(512)S(1)} fusion(s32[256]{0:T(256)S(1)} %bitcast.67, s32[1024]{0:T(1024)S(1)} %pad_clamp_fusion.1), kind=kCustom, calls=%fused_computation.1 | custom fusion | bytes 6144 | tf_op jit(solution)/shard_map/gather | solution.py:150
  29.2 0.7 multiply_add_fusion
  29.9 1.4 collective-permute-start.4
  31.3 1.0 collective-permute-done.4
  32.5 4.6 %collective-permute-done.5 = f32[2,65,1]{2,1,0:T(8,128)S(1)} collective-permute-done((f32[2,65,1]{2,1,0:T(8,128)S(1)}, f32[2,65,1]{2,1,0:T(8,128)S(1)}, u32[]{:S(2)}, u32[]{:S(2)}) %collective-permute-start.5) | collective-permute-done | bytes 552 | tf_op jit(solution)/shard_map/ppermute | solution.py:12
  37.7 0.9 copy.47
  38.6 3.8 %gather_fusion.2 = f32[512,24,128]{2,1,0:T(8,128)} fusion(f32[24,128,128]{2,0,1:T(8,128)S(1)} %copy.47, s32[1024]{0:T(1024)S(1)} %pad_clamp_fusion), kind=kCustom, calls=%fused_computation.2 | custom fusion | bytes 12584960 | tf_op jit(solution)/shard_map/gather | solution.py:150
  42.4 4.9 %broadcast_multiply_fusion = f32[24,2,16,16,128]{4,0,3,2,1:T(8,128)} fusion(f32[24,2,16,16,128]{4,0,3,2,1:T(8,128)} %bitcast.69, f32[2,16,16]{2,1,0:T(8,128)S(1)} %select_n.68), kind=kLoop, calls=%fused_computation.5 | loop fusion | flops 1572864 | bytes 12584960 | tf_op jit(solution)/shard_map/mul | solution.py:150
  47.3 6.3 %all-to-all-start.2 = ((f32[24,2,16,16,128]{4,0,3,2,1:T(8,128)}), f32[24,2,16,16,128]{4,0,3,2,1:T(8,128)}, u32[]{:S(2)}, u32[]{:S(2)}) async-start(f32[24,2,16,16,128]{4,0,3,2,1:T(8,128)} %broadcast_multiply_fusion), calls=%async_computation.2 | async-start | bytes 12582912 | tf_op jit(solution)/shard_map/all_to_all | solution.py:155
  55.5 66.4 %all-to-all-done.2 = f32[24,2,16,16,128]{4,0,3,2,1:T(8,128)} async-done(((f32[24,2,16,16,128]{4,0,3,2,1:T(8,128)}), f32[24,2,16,16,128]{4,0,3,2,1:T(8,128)}, u32[]{:S(2)}, u32[]{:S(2)}) %all-to-all-start.2) | async-done | bytes 6291488 | tf_op jit(solution)/shard_map/all_to_all | solution.py:155
  121.9 8.5 %all-to-all-start.1 = ((s32[1,2,16,16]{3,1,0,2:T(2,128)}), s32[1,2,16,16]{3,1,0,2:T(2,128)S(1)}, u32[]{:S(2)}, u32[]{:S(2)}) async-start(s32[1,2,16,16]{3,1,0,2:T(2,128)} %copy.49), calls=%async_computation.1 | async-start | bytes 32768 | tf_op jit(solution)/shard_map/all_to_all | solution.py:161
  130.4 6.1 %copy.52 = f32[24,2,16,16,128]{4,0,3,1,2:T(8,128)} copy(f32[24,2,16,16,128]{4,0,3,2,1:T(8,128)} %all-to-all-done.2) | data formatting | bytes 12582912 | tf_op jit(solution)/shard_map/all_to_all | solution.py:155
  136.5 6.1 %all-to-all-start.3 = ((f32[24,2,16,16,128]{4,0,3,1,2:T(8,128)}), f32[24,2,16,16,128]{4,0,3,1,2:T(8,128)}, u32[]{:S(2)}, u32[]{:S(2)}) async-start(f32[24,2,16,16,128]{4,0,3,1,2:T(8,128)} %copy.52), calls=%async_computation.3 | async-start | bytes 12582912 | tf_op jit(solution)/shard_map/all_to_all | solution.py:154
  142.7 137.3 %all-to-all-done.3 = f32[24,2,16,16,128]{4,0,3,1,2:T(8,128)} async-done(((f32[24,2,16,16,128]{4,0,3,1,2:T(8,128)}), f32[24,2,16,16,128]{4,0,3,1,2:T(8,128)}, u32[]{:S(2)}, u32[]{:S(2)}) %all-to-all-start.3) | async-done | bytes 6291488 | tf_op jit(solution)/shard_map/all_to_all | solution.py:154
  280.0 4.0 %copy.53 = f32[24,2,16,16,128]{4,3,2,1,0:T(8,128)S(1)} copy(f32[24,2,16,16,128]{4,0,3,1,2:T(8,128)} %all-to-all-done.3) | data formatting | bytes 12582912 | tf_op jit(solution)/shard_map/all_to_all | solution.py:154
  284.0 6.3 %copy.54 = f32[512,24,128]{2,1,0:T(8,128)} copy(f32[512,24,128]{2,0,1:T(8,128)S(1)} %bitcast.68) | data formatting | bytes 12582912 | tf_op jit(solution)/shard_map/reshape | solution.py:169
  290.4 44.1 %scatter_fusion = f32[24,129,128]{2,0,1:T(8,128)S(1)} fusion(f32[24,129,128]{2,0,1:T(8,128)S(1)} %broadcast_in_dim.23, s32[512]{0:T(512)S(1)} %bitcast.78, f32[512,24,128]{2,1,0:T(8,128)} %copy.54), kind=kCustom, calls=%fused_computation.4 | custom fusion | flops 1572864 | bytes 18876416 | tf_op jit(solution)/shard_map/scatter-add | solution.py:172
  334.5 1.0 slice_add_fusion
  335.9 1.6 reshape.168
  (73 shorter events, 6.8 us)
Async XLA Ops:
  0.6 6.6 %copy-start = (s32[1,1,256]{2,1,0:T(1,128)S(1)}, s32[1,1,256]{2,1,0:T(1,128)}, u32[]{:S(2)}) copy-start(s32[1,1,256]{2,1,0:T(1,128)} %param.17) | copy-start | bytes 3076
  0.6 15.1 %copy-start.4 = (f32[8,64,256]{2,1,0:T(8,128)S(1)}, f32[8,64,256]{2,1,0:T(8,128)}, u32[]{:S(2)}) copy-start(f32[8,64,256]{2,1,0:T(8,128)} %param.10) | copy-start | bytes 1572868
  0.7 15.1 %copy-start.6 = (f32[8,64,256]{2,1,0:T(8,128)S(1)}, f32[8,64,256]{2,1,0:T(8,128)}, u32[]{:S(2)}) copy-start(f32[8,64,256]{2,1,0:T(8,128)} %param.11) | copy-start | bytes 1572868
  0.7 15.1 %copy-start.5 = (f32[8,64,256]{2,1,0:T(8,128)S(1)}, f32[8,64,256]{2,1,0:T(8,128)}, u32[]{:S(2)}) copy-start(f32[8,64,256]{2,1,0:T(8,128)} %param.12) | copy-start | bytes 1572868
  2.6 12.1 %collective-permute-start = (f32[4,1,256]{2,1,0:T(1,128)S(1)}, f32[4,1,256]{2,1,0:T(1,128)S(1)}, u32[]{:S(2)}, u32[]{:S(2)}) collective-permute-start(f32[4,1,256]{2,1,0:T(1,128)S(1)} %slice.223), channel_id=1, source_target_pairs={{0,16},{16,0},{1,17},{17,1},{2,18},{18,2},{3,19},{19,3},{4,20},{20... | collective-permute-start | bytes 12296 | tf_op jit(solution)/shard_map/ppermute | solution.py:12
  10.7 5.3 %copy-start.1 = (f32[1,1,256]{2,1,0:T(1,128)S(1)}, f32[1,1,256]{2,1,0:T(1,128)}, u32[]{:S(2)}) copy-start(f32[1,1,256]{2,1,0:T(1,128)} %param.18) | copy-start | bytes 3076
  11.5 35.8 %all-to-all-start = ((s32[2,1,256]{2,1,0:T(1,128)}), s32[2,1,256]{2,1,0:T(1,128)S(1)}, u32[]{:S(2)}, u32[]{:S(2)}) async-start(s32[2,1,256]{2,1,0:T(1,128)} %reshape.210), calls=%async_computation | async-start | bytes 4096 | tf_op jit(solution)/shard_map/all_to_all | solution.py:162
  14.8 5.5 %collective-permute-start.1 = (f32[4,65,1]{2,1,0:T(8,128)S(1)}, f32[4,65,1]{2,1,0:T(8,128)S(1)}, u32[]{:S(2)}, u32[]{:S(2)}) collective-permute-start(f32[4,65,1]{2,1,0:T(8,128)S(1)} %fusion.2), channel_id=1, source_target_pairs={{0,15},{1,0},{2,1},{3,2},{4,3},{5,4},{6,5},{7,6},{8,7},{9,8},{10,9... | collective-permute-start | bytes 3128 | tf_op jit(solution)/shard_map/ppermute | solution.py:12
  16.0 4.4 %copy-start.7 = (f32[2,64,256]{2,1,0:T(8,128)S(1)}, f32[2,64,256]{2,1,0:T(8,128)}, u32[]{:S(2)}) copy-start(f32[2,64,256]{2,1,0:T(8,128)} %param.14) | copy-start | bytes 393220
  16.0 4.4 %copy-start.8 = (f32[2,64,256]{2,1,0:T(8,128)S(1)}, f32[2,64,256]{2,1,0:T(8,128)}, u32[]{:S(2)}) copy-start(f32[2,64,256]{2,1,0:T(8,128)} %param.13) | copy-start | bytes 393220
  20.7 4.9 %copy-start.2 = (s32[1,1,256]{2,1,0:T(1,128)S(1)}, s32[1,1,256]{2,1,0:T(1,128)}, u32[]{:S(2)}) copy-start(s32[1,1,256]{2,1,0:T(1,128)} %param.16) | copy-start | bytes 3076
  20.8 2.6 collective-permute-start.2
  23.5 5.6 %collective-permute-start.3 = (f32[3,64,1]{2,1,0:T(8,128)S(1)}, f32[3,64,1]{2,1,0:T(8,128)S(1)}, u32[]{:S(2)}, u32[]{:S(2)}) collective-permute-start(f32[3,64,1]{2,1,0:T(8,128)S(1)} %fusion.5), channel_id=1, source_target_pairs={{0,1},{1,2},{2,3},{3,4},{4,5},{5,6},{6,7},{7,8},{8,9},{9,10},{10,1... | collective-permute-start | bytes 2312 | tf_op jit(solution)/shard_map/ppermute | solution.py:12
  29.9 7.6 %copy-start.3 = (f32[2,64,256]{2,1,0:T(8,128)}, f32[2,64,256]{2,1,0:T(8,128)S(1)}, u32[]{:S(2)}) copy-start(f32[2,64,256]{2,1,0:T(8,128)S(1)} %get-tuple-element.7) | copy-start | bytes 393220
  29.9 2.4 collective-permute-start.4
  32.3 4.7 %collective-permute-start.5 = (f32[2,65,1]{2,1,0:T(8,128)S(1)}, f32[2,65,1]{2,1,0:T(8,128)S(1)}, u32[]{:S(2)}, u32[]{:S(2)}) collective-permute-start(f32[2,65,1]{2,1,0:T(8,128)S(1)} %fusion.8), channel_id=1, source_target_pairs={{0,15},{1,0},{2,1},{3,2},{4,3},{5,4},{6,5},{7,6},{8,7},{9,8},{10,9... | collective-permute-start | bytes 1568 | tf_op jit(solution)/shard_map/ppermute | solution.py:12
  47.3 74.5 %all-to-all-start.2 = ((f32[24,2,16,16,128]{4,0,3,2,1:T(8,128)}), f32[24,2,16,16,128]{4,0,3,2,1:T(8,128)}, u32[]{:S(2)}, u32[]{:S(2)}) async-start(f32[24,2,16,16,128]{4,0,3,2,1:T(8,128)} %broadcast_multiply_fusion), calls=%async_computation.2 | async-start | bytes 12582912 | tf_op jit(solution)/shard_map/all_to_all | solution.py:155
  121.9 14.7 %all-to-all-start.1 = ((s32[1,2,16,16]{3,1,0,2:T(2,128)}), s32[1,2,16,16]{3,1,0,2:T(2,128)S(1)}, u32[]{:S(2)}, u32[]{:S(2)}) async-start(s32[1,2,16,16]{3,1,0,2:T(2,128)} %copy.49), calls=%async_computation.1 | async-start | bytes 32768 | tf_op jit(solution)/shard_map/all_to_all | solution.py:161
  136.5 143.5 %all-to-all-start.3 = ((f32[24,2,16,16,128]{4,0,3,1,2:T(8,128)}), f32[24,2,16,16,128]{4,0,3,1,2:T(8,128)}, u32[]{:S(2)}, u32[]{:S(2)}) async-start(f32[24,2,16,16,128]{4,0,3,1,2:T(8,128)} %copy.52), calls=%async_computation.3 | async-start | bytes 12582912 | tf_op jit(solution)/shard_map/all_to_all | solution.py:154
  290.4 44.2 %copy-start.9 = (f32[1,1,128]{2,1,0:T(1,128)S(1)}, f32[1,1,128]{2,1,0:T(1,128)}, u32[]{:S(2)}) copy-start(f32[1,1,128]{2,1,0:T(1,128)} %param.19) | copy-start | bytes 1540
where the time goes:
time: 339 us; the launch traced here: 337 us
  waiting for transfers between devices  211 us (62%)
  other arithmetic  56 us (17%)
  local copies, waits for them, and re-layouts  38.1 us (11%)
  starting transfers between devices  31.4 us (9%)
    all_to_all x1, waiting for transfers between devices, local(): lax.all_to_all(lax.all_to_all(payload, 'zx', split_axis=1, concat_axis=1,...  137 us
    all_to_all x1, waiting for transfers between devices, local(): lax.all_to_all(payload, 'zx', split_axis=1, concat_axis=1, tiled=True)  66.4 us
    scatter-add x1, other arithmetic, local(): jnp.zeros((fields, nblocks + 1, block_len), jnp.float32)  44.1 us
    all_to_all x1, starting transfers between devices, local(): lax.all_to_all(lax.all_to_all(place_ids, 'zx', split_axis=1, concat_axis=...  8.53 us
    ppermute x6, starting transfers between devices, shifted(): lax.ppermute(value, axis, [(i, (i + by) % peers) for i in range(peers)])  7.34 us
    gather x2, local copies, waits for them, and re-layouts, local(): payload = blocks[:, sources[owners], :] * slot_weight[None, :, None]  7.31 us
    ppermute x6, waiting for transfers between devices, shifted(): lax.ppermute(value, axis, [(i, (i + by) % peers) for i in range(peers)])  7.19 us
  transfers between devices with their start and end apart: 10, of which 6 were waited for; matrix products, arithmetic and copies ran while one was open for 10% of the time, Pallas kernels for 0%

commit v1 on v0

--- a/solution.py
+++ b/solution.py
@@ -1,6 +1,9 @@
 import jax
 import jax.numpy as jnp
+import numpy as np
 from jax import lax
+from jax.experimental import pallas as pl
+from jax.experimental.pallas import tpu as pltpu
 from jax.sharding import PartitionSpec as P
 
 TIME_STEP = 0.02
@@ -101,7 +104,315 @@
     return (extended[:, :-1, :-1], extended[:, 1:, :-1], extended[:, 1:, 1:], extended[:, :-1, 1:])
 
 
-def local(
+SUB = 8
+LANES = 128
+QUAD = 4
+
+
+def lower_half(shape):
+    return lax.broadcasted_iota(jnp.int32, shape, len(shape) - 2) % SUB < QUAD
+
+
+def zones_first(field):
+    return jnp.concatenate([field[:, :LANES], field[:, LANES:]], axis=0).T
+
+
+def pair_to_pieces(first, second, low):
+    even = jnp.where(low, first, pltpu.roll(second, QUAD, 0))
+    odd = jnp.where(low, pltpu.roll(first, QUAD, 0), second)
+    return even, odd
+
+
+def pack_kernel(frac_ref, density_ref, energy_ref, out_ref):
+    low = lower_half((SUB, LANES))
+    for group, ref in enumerate((frac_ref, density_ref, energy_ref)):
+        for pair in range(ref.shape[0] // 2):
+            first, second = zones_first(ref[2 * pair]), zones_first(ref[2 * pair + 1])
+            row = SUB * (group * (ref.shape[0] // 2) + pair)
+            for octet in range(LANES // SUB):
+                at = slice(SUB * octet, SUB * octet + SUB)
+                even, odd = pair_to_pieces(first[at], second[at], low)
+                out_ref[2 * octet, row : row + SUB, :] = even
+                out_ref[2 * octet + 1, row : row + SUB, :] = odd
+
+
+def split3(value):
+    high = value.astype(jnp.bfloat16)
+    left = value - high.astype(jnp.float32)
+    middle = left.astype(jnp.bfloat16)
+    low = (left - middle.astype(jnp.float32)).astype(jnp.bfloat16)
+    return high, middle, low
+
+
+def table_kernel(me_ref, target_ref, source_ref, place_ref, weight_ref, out_ref):
+    entries = target_ref.shape[0]
+    capacity = LANES // SUB
+    me = me_ref[0, 0]
+    target = target_ref[...]
+    down = lax.broadcasted_iota(jnp.int32, (entries, entries), 0)
+    across = lax.broadcasted_iota(jnp.int32, (entries, entries), 1)
+    column = target.astype(jnp.float32)
+    row = jnp.sum(jnp.where(down == across, column, 0.0), axis=0, keepdims=True)
+    earlier = (row == column) & (across < down)
+    rank = jnp.sum(jnp.where(earlier, 1.0, 0.0), axis=1, keepdims=True).astype(jnp.int32)
+    slot = (target >> 3) * LANES + ((target & 7) ^ (me & 7)) * capacity + rank
+    slots = 4 * LANES
+    hot = jnp.where(lax.broadcasted_iota(jnp.int32, (entries, slots), 1) == slot, 1.0, 0.0)
+    weight = weight_ref[...]
+    source, place = source_ref[...], place_ref[...]
+    source = ((source & 1) * 64 + (source >> 1)).astype(jnp.float32).astype(jnp.bfloat16)
+    place = ((place & 1) * 64 + (place >> 1)).astype(jnp.float32).astype(jnp.bfloat16)
+    parts = [part.astype(jnp.float32) for part in (*split3(weight), source, place)]
+    values = jnp.concatenate(parts + [jnp.zeros((SUB - len(parts), entries), jnp.float32)], axis=0)
+    tables = jnp.dot(
+        values.astype(jnp.bfloat16), hot.astype(jnp.bfloat16), preferred_element_type=jnp.float32
+    )
+    weights = tables[0:1] + tables[1:2] + tables[2:3]
+    for octet in range(4):
+        at = slice(LANES * octet, LANES * octet + LANES)
+        out_ref[octet : octet + 1, :] = jnp.zeros((1, LANES), jnp.float32)
+        out_ref[4 + octet : 5 + octet, :] = tables[3:4, at]
+        out_ref[8 + octet : 9 + octet, :] = weights[:, at]
+        out_ref[12 + octet : 13 + octet, :] = tables[4:5, at]
+
+
+def extras_kernel(area_ref, after_ref, viscous_ref, tables_ref, out_ref):
+    low = lower_half((SUB, LANES))
+    area, after = zones_first(area_ref[...]), zones_first(after_ref[...])
+    viscous = zones_first(viscous_ref[...])
+    first, second = tables_ref[0:8], tables_ref[8:16]
+    for octet in range(LANES // SUB):
+        at = slice(SUB * octet, SUB * octet + SUB)
+        even, odd = pair_to_pieces(area[at], after[at], low)
+        out_ref[2 * octet, 0:8, :] = even
+        out_ref[2 * octet + 1, 0:8, :] = odd
+        out_ref[2 * octet, 8:16, :] = jnp.where(low, viscous[at], first)
+        out_ref[2 * octet + 1, 8:16, :] = jnp.where(low, pltpu.roll(viscous[at], QUAD, 0), first)
+        out_ref[2 * octet, 16:24, :] = second
+        out_ref[2 * octet + 1, 16:24, :] = second
+
+
+def crossing_kernel(raw_ref, extra_ref, out_ref, state_ref, slots_ref, places_ref):
+    devices, rows, lanes = raw_ref.shape
+    tiles = rows // SUB
+    pairs = tiles // 3
+    low = lower_half((SUB, LANES))
+    gammas = (np.float32(1.3) + np.float32(0.05) * np.arange(2 * pairs, dtype=np.float32)) - np.float32(1.0)
+
+    def conserve(source, carry):
+        area_pair, viscous_pair = extra_ref[source, 0:8], extra_ref[source, 8:16]
+        area_swap = pltpu.roll(area_pair, QUAD, 0)
+        area, after = jnp.where(low, area_pair, area_swap), jnp.where(low, area_swap, area_pair)
+        viscous = jnp.where(low, viscous_pair, pltpu.roll(viscous_pair, QUAD, 0))
+        change = after - area
+        for pair in range(pairs):
+            at = [slice(SUB * (pair + pairs * group), SUB * (pair + pairs * group) + SUB) for group in range(3)]
+            frac, density, energy = raw_ref[source, at[0]], raw_ref[source, at[1]], raw_ref[source, at[2]]
+            stiff = jnp.where(low, gammas[2 * pair], gammas[2 * pair + 1])
+            mass = frac * density * area
+            pressure = stiff * density * energy
+            state_ref[source, at[0]] = frac * after
+            state_ref[source, at[1]] = mass
+            state_ref[source, at[2]] = mass * energy - frac * (pressure + viscous) * change
+        return carry
+
+    lax.fori_loop(0, devices, conserve, 0)
+    piece = lax.broadcasted_iota(jnp.int32, (SUB, LANES), 1) // (LANES // SUB)
+    odd = [(piece >> bit) & 1 == 1 for bit in range(3)]
+
+    def regroup(values):
+        for bit in range(3):
+            values = [
+                jnp.where(odd[bit], values[i | (1 << bit)], values[i & ~(1 << bit)])
+                if not (i >> bit) & 1
+                else jnp.where(odd[bit], values[i & ~(1 << bit)], values[i | (1 << bit)])
+                for i in range(SUB)
+            ]
+        return values
+
+    def gather(a, carry):
+        for octet in range(devices // SUB):
+            index, weight, place = [], [], []
+            for sigma in range(SUB):
+                source = a * SUB + sigma
+                spread = (SUB, LANES)
+                index.append(
+                    jnp.broadcast_to(extra_ref[source, 12 + octet : 13 + octet], spread).astype(jnp.int32)
+                )
+                weight.append(jnp.broadcast_to(extra_ref[source, 16 + octet : 17 + octet], spread))
+                place.append(jnp.broadcast_to(extra_ref[source, 20 + octet : 21 + octet], spread))
+            for delta, value in enumerate(regroup(place)):
+                places_ref[SUB * octet + delta, a] = value
+            for tile in range(tiles):
+                at = slice(SUB * tile, SUB * tile + SUB)
+                values = [
+                    jnp.take_along_axis(
+                        state_ref[a * SUB + sigma, at], index[sigma], axis=1, mode="promise_in_bounds"
+                    )
+                    * weight[sigma]
+                    for sigma in range(SUB)
+                ]
+                for delta, value in enumerate(regroup(values)):
+                    slots_ref[SUB * octet + delta, a, at] = value
+        return carry
+
+    lax.fori_loop(0, devices // SUB, gather, 0)
+
+    def scatter(target, carry):
+        groups = devices // SUB
+        value = jnp.concatenate([slots_ref[target, a] for a in range(groups)], axis=1)
+        parts = jnp.concatenate(split3(value), axis=0)
+        place = [places_ref[target, a] for a in range(groups)]
+        block = lax.broadcasted_iota(jnp.int32, (SUB, LANES), 0).astype(jnp.float32)
+        hot = jnp.concatenate(
+            [
+                jnp.concatenate(
+                    [
+                        jnp.where(place[a] == block + float(SUB * tile), 1.0, 0.0)
+                        for tile in range(LANES // SUB)
+                    ],
+                    axis=0,
+                )
+                for a in range(groups)
+            ],
+            axis=1,
+        ).astype(jnp.bfloat16)
+        total = lax.dot_general(
+            parts, hot, (((1,), (1,)), ((), ())), preferred_element_type=jnp.float32
+        )
+        out_ref[target] = total[0:rows] + total[rows : 2 * rows] + total[2 * rows : 3 * rows]
+        return carry
+
+    lax.fori_loop(0, devices, scatter, 0)
+
+
+def unpack_kernel(sums_ref, own_ref, out_ref):
+    low = lower_half((SUB, LANES))
+    half = LANES // 2
+    for pair in range(sums_ref.shape[1] // SUB):
+        at = slice(SUB * pair, SUB * pair + SUB)
+        first, second = [], []
+        for octet in range(LANES // SUB):
+            even, odd = pair_to_pieces(sums_ref[2 * octet, at], sums_ref[2 * octet + 1, at], low)
+            first.append(even)
+            second.append(odd)
+        for field, tiles in ((2 * pair, first), (2 * pair + 1, second)):
+            blocks = jnp.concatenate(tiles, axis=0).T
+            out_ref[field, :, :LANES] = own_ref[field, :, :LANES] + blocks[:half]
+            out_ref[field, :, LANES:] = own_ref[field, :, LANES:] + blocks[half:]
+
+
+def whole(count):
+    return [pl.BlockSpec(memory_space=pltpu.VMEM)] * count
+
+
+def exchange(value):
+    return lax.all_to_all(value, ("zx", "zy"), 0, 0, tiled=True)
+
+
+def remap_by_zones(
+    frac, density, energy, area_now, area_after, viscous, dest_tile, src_block, dest_block, crossing
+):
+    devices = lax.axis_size("zx") * lax.axis_size("zy")
+    fields = 3 * frac.shape[0]
+    rows = fields * QUAD
+    f32 = jnp.float32
+    raw = pl.pallas_call(
+        pack_kernel,
+        out_shape=jax.ShapeDtypeStruct((devices, rows, LANES), f32),
+        in_specs=whole(3),
+        out_specs=whole(1)[0],
+        name="pack",
+    )(frac, density, energy)
+    raw = exchange(raw)
+    me = (lax.axis_index("zx") * lax.axis_size("zy") + lax.axis_index("zy")).astype(jnp.int32)
+    tables = pl.pallas_call(
+        table_kernel,
+        out_shape=jax.ShapeDtypeStruct((16, LANES), f32),
+        in_specs=[pl.BlockSpec(memory_space=pltpu.SMEM)] + whole(4),
+        out_specs=whole(1)[0],
+        name="tables",
+    )(me.reshape(1, 1), dest_tile[0, 0], src_block[0], dest_block[0], crossing[0])
+    extras = pl.pallas_call(
+        extras_kernel,
+        out_shape=jax.ShapeDtypeStruct((devices, 24, LANES), f32),
+        in_specs=whole(4),
+        out_specs=whole(1)[0],
+        name="extras",
+    )(area_now, area_after, viscous, tables)
+    extras = exchange(extras)
+    sums = pl.pallas_call(
+        crossing_kernel,
+        out_shape=jax.ShapeDtypeStruct((devices, rows, LANES), f32),
+        in_specs=whole(2),
+        out_specs=whole(1)[0],
+        scratch_shapes=[
+            pltpu.VMEM((devices, rows, LANES), f32),
+            pltpu.VMEM((devices, devices // SUB, rows, LANES), f32),
+            pltpu.VMEM((devices, devices // SUB, SUB, LANES), f32),
+        ],
+        name="crossings",
+    )(raw, extras)
+    return exchange(sums)
+
+
+def lagrange(frac, density, energy, node_shift, node_speed):
+    node_fields = jnp.concatenate([node_shift, node_speed], axis=0)
+    extended = upper_rim(node_fields)
+    area_now, mat_pressure, viscous, terms = zone_phase(
+        frac, density, energy, slice_corners(extended[0:2]), slice_corners(extended[2:4])
+    )
+    term_one, term_two, term_three, term_four = terms
+    gathered = (
+        jnp.pad(term_one, ((0, 0), (0, 1), (0, 1)))
+        + jnp.pad(term_two, ((0, 0), (1, 0), (0, 1)))
+        + jnp.pad(term_three, ((0, 0), (1, 0), (1, 0)))
+        + jnp.pad(term_four, ((0, 0), (0, 1), (1, 0)))
+    )
+    totals = spill_rim(gathered)
+    speed_after, shift_after = node_update(totals, node_shift, node_speed)
+    moved_rim = upper_rim(shift_after)
+    area_after = zone_area(slice_corners(moved_rim))
+    return area_now, area_after, viscous, mat_pressure, speed_after, shift_after
+
+
+def local(*arguments):
+    materials, rows_x, rows_y = arguments[0].shape
+    devices = lax.axis_size("zx") * lax.axis_size("zy")
+    entries, nblocks = arguments[6].shape[2], arguments[9].shape[2]
+    fits = (rows_x, rows_y, nblocks) == (64, 256, LANES) and materials == 8
+    if fits and devices == LANES // QUAD and entries <= 2 * LANES:
+        return local_by_zones(*arguments)
+    return local_by_entries(*arguments)
+
+
+def local_by_zones(
+    frac, density, energy, node_shift, node_speed, dest_tile, src_block, dest_block, crossing, keep
+):
+    materials, rows_x, rows_y = frac.shape
+    area_now, area_after, viscous, mat_pressure, speed_after, shift_after = lagrange(
+        frac, density, energy, node_shift, node_speed
+    )
+    sums = remap_by_zones(
+        frac, density, energy, area_now, area_after, viscous, dest_tile, src_block, dest_block, crossing
+    )
+    conserved = material_state(frac, density, energy, area_now, area_after, mat_pressure, viscous)
+    share = keep[0, 0].reshape(rows_x, 2)
+    share = jnp.concatenate(
+        [jnp.broadcast_to(share[:, h : h + 1], (rows_x, LANES)) for h in range(2)], axis=1
+    )
+    own = (conserved * share).reshape(3 * materials, rows_x, rows_y)
+    remapped = pl.pallas_call(
+        unpack_kernel,
+        out_shape=jax.ShapeDtypeStruct(own.shape, jnp.float32),
+        in_specs=whole(2),
+        out_specs=whole(1)[0],
+        name="unpack",
+    )(sums, own)
+    return (remapped.reshape(3, materials, rows_x, rows_y), speed_after, shift_after)
+
+
+def local_by_entries(
     frac, density, energy, node_shift, node_speed, dest_tile, src_block, dest_block, crossing, keep
 ):
     materials, rows_x, rows_y = frac.shape

time: 339 us -> 156 us (0.46)
  the two profiles are of different devices: /device:TPU:13 before, /device:TPU:0 now
where the time goes in v1:
time: 156 us
  waiting for transfers between devices  58.1 us (37%)
  blocking collectives  41.8 us (27%)
  Pallas kernels  25.7 us (16%)
  starting transfers between devices  17.6 us (11%)
  other arithmetic  6.84 us (4%)
  local copies, waits for them, and re-layouts  4.85 us (3%)
    all_to_all x2, waiting for transfers between devices, exchange(): return lax.all_to_all(value, ('zx', 'zy'), 0, 0, tiled=True)  45.5 us
    all_to_all x1, blocking collectives, exchange(): return lax.all_to_all(value, ('zx', 'zy'), 0, 0, tiled=True)  41.8 us
    pallas_call x1, Pallas kernels, remap_by_zones(): pl.pallas_call(crossing_kernel, out_shape=jax.ShapeDtypeStruct((devices,...  15.5 us
    ppermute x6, waiting for transfers between devices, shifted(): lax.ppermute(value, axis, [(i, (i + by) % peers) for i in range(peers)])  12.6 us
    ppermute x6, starting transfers between devices, shifted(): lax.ppermute(value, axis, [(i, (i + by) % peers) for i in range(peers)])  9.58 us
    all_to_all x2, starting transfers between devices, exchange(): return lax.all_to_all(value, ('zx', 'zy'), 0, 0, tiled=True)  7.99 us
    pallas_call x1, Pallas kernels, local_by_zones(): pl.pallas_call(unpack_kernel, out_shape=jax.ShapeDtypeStruct(own.shape, j...  3.5 us
  transfers between devices with their start and end apart: 8, of which 7 were waited for; matrix products, arithmetic and copies ran while one was open for 4% of the time, Pallas kernels for 3%

profile of v1, /device:TPU:0, one launch (start us, length us, event | category | flops | bytes accessed | tf_op | source)
XLA Modules:
  0.0 155.8 jit_solution(7732751001805007344)
XLA Ops:
  0.6 0.9 constant_dynamic-update-slice_fusion.1
  1.6 1.0 constant_dynamic-update-slice_fusion
  2.6 3.0 %collective-permute-start = (f32[4,1,256]{2,1,0:T(1,128)S(1)}, f32[4,1,256]{2,1,0:T(1,128)S(1)}, u32[]{:S(2)}, u32[]{:S(2)}) collective-permute-start(f32[4,1,256]{2,1,0:T(1,128)S(1)} %slice.211), channel_id=1, source_target_pairs={{0,16},{16,0},{1,17},{17,1},{2,18},{18,2},{3,19},{19,3},{4,20},{20... | collective-permute-start | bytes 12296 | tf_op jit(solution)/shard_map/ppermute | solution.py:15
  5.6 1.6 %collective-permute-done = f32[4,1,256]{2,1,0:T(1,128)S(1)} collective-permute-done((f32[4,1,256]{2,1,0:T(1,128)S(1)}, f32[4,1,256]{2,1,0:T(1,128)S(1)}, u32[]{:S(2)}, u32[]{:S(2)}) %collective-permute-start) | collective-permute-done | bytes 4128 | tf_op jit(solution)/shard_map/ppermute | solution.py:15
  7.2 3.4 %collective-permute-start.1 = (f32[4,65,1]{2,1,0:T(8,128)S(1)}, f32[4,65,1]{2,1,0:T(8,128)S(1)}, u32[]{:S(2)}, u32[]{:S(2)}) collective-permute-start(f32[4,65,1]{2,1,0:T(8,128)S(1)} %fusion.1), channel_id=1, source_target_pairs={{0,15},{1,0},{2,1},{3,2},{4,3},{5,4},{6,5},{7,6},{8,7},{9,8},{10,9... | collective-permute-start | bytes 3128 | tf_op jit(solution)/shard_map/ppermute | solution.py:15
  10.6 1.5 multiply_reduce_fusion
  12.1 1.1 collective-permute-done.1
  13.8 1.5 collective-permute-start.2
  15.3 0.2 pad_add_fusion
  15.6 1.9 %collective-permute-done.2 = f32[3,1,257]{2,1,0:T(1,128)S(1)} collective-permute-done((f32[3,1,257]{2,1,0:T(1,128)S(1)}, f32[3,1,257]{2,1,0:T(1,128)S(1)}, u32[]{:S(2)}, u32[]{:S(2)}) %collective-permute-start.2) | collective-permute-done | bytes 3116 | tf_op jit(solution)/shard_map/ppermute | solution.py:15
  17.6 6.7 %collective-permute-done.3 = f32[3,64,1]{2,1,0:T(8,128)S(1)} collective-permute-done((f32[3,64,1]{2,1,0:T(8,128)S(1)}, f32[3,64,1]{2,1,0:T(8,128)S(1)}, u32[]{:S(2)}, u32[]{:S(2)}) %collective-permute-start.3) | collective-permute-done | bytes 800 | tf_op jit(solution)/shard_map/ppermute | solution.py:15
  24.4 0.7 multiply_add_fusion
  25.1 1.5 collective-permute-start.4
  26.6 0.8 copy.13.target_ref
  27.4 1.9 %tables.1.tables_ref = f32[16,128]{1,0:T(8,128)} custom-call(s32[1,1]{1,0:T(1,128)} %bitcast.6.me_ref, s32[256,1]{1,0:T(8,128)} %copy.13.target_ref, s32[1,256]{1,0:T(1,128)} %bitcast.49, s32[1,256]{1,0:T(1,128)} %bitcast.50, f32[1,256]{1,0:T(1,128)} %bitcast.51), custom_call_target="tpu_custom_call" | custom-call | tf_op jit(solution)/shard_map/tables/pallas_call | solution.py:329
  29.4 0.7 multiply_multiply_fusion.1.viscous_ref
  30.1 1.3 collective-permute-done.5
  31.4 0.8 subtract_bitcast_fusion
  32.2 1.8 %extras.1 = f32[32,24,128]{2,1,0:T(8,128)} custom-call(f32[64,256]{1,0:T(8,128)} %bitcast.43, f32[64,256]{1,0:T(8,128)} %bitcast.46, f32[64,256]{1,0:T(8,128)} %multiply_multiply_fusion.1.viscous_ref, f32[16,128]{1,0:T(8,128)} %tables.1.tables_ref), custom_call_target="tpu_custom_call" | custom-call | tf_op jit(solution)/shard_map/extras/pallas_call | solution.py:336
  34.0 5.2 %all-to-all-start.1 = ((f32[32,24,128]{2,1,0:T(8,128)}), f32[32,24,128]{2,1,0:T(8,128)S(1)}, u32[]{:S(2)}, u32[]{:S(2)}) async-start(f32[32,24,128]{2,1,0:T(8,128)} %extras.1), calls=%async_computation.1 | async-start | bytes 786432 | tf_op jit(solution)/shard_map/all_to_all | solution.py:310
  39.2 3.0 %pack.1 = f32[32,96,128]{2,1,0:T(8,128)} custom-call(f32[8,64,256]{2,1,0:T(8,128)} %frac_ref.1, f32[8,64,256]{2,1,0:T(8,128)} %density_ref.1, f32[8,64,256]{2,1,0:T(8,128)} %energy_ref.1), custom_call_target="tpu_custom_call" | custom-call | tf_op jit(solution)/shard_map/pack/pallas_call | solution.py:320
  42.1 10.1 %all-to-all-done.1.extra_ref = f32[32,24,128]{2,1,0:T(8,128)S(1)} async-done(((f32[32,24,128]{2,1,0:T(8,128)}), f32[32,24,128]{2,1,0:T(8,128)S(1)}, u32[]{:S(2)}, u32[]{:S(2)}) %all-to-all-start.1) | async-done | bytes 393248 | tf_op jit(solution)/shard_map/all_to_all | solution.py:310
  52.3 41.8 %all_to_all.15.raw_ref = f32[32,96,128]{2,1,0:T(8,128)} all-to-all(f32[32,96,128]{2,1,0:T(8,128)} %pack.1), channel_id=1, replica_groups=mesh['zx'=2,'zy'=16] {'zx','zy'}, dimensions={0} | all-to-all | bytes 3145728 | tf_op jit(solution)/shard_map/all_to_all | solution.py:310
  94.1 15.5 %crossings.1 = f32[32,96,128]{2,1,0:T(8,128)} custom-call(f32[32,96,128]{2,1,0:T(8,128)} %all_to_all.15.raw_ref, f32[32,24,128]{2,1,0:T(8,128)} %copy-done.7), custom_call_target="tpu_custom_call" | custom-call | tf_op jit(solution)/shard_map/crossings/pallas_call | solution.py:344
  109.6 2.8 %all-to-all-start.2 = ((f32[32,96,128]{2,1,0:T(8,128)}), f32[32,96,128]{2,1,0:T(8,128)S(1)}, u32[]{:S(2)}, u32[]{:S(2)}) async-start(f32[32,96,128]{2,1,0:T(8,128)} %crossings.1), calls=%async_computation.2 | async-start | bytes 3145728 | tf_op jit(solution)/shard_map/all_to_all | solution.py:310
  112.5 0.5 broadcast.212
  112.9 0.6 reduce.7
  114.1 0.3 multiply_bitcast_fusion.2
  114.5 1.3 bitcast_multiply_fusion.own_ref
  115.8 35.3 %all-to-all-done.2.sums_ref = f32[32,96,128]{2,1,0:T(8,128)S(1)} async-done(((f32[32,96,128]{2,1,0:T(8,128)}), f32[32,96,128]{2,1,0:T(8,128)S(1)}, u32[]{:S(2)}, u32[]{:S(2)}) %all-to-all-start.2) | async-done | bytes 1572896 | tf_op jit(solution)/shard_map/all_to_all | solution.py:310
  151.1 1.2 copy-done
  152.3 3.5 %unpack.1 = f32[24,64,256]{2,1,0:T(8,128)} custom-call(f32[32,96,128]{2,1,0:T(8,128)} %copy-done, f32[24,64,256]{2,1,0:T(8,128)} %bitcast_multiply_fusion.own_ref), custom_call_target="tpu_custom_call" | custom-call | tf_op jit(solution)/shard_map/unpack/pallas_call | solution.py:405
  (51 shorter events, 1.5 us)
Async XLA Ops:
  1.5 11.8 %copy-start.8 = (f32[2,64,256]{2,1,0:T(8,128)S(1)}, f32[2,64,256]{2,1,0:T(8,128)}, u32[]{:S(2)}) copy-start(f32[2,64,256]{2,1,0:T(8,128)} %param.14) | copy-start | bytes 393220
  1.6 11.8 %copy-start.9 = (f32[2,64,256]{2,1,0:T(8,128)S(1)}, f32[2,64,256]{2,1,0:T(8,128)}, u32[]{:S(2)}) copy-start(f32[2,64,256]{2,1,0:T(8,128)} %param.13) | copy-start | bytes 393220
  2.6 4.6 %collective-permute-start = (f32[4,1,256]{2,1,0:T(1,128)S(1)}, f32[4,1,256]{2,1,0:T(1,128)S(1)}, u32[]{:S(2)}, u32[]{:S(2)}) collective-permute-start(f32[4,1,256]{2,1,0:T(1,128)S(1)} %slice.211), channel_id=1, source_target_pairs={{0,16},{16,0},{1,17},{17,1},{2,18},{18,2},{3,19},{19,3},{4,20},{20... | collective-permute-start | bytes 12296 | tf_op jit(solution)/shard_map/ppermute | solution.py:15
  7.2 6.1 %collective-permute-start.1 = (f32[4,65,1]{2,1,0:T(8,128)S(1)}, f32[4,65,1]{2,1,0:T(8,128)S(1)}, u32[]{:S(2)}, u32[]{:S(2)}) collective-permute-start(f32[4,65,1]{2,1,0:T(8,128)S(1)} %fusion.1), channel_id=1, source_target_pairs={{0,15},{1,0},{2,1},{3,2},{4,3},{5,4},{6,5},{7,6},{8,7},{9,8},{10,9... | collective-permute-start | bytes 3128 | tf_op jit(solution)/shard_map/ppermute | solution.py:15
  13.5 17.9 %copy-start.5 = (f32[1,64,256]{2,1,0:T(8,128)}, f32[1,64,256]{2,1,0:T(8,128)S(1)}, u32[]{:S(2)}) copy-start(f32[1,64,256]{2,1,0:T(8,128)S(1)} %get-tuple-element.9) | copy-start | bytes 196612
  13.8 3.7 %collective-permute-start.2 = (f32[3,1,257]{2,1,0:T(1,128)S(1)}, f32[3,1,257]{2,1,0:T(1,128)S(1)}, u32[]{:S(2)}, u32[]{:S(2)}) collective-permute-start(f32[3,1,257]{2,1,0:T(1,128)S(1)} %pad_add_fusion.3), channel_id=1, source_target_pairs={{0,16},{16,0},{1,17},{17,1},{2,18},{18,2},{3,19},{19,3},{4,20},{20... | collective-permute-start | bytes 9260 | tf_op jit(solution)/shard_map/ppermute | solution.py:15
  15.6 11.1 %copy-start.11 = (s32[1,1,256,1]{2,3,1,0:T(1,128)S(1)}, s32[1,1,256,1]{2,3,1,0:T(1,128)}, u32[]{:S(2)}) copy-start(s32[1,1,256,1]{2,3,1,0:T(1,128)} %param.15) | copy-start | bytes 3076
  17.6 6.8 %collective-permute-start.3 = (f32[3,64,1]{2,1,0:T(8,128)S(1)}, f32[3,64,1]{2,1,0:T(8,128)S(1)}, u32[]{:S(2)}, u32[]{:S(2)}) collective-permute-start(f32[3,64,1]{2,1,0:T(8,128)S(1)} %fusion.4), channel_id=1, source_target_pairs={{0,1},{1,2},{2,3},{3,4},{4,5},{5,6},{6,7},{7,8},{8,9},{9,10},{10,1... | collective-permute-start | bytes 2312 | tf_op jit(solution)/shard_map/ppermute | solution.py:15
  25.1 8.9 %copy-start.4 = (f32[2,64,256]{2,1,0:T(8,128)}, f32[2,64,256]{2,1,0:T(8,128)S(1)}, u32[]{:S(2)}) copy-start(f32[2,64,256]{2,1,0:T(8,128)S(1)} %get-tuple-element.16) | copy-start | bytes 393220
  25.1 4.2 %collective-permute-start.4 = (f32[2,1,256]{2,1,0:T(1,128)S(1)}, f32[2,1,256]{2,1,0:T(1,128)S(1)}, u32[]{:S(2)}, u32[]{:S(2)}) collective-permute-start(f32[2,1,256]{2,1,0:T(1,128)S(1)} %slice.234), channel_id=1, source_target_pairs={{0,16},{16,0},{1,17},{17,1},{2,18},{18,2},{3,19},{19,3},{4,20},{20... | collective-permute-start | bytes 6152 | tf_op jit(solution)/shard_map/ppermute | solution.py:15
  29.4 2.0 %collective-permute-start.5 = (f32[2,65,1]{2,1,0:T(8,128)S(1)}, f32[2,65,1]{2,1,0:T(8,128)S(1)}, u32[]{:S(2)}, u32[]{:S(2)}) collective-permute-start(f32[2,65,1]{2,1,0:T(8,128)S(1)} %fusion.7), channel_id=1, source_target_pairs={{0,15},{1,0},{2,1},{3,2},{4,3},{5,4},{6,5},{7,6},{8,7},{9,8},{10,9... | collective-permute-start | bytes 1568 | tf_op jit(solution)/shard_map/ppermute | solution.py:15
  34.0 18.3 %all-to-all-start.1 = ((f32[32,24,128]{2,1,0:T(8,128)}), f32[32,24,128]{2,1,0:T(8,128)S(1)}, u32[]{:S(2)}, u32[]{:S(2)}) async-start(f32[32,24,128]{2,1,0:T(8,128)} %extras.1), calls=%async_computation.1 | async-start | bytes 786432 | tf_op jit(solution)/shard_map/all_to_all | solution.py:310
  52.3 41.8 %copy-start.7 = (f32[32,24,128]{2,1,0:T(8,128)}, f32[32,24,128]{2,1,0:T(8,128)S(1)}, u32[]{:S(2)}) copy-start(f32[32,24,128]{2,1,0:T(8,128)S(1)} %all-to-all-done.1.extra_ref) | copy-start | bytes 1179652
  109.6 3.4 %copy-start.12 = (f32[1,1,128]{2,1,0:T(1,128)S(1)}, f32[1,1,128]{2,1,0:T(1,128)}, u32[]{:S(2)}) copy-start(f32[1,1,128]{2,1,0:T(1,128)} %param.19) | copy-start | bytes 1540
  109.6 4.4 %copy-start.1 = (f32[8,64,256]{2,1,0:T(8,128)S(1)}, f32[8,64,256]{2,1,0:T(8,128)}, u32[]{:S(2)}) copy-start(f32[8,64,256]{2,1,0:T(8,128)} %frac_ref.1) | copy-start | bytes 1572868
  109.6 4.4 %copy-start.2 = (f32[8,64,256]{2,1,0:T(8,128)S(1)}, f32[8,64,256]{2,1,0:T(8,128)}, u32[]{:S(2)}) copy-start(f32[8,64,256]{2,1,0:T(8,128)} %density_ref.1) | copy-start | bytes 1572868
  109.6 4.4 %copy-start.3 = (f32[8,64,256]{2,1,0:T(8,128)S(1)}, f32[8,64,256]{2,1,0:T(8,128)}, u32[]{:S(2)}) copy-start(f32[8,64,256]{2,1,0:T(8,128)} %energy_ref.1) | copy-start | bytes 1572868
  109.6 4.4 %copy-start.6 = (f32[1,64,256]{2,1,0:T(8,128)S(1)}, f32[1,64,256]{2,1,0:T(8,128)}, u32[]{:S(2)}) copy-start(f32[1,64,256]{2,1,0:T(8,128)} %copy-done.5) | copy-start | bytes 196612
  109.6 4.4 %copy-start.10 = (f32[1,64,256]{2,1,0:T(8,128)S(1)}, f32[1,64,256]{2,1,0:T(8,128)}, u32[]{:S(2)}) copy-start(f32[1,64,256]{2,1,0:T(8,128)} %get-tuple-element.15) | copy-start | bytes 196612
  109.6 41.5 %all-to-all-start.2 = ((f32[32,96,128]{2,1,0:T(8,128)}), f32[32,96,128]{2,1,0:T(8,128)S(1)}, u32[]{:S(2)}, u32[]{:S(2)}) async-start(f32[32,96,128]{2,1,0:T(8,128)} %crossings.1), calls=%async_computation.2 | async-start | bytes 3145728 | tf_op jit(solution)/shard_map/all_to_all | solution.py:310
  151.1 1.2 copy-start

commit v2 on v1

--- a/solution.py
+++ b/solution.py
@@ -144,7 +144,7 @@
     return high, middle, low
 
 
-def table_kernel(me_ref, target_ref, source_ref, place_ref, weight_ref, out_ref):
+def table_kernel(me_ref, target_ref, source_ref, place_ref, weight_ref, keep_ref, out_ref):
     entries = target_ref.shape[0]
     capacity = LANES // SUB
     me = me_ref[0, 0]
@@ -170,53 +170,160 @@
     weights = tables[0:1] + tables[1:2] + tables[2:3]
     for octet in range(4):
         at = slice(LANES * octet, LANES * octet + LANES)
-        out_ref[octet : octet + 1, :] = jnp.zeros((1, LANES), jnp.float32)
-        out_ref[4 + octet : 5 + octet, :] = tables[3:4, at]
-        out_ref[8 + octet : 9 + octet, :] = weights[:, at]
-        out_ref[12 + octet : 13 + octet, :] = tables[4:5, at]
-
-
-def extras_kernel(area_ref, after_ref, viscous_ref, tables_ref, out_ref):
+        out_ref[octet : octet + 1, :] = tables[3:4, at]
+        out_ref[4 + octet : 5 + octet, :] = weights[:, at]
+        out_ref[8 + octet : 9 + octet, :] = tables[4:5, at]
+    lane = lax.broadcasted_iota(jnp.int32, (SUB, LANES), 1)
+    block = 2 * (lane % 64) + lane // 64
+    keep = jnp.take_along_axis(
+        jnp.broadcast_to(keep_ref[...], (SUB, LANES)), block, axis=1, mode="promise_in_bounds"
+    )
+    out_ref[12:16, :] = keep[0:4]
+
+
+def stiffness(materials):
+    gammas = np.float32(1.3) + np.float32(0.05) * np.arange(materials, dtype=np.float32)
+    return [float(gamma) for gamma in gammas - np.float32(1.0)]
+
+
+def sums_kernel(frac_ref, density_ref, energy_ref, shift_ref, speed_ref, sums_ref, rim_ref):
+    stiff = stiffness(frac_ref.shape[0])
+    mass = pressure = None
+    for material in range(frac_ref.shape[0]):
+        part = frac_ref[material] * density_ref[material]
+        force = part * energy_ref[material] * stiff[material]
+        mass = part if mass is None else mass + part
+        pressure = force if pressure is None else pressure + force
+    sums_ref[0], sums_ref[1] = mass, pressure
+    last = mass.shape[0] - 1
+    for field in range(2):
+        for at, ref in ((0, shift_ref), (4, speed_ref)):
+            rim_ref[at + 2 * field : at + 2 * field + 2, :] = ref[field, 0:2, :]
+            rim_ref[10 + at // 2 + field : 11 + at // 2 + field, :] = ref[field, last : last + 1, :]
+    for field, value in enumerate((mass, pressure)):
+        rim_ref[8 + field : 9 + field, :] = value[0:1]
+        rim_ref[14 + field : 15 + field, :] = value[last : last + 1]
+
+
+def rows_kernel(shift_ref, speed_ref, sums_ref, above_ref, below_ref, out_ref, first_ref, last_ref):
+    height, width = shift_ref.shape[1:]
+    for field in range(6):
+        value = (shift_ref, speed_ref, sums_ref)[field // 2][field % 2]
+        out_ref[field, 1 : height + 1, :] = value
+        out_ref[field, 0:1, :] = below_ref[10 + field : 11 + field, :]
+        if field < 4:
+            out_ref[field, height + 1 : height + 3, :] = above_ref[2 * field : 2 * field + 2, :]
+        else:
+            for row in (1, 2):
+                out_ref[field, height + row : height + row + 1, :] = above_ref[4 + field : 5 + field, :]
+        out_ref[field, height + 3 : height + 8, :] = jnp.zeros((5, width), jnp.float32)
+        whole_column = out_ref[field]
+        if field < 4:
+            first_ref[:, 2 * field : 2 * field + 2] = whole_column[:, 0:2]
+        else:
+            first_ref[:, 4 + field : 5 + field] = whole_column[:, 0:1]
+        last_ref[:, field : field + 1] = whole_column[:, width - 1 : width]
+
+
+def lagrange_kernel(
+    rows_ref, right_ref, left_ref, raw_ref, tables_ref, speed_ref, shift_ref, out_ref
+):
+    height, width = rows_ref.shape[1] - SUB, rows_ref.shape[2]
+    shape = (height + SUB, width + LANES)
+    lane = lax.broadcasted_iota(jnp.int32, shape, 1)
+    right, left = right_ref[...], left_ref[...]
+
+    def extend(field):
+        value = jnp.concatenate([rows_ref[field], jnp.zeros((shape[0], LANES), jnp.float32)], axis=1)
+        value = pltpu.roll(value, 1, 1)
+        value = jnp.where(lane == 0, left[:, field : field + 1], value)
+        if field < 4:
+            value = jnp.where(lane == width + 1, right[:, 2 * field : 2 * field + 1], value)
+            return jnp.where(lane == width + 2, right[:, 2 * field + 1 : 2 * field + 2], value)
+        return jnp.where(lane == width + 1, right[:, 4 + field : 5 + field], value)
+
+    def next_row(value):
+        return pltpu.roll(value, shape[0] - 1, 0)
+
+    def next_column(value):
+        return pltpu.roll(value, shape[1] - 1, 1)
+
+    def before_row(value):
+        return pltpu.roll(value, 1, 0)
+
+    def before_column(value):
+        return pltpu.roll(value, 1, 1)
+
+    def diagonals(value):
+        across = next_column(value)
+        down = next_row(value)
+        return next_row(across) - value, across - down
+
+    def geometry(shift_x, shift_y):
+        rise_x, cross_x = diagonals(shift_x)
+        rise_y, cross_y = diagonals(shift_y)
+        return 1.0 + rise_x, 1.0 + rise_y, -1.0 + cross_x, 1.0 + cross_y
+
+    shift_x, shift_y, speed_x, speed_y, density, pressure = [extend(field) for field in range(6)]
+    rise_x, rise_y, cross_x, cross_y = geometry(shift_x, shift_y)
+    area = 0.5 * (rise_x * cross_y - cross_x * rise_y)
+    up_x, over_x = diagonals(speed_x)
+    up_y, over_y = diagonals(speed_y)
+    rate = 0.5 * (up_x * cross_y + rise_x * over_y - over_x * rise_y - cross_x * up_y)
+    squeeze = jnp.minimum(rate / area, 0.0)
+    viscous = VISC_COEF * density * area * squeeze * squeeze
+    half = 0.5 * (pressure + viscous)
+    quarter = 0.25 * density * area
+
+    def corners(one, two, sign):
+        upper = before_row(two - before_column(one))
+        return sign * (one - before_column(two) + upper)
+
+    force_x = corners(-half * cross_y, half * rise_y, 1.0)
+    force_y = corners(half * cross_x, -half * rise_x, 1.0)
+    both = quarter + before_column(quarter)
+    mass = both + before_row(both)
+    speed_x = speed_x + TIME_STEP * (force_x / mass)
+    speed_y = speed_y + TIME_STEP * (force_y / mass)
+    shift_x = shift_x + TIME_STEP * speed_x
+    shift_y = shift_y + TIME_STEP * speed_y
+    rise_x, rise_y, cross_x, cross_y = geometry(shift_x, shift_y)
+    after = 0.5 * (rise_x * cross_y - cross_x * rise_y)
+
+    def own(value):
+        return next_column(next_row(value))[0:height, 0:width]
+
+    speed_ref[0], speed_ref[1] = own(speed_x), own(speed_y)
+    shift_ref[0], shift_ref[1] = own(shift_x), own(shift_y)
+
     low = lower_half((SUB, LANES))
-    area, after = zones_first(area_ref[...]), zones_first(after_ref[...])
-    viscous = zones_first(viscous_ref[...])
-    first, second = tables_ref[0:8], tables_ref[8:16]
+    area, after, viscous = [zones_first(own(value)) for value in (area, after, viscous)]
+    pairs = raw_ref.shape[1] // (3 * SUB)
+    stiff = stiffness(2 * pairs)
     for octet in range(LANES // SUB):
         at = slice(SUB * octet, SUB * octet + SUB)
-        even, odd = pair_to_pieces(area[at], after[at], low)
-        out_ref[2 * octet, 0:8, :] = even
-        out_ref[2 * octet + 1, 0:8, :] = odd
-        out_ref[2 * octet, 8:16, :] = jnp.where(low, viscous[at], first)
-        out_ref[2 * octet + 1, 8:16, :] = jnp.where(low, pltpu.roll(viscous[at], QUAD, 0), first)
-        out_ref[2 * octet, 16:24, :] = second
-        out_ref[2 * octet + 1, 16:24, :] = second
-
-
-def crossing_kernel(raw_ref, extra_ref, out_ref, state_ref, slots_ref, places_ref):
-    devices, rows, lanes = raw_ref.shape
+        tiles = [pair_to_pieces(value[at], value[at], low) for value in (area, after, viscous)]
+        for side in range(2):
+            piece = 2 * octet + side
+            now, then, thick = [tile[side] for tile in tiles]
+            change = then - now
+            for pair in range(pairs):
+                at_pair = [slice(SUB * (pair + pairs * g), SUB * (pair + pairs * g) + SUB) for g in range(3)]
+                frac, rho, heat = [raw_ref[piece, rows] for rows in at_pair]
+                held = frac * rho
+                mass_now = held * now
+                force = jnp.where(low, stiff[2 * pair], stiff[2 * pair + 1]) * rho * heat
+                out_ref[piece, at_pair[0]] = frac * then
+                out_ref[piece, at_pair[1]] = mass_now
+                out_ref[piece, at_pair[2]] = mass_now * heat - frac * (force + thick) * change
+            end = 3 * SUB * pairs
+            out_ref[piece, end : end + 2 * SUB] = tables_ref[...]
+
+
+def crossing_kernel(state_ref, out_ref, slots_ref, places_ref):
+    devices = state_ref.shape[0]
+    rows = state_ref.shape[1] - 2 * SUB
     tiles = rows // SUB
-    pairs = tiles // 3
-    low = lower_half((SUB, LANES))
-    gammas = (np.float32(1.3) + np.float32(0.05) * np.arange(2 * pairs, dtype=np.float32)) - np.float32(1.0)
-
-    def conserve(source, carry):
-        area_pair, viscous_pair = extra_ref[source, 0:8], extra_ref[source, 8:16]
-        area_swap = pltpu.roll(area_pair, QUAD, 0)
-        area, after = jnp.where(low, area_pair, area_swap), jnp.where(low, area_swap, area_pair)
-        viscous = jnp.where(low, viscous_pair, pltpu.roll(viscous_pair, QUAD, 0))
-        change = after - area
-        for pair in range(pairs):
-            at = [slice(SUB * (pair + pairs * group), SUB * (pair + pairs * group) + SUB) for group in range(3)]
-            frac, density, energy = raw_ref[source, at[0]], raw_ref[source, at[1]], raw_ref[source, at[2]]
-            stiff = jnp.where(low, gammas[2 * pair], gammas[2 * pair + 1])
-            mass = frac * density * area
-            pressure = stiff * density * energy
-            state_ref[source, at[0]] = frac * after
-            state_ref[source, at[1]] = mass
-            state_ref[source, at[2]] = mass * energy - frac * (pressure + viscous) * change
-        return carry
-
-    lax.fori_loop(0, devices, conserve, 0)
     piece = lax.broadcasted_iota(jnp.int32, (SUB, LANES), 1) // (LANES // SUB)
     odd = [(piece >> bit) & 1 == 1 for bit in range(3)]
 
@@ -237,10 +344,10 @@
                 source = a * SUB + sigma
                 spread = (SUB, LANES)
                 index.append(
-                    jnp.broadcast_to(extra_ref[source, 12 + octet : 13 + octet], spread).astype(jnp.int32)
+                    jnp.broadcast_to(state_ref[source, rows + octet : rows + octet + 1], spread).astype(jnp.int32)
                 )
-                weight.append(jnp.broadcast_to(extra_ref[source, 16 + octet : 17 + octet], spread))
-                place.append(jnp.broadcast_to(extra_ref[source, 20 + octet : 21 + octet], spread))
+                weight.append(jnp.broadcast_to(state_ref[source, rows + 4 + octet : rows + octet + 5], spread))
+                place.append(jnp.broadcast_to(state_ref[source, rows + 8 + octet : rows + octet + 9], spread))
             for delta, value in enumerate(regroup(place)):
                 places_ref[SUB * octet + delta, a] = value
             for tile in range(tiles):
@@ -280,13 +387,15 @@
         total = lax.dot_general(
             parts, hot, (((1,), (1,)), ((), ())), preferred_element_type=jnp.float32
         )
-        out_ref[target] = total[0:rows] + total[rows : 2 * rows] + total[2 * rows : 3 * rows]
+        keep = jnp.broadcast_to(state_ref[target, rows + 12 : rows + 13], (rows, LANES))
+        stay = keep * state_ref[target, 0:rows]
+        out_ref[target] = stay + total[0:rows] + total[rows : 2 * rows] + total[2 * rows : 3 * rows]
         return carry
 
     lax.fori_loop(0, devices, scatter, 0)
 
 
-def unpack_kernel(sums_ref, own_ref, out_ref):
+def unpack_kernel(sums_ref, out_ref):
     low = lower_half((SUB, LANES))
     half = LANES // 2
     for pair in range(sums_ref.shape[1] // SUB):
@@ -298,82 +407,31 @@
             second.append(odd)
         for field, tiles in ((2 * pair, first), (2 * pair + 1, second)):
             blocks = jnp.concatenate(tiles, axis=0).T
-            out_ref[field, :, :LANES] = own_ref[field, :, :LANES] + blocks[:half]
-            out_ref[field, :, LANES:] = own_ref[field, :, LANES:] + blocks[half:]
+            out_ref[field, :, :LANES] = blocks[:half]
+            out_ref[field, :, LANES:] = blocks[half:]
 
 
 def whole(count):
     return [pl.BlockSpec(memory_space=pltpu.VMEM)] * count
 
 
+def call(kernel, name, outs, inputs, scratch=(), cycles=0):
+    specs = [
+        pl.BlockSpec(memory_space=pltpu.SMEM if value.size == 1 else pltpu.VMEM) for value in inputs
+    ]
+    shapes = [jax.ShapeDtypeStruct(shape, jnp.float32) for shape in outs]
+    return pl.pallas_call(
+        kernel,
+        out_shape=shapes if len(shapes) > 1 else shapes[0],
+        in_specs=specs,
+        out_specs=whole(len(shapes)) if len(shapes) > 1 else whole(1)[0],
+        scratch_shapes=[pltpu.VMEM(shape, jnp.float32) for shape in scratch],
+        name=name,
+    )(*inputs)
+
+
 def exchange(value):
     return lax.all_to_all(value, ("zx", "zy"), 0, 0, tiled=True)
-
-
-def remap_by_zones(
-    frac, density, energy, area_now, area_after, viscous, dest_tile, src_block, dest_block, crossing
-):
-    devices = lax.axis_size("zx") * lax.axis_size("zy")
-    fields = 3 * frac.shape[0]
-    rows = fields * QUAD
-    f32 = jnp.float32
-    raw = pl.pallas_call(
-        pack_kernel,
-        out_shape=jax.ShapeDtypeStruct((devices, rows, LANES), f32),
-        in_specs=whole(3),
-        out_specs=whole(1)[0],
-        name="pack",
-    )(frac, density, energy)
-    raw = exchange(raw)
-    me = (lax.axis_index("zx") * lax.axis_size("zy") + lax.axis_index("zy")).astype(jnp.int32)
-    tables = pl.pallas_call(
-        table_kernel,
-        out_shape=jax.ShapeDtypeStruct((16, LANES), f32),
-        in_specs=[pl.BlockSpec(memory_space=pltpu.SMEM)] + whole(4),
-        out_specs=whole(1)[0],
-        name="tables",
-    )(me.reshape(1, 1), dest_tile[0, 0], src_block[0], dest_block[0], crossing[0])
-    extras = pl.pallas_call(
-        extras_kernel,
-        out_shape=jax.ShapeDtypeStruct((devices, 24, LANES), f32),
-        in_specs=whole(4),
-        out_specs=whole(1)[0],
-        name="extras",
-    )(area_now, area_after, viscous, tables)
-    extras = exchange(extras)
-    sums = pl.pallas_call(
-        crossing_kernel,
-        out_shape=jax.ShapeDtypeStruct((devices, rows, LANES), f32),
-        in_specs=whole(2),
-        out_specs=whole(1)[0],
-        scratch_shapes=[
-            pltpu.VMEM((devices, rows, LANES), f32),
-            pltpu.VMEM((devices, devices // SUB, rows, LANES), f32),
-            pltpu.VMEM((devices, devices // SUB, SUB, LANES), f32),
-        ],
-        name="crossings",
-    )(raw, extras)
-    return exchange(sums)
-
-
-def lagrange(frac, density, energy, node_shift, node_speed):
-    node_fields = jnp.concatenate([node_shift, node_speed], axis=0)
-    extended = upper_rim(node_fields)
-    area_now, mat_pressure, viscous, terms = zone_phase(
-        frac, density, energy, slice_corners(extended[0:2]), slice_corners(extended[2:4])
-    )
-    term_one, term_two, term_three, term_four = terms
-    gathered = (
-        jnp.pad(term_one, ((0, 0), (0, 1), (0, 1)))
-        + jnp.pad(term_two, ((0, 0), (1, 0), (0, 1)))
-        + jnp.pad(term_three, ((0, 0), (1, 0), (1, 0)))
-        + jnp.pad(term_four, ((0, 0), (0, 1), (1, 0)))
-    )
-    totals = spill_rim(gathered)
-    speed_after, shift_after = node_update(totals, node_shift, node_speed)
-    moved_rim = upper_rim(shift_after)
-    area_after = zone_area(slice_corners(moved_rim))
-    return area_now, area_after, viscous, mat_pressure, speed_after, shift_after
 
 
 def local(*arguments):
@@ -381,7 +439,7 @@
     devices = lax.axis_size("zx") * lax.axis_size("zy")
     entries, nblocks = arguments[6].shape[2], arguments[9].shape[2]
     fits = (rows_x, rows_y, nblocks) == (64, 256, LANES) and materials == 8
-    if fits and devices == LANES // QUAD and entries <= 2 * LANES:
+    if fits and devices == LANES // QUAD and entries == 2 * LANES:
         return local_by_zones(*arguments)
     return local_by_entries(*arguments)
 
@@ -390,25 +448,49 @@
     frac, density, energy, node_shift, node_speed, dest_tile, src_block, dest_block, crossing, keep
 ):
     materials, rows_x, rows_y = frac.shape
-    area_now, area_after, viscous, mat_pressure, speed_after, shift_after = lagrange(
-        frac, density, energy, node_shift, node_speed
-    )
-    sums = remap_by_zones(
-        frac, density, energy, area_now, area_after, viscous, dest_tile, src_block, dest_block, crossing
-    )
-    conserved = material_state(frac, density, energy, area_now, area_after, mat_pressure, viscous)
-    share = keep[0, 0].reshape(rows_x, 2)
-    share = jnp.concatenate(
-        [jnp.broadcast_to(share[:, h : h + 1], (rows_x, LANES)) for h in range(2)], axis=1
-    )
-    own = (conserved * share).reshape(3 * materials, rows_x, rows_y)
-    remapped = pl.pallas_call(
-        unpack_kernel,
-        out_shape=jax.ShapeDtypeStruct(own.shape, jnp.float32),
-        in_specs=whole(2),
-        out_specs=whole(1)[0],
-        name="unpack",
-    )(sums, own)
+    devices = lax.axis_size("zx") * lax.axis_size("zy")
+    fields = 3 * materials
+    rows = fields * QUAD
+    plane = (2, rows_x, rows_y)
+    sums, rim = call(
+        sums_kernel, "sums", [plane, (16, rows_y)], (frac, density, energy, node_shift, node_speed)
+    )
+    above = shifted(rim, "zx", -1)
+    below = above if lax.axis_size("zx") == 2 else shifted(rim, "zx", 1)
+    tall = (rows_x + SUB, LANES)
+    extended, first, last = call(
+        rows_kernel,
+        "rows",
+        [(6, rows_x + SUB, rows_y), tall, tall],
+        (node_shift, node_speed, sums, above, below),
+    )
+    right = shifted(first, "zy", -1)
+    left = shifted(last, "zy", 1)
+    me = (lax.axis_index("zx") * lax.axis_size("zy") + lax.axis_index("zy")).astype(jnp.int32)
+    tables = call(
+        table_kernel,
+        "tables",
+        [(16, LANES)],
+        (me.reshape(1, 1), dest_tile[0, 0], src_block[0], dest_block[0], crossing[0], keep[0]),
+    )
+    raw = call(pack_kernel, "pack", [(devices, rows, LANES)], (frac, density, energy))
+    speed_after, shift_after, state = call(
+        lagrange_kernel,
+        "lagrange",
+        [plane, plane, (devices, rows + 2 * SUB, LANES)],
+        (extended, right, left, raw, tables),
+    )
+    state = exchange(state)
+    groups = devices // SUB
+    totals = call(
+        crossing_kernel,
+        "crossings",
+        [(devices, rows, LANES)],
+        (state,),
+        scratch=[(devices, groups, rows, LANES), (devices, groups, SUB, LANES)],
+    )
+    totals = exchange(totals)
+    remapped = call(unpack_kernel, "unpack", [(fields, rows_x, rows_y)], (totals,))
     return (remapped.reshape(3, materials, rows_x, rows_y), speed_after, shift_after)
 
 

time: 156 us -> 134 us (0.86)
  waiting for transfers between devices: 58.1 us -> 2.49 us
  blocking collectives: 41.8 us -> 91.2 us
  starting transfers between devices: 17.6 us -> 6.32 us
  other arithmetic: 6.84 us -> 0 us
  Pallas kernels: 25.7 us -> 31.3 us
  local copies, waits for them, and re-layouts: 4.85 us -> 2.01 us
    all_to_all x1 -> x2, blocking collectives: 41.8 us -> 91.2 us  [exchange(): return lax.all_to_all(value, ('zx', 'zy'), 0, 0, tiled=True)]
    all_to_all x2 -> x0, waiting for transfers between devices: 45.5 us -> none  [exchange(): return lax.all_to_all(value, ('zx', 'zy'), 0, 0, tiled=True)]
    ppermute x6 -> x3, waiting for transfers between devices: 12.6 us -> 2.49 us  [shifted(): lax.ppermute(value, axis, [(i, (i + by) % peers) for i in range(peers)])]
    all_to_all x2 -> x0, starting transfers between devices: 7.99 us -> none  [exchange(): return lax.all_to_all(value, ('zx', 'zy'), 0, 0, tiled=True)]
    pallas_call x5 -> x7, Pallas kernels: 25.7 us -> 31.3 us  [call(): pl.pallas_call(kernel, out_shape=shapes if len(shapes) > 1 else shapes[0]...]
    ppermute x6 -> x3, starting transfers between devices: 9.58 us -> 6.32 us  [shifted(): lax.ppermute(value, axis, [(i, (i + by) % peers) for i in range(peers)])]
    mul x5 -> x0, other arithmetic: 2.82 us -> none  [the longest x1 1.32 us: local_by_zones(): own = (conserved * share).reshape(3 * materials, rows_x, rows_y)]
  transfers between devices with their start and end apart: 8 -> 3, of which waited for: 7 -> 2; matrix products, arithmetic and copies ran while one was open for 4% -> 1% of each run, Pallas kernels for 3% -> 4%
where the time goes in v2:
time: 134 us
  blocking collectives  91.2 us (68%)
  Pallas kernels  31.3 us (23%)
  starting transfers between devices  6.32 us (5%)
  waiting for transfers between devices  2.49 us (2%)
  local copies, waits for them, and re-layouts  2.01 us (1%)
    all_to_all x2, blocking collectives, exchange(): return lax.all_to_all(value, ('zx', 'zy'), 0, 0, tiled=True)  91.2 us
    pallas_call x7, Pallas kernels, call(): pl.pallas_call(kernel, out_shape=shapes if len(shapes) > 1 else shapes[0]...  31.3 us
    ppermute x3, starting transfers between devices, shifted(): lax.ppermute(value, axis, [(i, (i + by) % peers) for i in range(peers)])  6.32 us
  transfers between devices with their start and end apart: 3, of which 2 were waited for; matrix products, arithmetic and copies ran while one was open for 1% of the time, Pallas kernels for 4%

profile of v2, /device:TPU:0, one launch (start us, length us, event | category | flops | bytes accessed | tf_op | source)
XLA Modules:
  0.0 133.9 jit_solution(15844257575614401194)
XLA Ops:
  0.6 2.2 %sums.1 = (f32[2,64,256]{2,1,0:T(8,128)}, f32[16,256]{1,0:T(8,128)}) custom-call(f32[8,64,256]{2,1,0:T(8,128)} %frac_ref.3, f32[8,64,256]{2,1,0:T(8,128)} %density_ref.3, f32[8,64,256]{2,1,0:T(8,128)} %energy_ref.3, f32[2,64,256]{2,1,0:T(8,128)} %shift_ref.3, f32[2,64,256]{2,1,0:T(8,128)} %speed_ref.3), custom_call_target="tpu_custom_call" | custom-call | tf_op jit(solution)/shard_map/sums/pallas_call | solution.py:423
  2.8 2.9 %collective-permute-start = (f32[16,256]{1,0:T(8,128)}, f32[16,256]{1,0:T(8,128)S(1)}, u32[]{:S(2)}, u32[]{:S(2)}) collective-permute-start(f32[16,256]{1,0:T(8,128)} %get-tuple-element.12), channel_id=1, source_target_pairs={{0,16},{16,0},{1,17},{17,1},{2,18},{18,2},{3,19},{19,3},{4,20},{20... | collective-permute-start | bytes 49160 | tf_op jit(solution)/shard_map/ppermute | solution.py:15
  5.8 1.9 %collective-permute-done.above_ref.below_ref = f32[16,256]{1,0:T(8,128)S(1)} collective-permute-done((f32[16,256]{1,0:T(8,128)}, f32[16,256]{1,0:T(8,128)S(1)}, u32[]{:S(2)}, u32[]{:S(2)}) %collective-permute-start) | collective-permute-done | bytes 16416 | tf_op jit(solution)/shard_map/ppermute | solution.py:15
  7.7 0.0 copy-start
  7.7 0.6 copy-done
  8.3 1.9 %rows.1 = (f32[6,72,256]{2,1,0:T(8,128)}, f32[72,128]{1,0:T(8,128)}, f32[72,128]{1,0:T(8,128)}) custom-call(f32[2,64,256]{2,1,0:T(8,128)} %shift_ref.3, f32[2,64,256]{2,1,0:T(8,128)} %speed_ref.3, f32[2,64,256]{2,1,0:T(8,128)} %get-tuple-element.11.sums_ref, f32[16,256]{1,0:T(8,128)} %copy-done, f32[16,256]{1,0:T(8,128)} %copy-done), custom_call_target="tpu_custom_call" | custom-call | tf_op jit(solution)/shard_map/rows/pallas_call | solution.py:423
  10.2 3.4 %collective-permute-start.1 = (f32[72,128]{1,0:T(8,128)}, f32[72,128]{1,0:T(8,128)S(1)}, u32[]{:S(2)}, u32[]{:S(2)}) collective-permute-start(f32[72,128]{1,0:T(8,128)} %get-tuple-element.14), channel_id=1, source_target_pairs={{0,15},{1,0},{2,1},{3,2},{4,3},{5,4},{6,5},{7,6},{8,7},{9,8},{10,9... | collective-permute-start | bytes 110600 | tf_op jit(solution)/shard_map/ppermute | solution.py:15
  13.6 0.0 collective-permute-start.2
  13.6 0.0 copy-start.3
  13.6 3.0 %pack.1.raw_ref = f32[32,96,128]{2,1,0:T(8,128)} custom-call(f32[8,64,256]{2,1,0:T(8,128)} %frac_ref.3, f32[8,64,256]{2,1,0:T(8,128)} %density_ref.3, f32[8,64,256]{2,1,0:T(8,128)} %energy_ref.3), custom_call_target="tpu_custom_call" | custom-call | tf_op jit(solution)/shard_map/pack/pallas_call | solution.py:423
  16.6 0.0 copy-done.3
  16.6 0.8 copy.13.target_ref
  17.4 1.9 %tables.1.tables_ref = f32[16,128]{1,0:T(8,128)} custom-call(s32[1,1]{1,0:T(1,128)} %bitcast.me_ref, s32[256,1]{1,0:T(8,128)} %copy.13.target_ref, s32[1,256]{1,0:T(1,128)} %bitcast.9, s32[1,256]{1,0:T(1,128)} %bitcast.10, f32[1,256]{1,0:T(1,128)} %bitcast.11, f32[1,128]{1,0:T(1,128)} %bitcast.12), custom_call_target="tpu_custom_call" | custom-call | tf_op jit(solution)/shard_map/tables/pallas_call | solution.py:423
  19.3 0.0 collective-permute-done.1.right_ref
  19.3 0.0 copy-start.1
  19.3 0.6 collective-permute-done.2.left_ref
  19.9 0.0 copy-start.2
  19.9 0.1 copy-done.1
  19.9 0.5 copy-done.2
  20.5 4.1 %lagrange.1 = (f32[2,64,256]{2,1,0:T(8,128)}, f32[2,64,256]{2,1,0:T(8,128)}, f32[32,112,128]{2,1,0:T(8,128)}) custom-call(f32[6,72,256]{2,1,0:T(8,128)} %get-tuple-element.13.rows_ref, f32[72,128]{1,0:T(8,128)} %copy-done.1, f32[72,128]{1,0:T(8,128)} %copy-done.2, f32[32,96,128]{2,1,0:T(8,128)} %pack.1.raw_ref, f32[16,128]{1,0:T(8,128)} %tables.1.tables_ref), custom_call_target="tpu_custom_call" | custom-call | tf_op jit(solution)/shard_map/lagrange/pallas_call | solution.py:423
  24.6 49.4 %all_to_all.10.state_ref = f32[32,112,128]{2,1,0:T(8,128)} all-to-all(f32[32,112,128]{2,1,0:T(8,128)} %get-tuple-element.16), channel_id=1, replica_groups=mesh['zx'=2,'zy'=16] {'zx','zy'}, dimensions={0} | all-to-all | bytes 3670016 | tf_op jit(solution)/shard_map/all_to_all | solution.py:434
  73.9 15.2 %crossings.1 = f32[32,96,128]{2,1,0:T(8,128)} custom-call(f32[32,112,128]{2,1,0:T(8,128)} %all_to_all.10.state_ref), custom_call_target="tpu_custom_call" | custom-call | tf_op jit(solution)/shard_map/crossings/pallas_call | solution.py:423
  89.1 41.8 %all_to_all.11.sums_ref = f32[32,96,128]{2,1,0:T(8,128)} all-to-all(f32[32,96,128]{2,1,0:T(8,128)} %crossings.1), channel_id=1, replica_groups=mesh['zx'=2,'zy'=16] {'zx','zy'}, dimensions={0} | all-to-all | bytes 3145728 | tf_op jit(solution)/shard_map/all_to_all | solution.py:434
  130.9 3.0 %unpack.1 = f32[24,64,256]{2,1,0:T(8,128)} custom-call(f32[32,96,128]{2,1,0:T(8,128)} %all_to_all.11.sums_ref), custom_call_target="tpu_custom_call" | custom-call | tf_op jit(solution)/shard_map/unpack/pallas_call | solution.py:423
Async XLA Ops:
  2.8 4.9 %collective-permute-start = (f32[16,256]{1,0:T(8,128)}, f32[16,256]{1,0:T(8,128)S(1)}, u32[]{:S(2)}, u32[]{:S(2)}) collective-permute-start(f32[16,256]{1,0:T(8,128)} %get-tuple-element.12), channel_id=1, source_target_pairs={{0,16},{16,0},{1,17},{17,1},{2,18},{18,2},{3,19},{19,3},{4,20},{20... | collective-permute-start | bytes 49160 | tf_op jit(solution)/shard_map/ppermute | solution.py:15
  7.7 0.6 copy-start
  10.2 9.1 %collective-permute-start.1 = (f32[72,128]{1,0:T(8,128)}, f32[72,128]{1,0:T(8,128)S(1)}, u32[]{:S(2)}, u32[]{:S(2)}) collective-permute-start(f32[72,128]{1,0:T(8,128)} %get-tuple-element.14), channel_id=1, source_target_pairs={{0,15},{1,0},{2,1},{3,2},{4,3},{5,4},{6,5},{7,6},{8,7},{9,8},{10,9... | collective-permute-start | bytes 110600 | tf_op jit(solution)/shard_map/ppermute | solution.py:15
  13.6 6.3 %collective-permute-start.2 = (f32[72,128]{1,0:T(8,128)}, f32[72,128]{1,0:T(8,128)S(1)}, u32[]{:S(2)}, u32[]{:S(2)}) collective-permute-start(f32[72,128]{1,0:T(8,128)} %get-tuple-element.15), channel_id=1, source_target_pairs={{0,1},{1,2},{2,3},{3,4},{4,5},{5,6},{6,7},{7,8},{8,9},{9,10},{10,1... | collective-permute-start | bytes 110600 | tf_op jit(solution)/shard_map/ppermute | solution.py:15
  13.6 3.0 %copy-start.3 = (s32[1,1,256,1]{2,3,1,0:T(1,128)S(1)}, s32[1,1,256,1]{2,3,1,0:T(1,128)}, u32[]{:S(2)}) copy-start(s32[1,1,256,1]{2,3,1,0:T(1,128)} %param.15) | copy-start | bytes 3076
  19.3 0.6 copy-start.1
  19.9 0.6 copy-start.2

commit v3 on v2

--- a/solution.py
+++ b/solution.py
@@ -123,17 +123,16 @@
     return even, odd
 
 
-def pack_kernel(frac_ref, density_ref, energy_ref, out_ref):
+def store_pairs(values, out_ref, row):
     low = lower_half((SUB, LANES))
-    for group, ref in enumerate((frac_ref, density_ref, energy_ref)):
-        for pair in range(ref.shape[0] // 2):
-            first, second = zones_first(ref[2 * pair]), zones_first(ref[2 * pair + 1])
-            row = SUB * (group * (ref.shape[0] // 2) + pair)
-            for octet in range(LANES // SUB):
-                at = slice(SUB * octet, SUB * octet + SUB)
-                even, odd = pair_to_pieces(first[at], second[at], low)
-                out_ref[2 * octet, row : row + SUB, :] = even
-                out_ref[2 * octet + 1, row : row + SUB, :] = odd
+    for pair in range(len(values) // 2):
+        first, second = zones_first(values[2 * pair]), zones_first(values[2 * pair + 1])
+        rows = slice(row + SUB * pair, row + SUB * pair + SUB)
+        for octet in range(LANES // SUB):
+            at = slice(SUB * octet, SUB * octet + SUB)
+            even, odd = pair_to_pieces(first[at], second[at], low)
+            out_ref[2 * octet, rows, :] = even
+            out_ref[2 * octet + 1, rows, :] = odd
 
 
 def split3(value):
@@ -144,41 +143,39 @@
     return high, middle, low
 
 
-def table_kernel(me_ref, target_ref, source_ref, place_ref, weight_ref, keep_ref, out_ref):
+def table_kernel(target_ref, source_ref, place_ref, weight_ref, keep_ref, out_ref):
     entries = target_ref.shape[0]
-    capacity = LANES // SUB
-    me = me_ref[0, 0]
-    target = target_ref[...]
+    column = target_ref[...].astype(jnp.float32)
     down = lax.broadcasted_iota(jnp.int32, (entries, entries), 0)
     across = lax.broadcasted_iota(jnp.int32, (entries, entries), 1)
-    column = target.astype(jnp.float32)
     row = jnp.sum(jnp.where(down == across, column, 0.0), axis=0, keepdims=True)
-    earlier = (row == column) & (across < down)
-    rank = jnp.sum(jnp.where(earlier, 1.0, 0.0), axis=1, keepdims=True).astype(jnp.int32)
-    slot = (target >> 3) * LANES + ((target & 7) ^ (me & 7)) * capacity + rank
-    slots = 4 * LANES
-    hot = jnp.where(lax.broadcasted_iota(jnp.int32, (entries, slots), 1) == slot, 1.0, 0.0)
-    weight = weight_ref[...]
+    earlier = (row < column) | ((row == column) & (across < down))
+    order = jnp.sum(jnp.where(earlier, 1.0, 0.0), axis=1, keepdims=True)
+    hot = jnp.where(across.astype(jnp.float32) == order, 1.0, 0.0)
     source, place = source_ref[...], place_ref[...]
-    source = ((source & 1) * 64 + (source >> 1)).astype(jnp.float32).astype(jnp.bfloat16)
-    place = ((place & 1) * 64 + (place >> 1)).astype(jnp.float32).astype(jnp.bfloat16)
-    parts = [part.astype(jnp.float32) for part in (*split3(weight), source, place)]
+    half = LANES // 2
+    source = ((source & 1) * half + (source >> 1)).astype(jnp.float32)
+    place = ((place & 1) * half + (place >> 1)).astype(jnp.float32)
+    parts = [part.astype(jnp.float32) for part in split3(weight_ref[...])] + [source, place]
     values = jnp.concatenate(parts + [jnp.zeros((SUB - len(parts), entries), jnp.float32)], axis=0)
     tables = jnp.dot(
         values.astype(jnp.bfloat16), hot.astype(jnp.bfloat16), preferred_element_type=jnp.float32
     )
     weights = tables[0:1] + tables[1:2] + tables[2:3]
-    for octet in range(4):
-        at = slice(LANES * octet, LANES * octet + LANES)
-        out_ref[octet : octet + 1, :] = tables[3:4, at]
-        out_ref[4 + octet : 5 + octet, :] = weights[:, at]
-        out_ref[8 + octet : 9 + octet, :] = tables[4:5, at]
+    for table, value in enumerate((tables[3:4], weights, tables[4:5])):
+        for side in range(2):
+            at = slice(LANES * side, LANES * side + LANES)
+            out_ref[2 * table + side : 2 * table + side + 1, :] = value[:, at]
+    device = lax.broadcasted_iota(jnp.int32, (entries, LANES), 1).astype(jnp.float32)
+    out_ref[6:7, :] = jnp.sum(jnp.where(column < device, 1.0, 0.0), axis=0, keepdims=True)
     lane = lax.broadcasted_iota(jnp.int32, (SUB, LANES), 1)
-    block = 2 * (lane % 64) + lane // 64
     keep = jnp.take_along_axis(
-        jnp.broadcast_to(keep_ref[...], (SUB, LANES)), block, axis=1, mode="promise_in_bounds"
-    )
-    out_ref[12:16, :] = keep[0:4]
+        jnp.broadcast_to(keep_ref[...], (SUB, LANES)),
+        2 * (lane % half) + lane // half,
+        axis=1,
+        mode="promise_in_bounds",
+    )
+    out_ref[7:8, :] = keep[0:1]
 
 
 def stiffness(materials):
@@ -186,14 +183,19 @@
     return [float(gamma) for gamma in gammas - np.float32(1.0)]
 
 
-def sums_kernel(frac_ref, density_ref, energy_ref, shift_ref, speed_ref, sums_ref, rim_ref):
-    stiff = stiffness(frac_ref.shape[0])
+def early_kernel(
+    frac_ref, density_ref, energy_ref, shift_ref, speed_ref, out_ref, sums_ref, rim_ref
+):
+    materials = frac_ref.shape[0]
+    stiff = stiffness(materials)
     mass = pressure = None
-    for material in range(frac_ref.shape[0]):
+    held = []
+    for material in range(materials):
         part = frac_ref[material] * density_ref[material]
         force = part * energy_ref[material] * stiff[material]
         mass = part if mass is None else mass + part
         pressure = force if pressure is None else pressure + force
+        held.append(part)
     sums_ref[0], sums_ref[1] = mass, pressure
     last = mass.shape[0] - 1
     for field in range(2):
@@ -203,6 +205,7 @@
     for field, value in enumerate((mass, pressure)):
         rim_ref[8 + field : 9 + field, :] = value[0:1]
         rim_ref[14 + field : 15 + field, :] = value[last : last + 1]
+    store_pairs([frac_ref[material] for material in range(materials)] + held, out_ref, 0)
 
 
 def rows_kernel(shift_ref, speed_ref, sums_ref, above_ref, below_ref, out_ref, first_ref, last_ref):
@@ -226,7 +229,8 @@
 
 
 def lagrange_kernel(
-    rows_ref, right_ref, left_ref, raw_ref, tables_ref, speed_ref, shift_ref, out_ref
+    rows_ref, right_ref, left_ref, frac_ref, density_ref, energy_ref, tables_ref,
+    speed_ref, shift_ref, out_ref,
 ):
     height, width = rows_ref.shape[1] - SUB, rows_ref.shape[2]
     shape = (height + SUB, width + LANES)
@@ -296,36 +300,36 @@
     speed_ref[0], speed_ref[1] = own(speed_x), own(speed_y)
     shift_ref[0], shift_ref[1] = own(shift_x), own(shift_y)
 
-    low = lower_half((SUB, LANES))
-    area, after, viscous = [zones_first(own(value)) for value in (area, after, viscous)]
-    pairs = raw_ref.shape[1] // (3 * SUB)
-    stiff = stiffness(2 * pairs)
-    for octet in range(LANES // SUB):
-        at = slice(SUB * octet, SUB * octet + SUB)
-        tiles = [pair_to_pieces(value[at], value[at], low) for value in (area, after, viscous)]
-        for side in range(2):
-            piece = 2 * octet + side
-            now, then, thick = [tile[side] for tile in tiles]
-            change = then - now
-            for pair in range(pairs):
-                at_pair = [slice(SUB * (pair + pairs * g), SUB * (pair + pairs * g) + SUB) for g in range(3)]
-                frac, rho, heat = [raw_ref[piece, rows] for rows in at_pair]
-                held = frac * rho
-                mass_now = held * now
-                force = jnp.where(low, stiff[2 * pair], stiff[2 * pair + 1]) * rho * heat
-                out_ref[piece, at_pair[0]] = frac * then
-                out_ref[piece, at_pair[1]] = mass_now
-                out_ref[piece, at_pair[2]] = mass_now * heat - frac * (force + thick) * change
-            end = 3 * SUB * pairs
-            out_ref[piece, end : end + 2 * SUB] = tables_ref[...]
-
-
-def crossing_kernel(state_ref, out_ref, slots_ref, places_ref):
-    devices = state_ref.shape[0]
-    rows = state_ref.shape[1] - 2 * SUB
+    area, after, viscous = own(area), own(after), own(viscous)
+    change = after - area
+    materials = frac_ref.shape[0]
+    values = []
+    for material, stiff in enumerate(stiffness(materials)):
+        frac, density, energy = frac_ref[material], density_ref[material], energy_ref[material]
+        force = stiff * density * energy + viscous
+        values.append(frac * density * area * energy - frac * force * change)
+    store_pairs(values + [area, after], out_ref, 0)
+    for piece in range(out_ref.shape[0]):
+        out_ref[piece, (materials + 2) * QUAD : (materials + 2) * QUAD + SUB] = tables_ref[...]
+
+
+def crossing_kernel(
+    early_ref, late_ref, out_ref, state_ref, even_ref, odd_ref, places_ref, sources_ref, weights_ref
+):
+    devices, rows = state_ref.shape[0], state_ref.shape[1]
+    table_row = late_ref.shape[1] - SUB
     tiles = rows // SUB
-    piece = lax.broadcasted_iota(jnp.int32, (SUB, LANES), 1) // (LANES // SUB)
+    groups = devices // SUB
+    capacity = LANES // SUB
+    slots_ref = (even_ref, odd_ref)
+    spread = (SUB, LANES)
+    lane = lax.broadcasted_iota(jnp.int32, spread, 1)
+    source_of = lax.broadcasted_iota(jnp.int32, spread, 0)
+    piece = lane // capacity
     odd = [(piece >> bit) & 1 == 1 for bit in range(3)]
+
+    def take(values, index):
+        return jnp.take_along_axis(values, index, axis=1, mode="promise_in_bounds")
 
     def regroup(values):
         for bit in range(3):
@@ -337,62 +341,89 @@
             ]
         return values
 
-    def gather(a, carry):
-        for octet in range(devices // SUB):
-            index, weight, place = [], [], []
-            for sigma in range(SUB):
-                source = a * SUB + sigma
-                spread = (SUB, LANES)
-                index.append(
-                    jnp.broadcast_to(state_ref[source, rows + octet : rows + octet + 1], spread).astype(jnp.int32)
-                )
-                weight.append(jnp.broadcast_to(state_ref[source, rows + 4 + octet : rows + octet + 5], spread))
-                place.append(jnp.broadcast_to(state_ref[source, rows + 8 + octet : rows + octet + 9], spread))
-            for delta, value in enumerate(regroup(place)):
+    low = lower_half(spread)
+    third = rows // 3
+
+    def conserve(source, carry):
+        areas = late_ref[source, third : third + SUB]
+        swapped = pltpu.roll(areas, QUAD, 0)
+        area, after = jnp.where(low, areas, swapped), jnp.where(low, swapped, areas)
+        for tile in range(tiles // 3):
+            at = [slice(SUB * tile + third * g, SUB * tile + third * g + SUB) for g in range(3)]
+            state_ref[source, at[0]] = early_ref[source, at[0]] * after
+            state_ref[source, at[1]] = early_ref[source, at[1]] * area
+            state_ref[source, at[2]] = late_ref[source, at[0]]
+        return carry
+
+    lax.fori_loop(0, devices, conserve, 0, unroll=4)
+    for a in range(groups):
+        table = [late_ref[a * SUB : a * SUB + SUB, table_row + i, :] for i in range(7)]
+        starts = table[6].astype(jnp.int32)
+        for octet in range(groups):
+            target = SUB * octet + (piece ^ source_of)
+            at = take(starts, target) + lane % capacity
+            valid = at < take(starts, target + 1)
+            later, at = at >= LANES, at & (LANES - 1)
+            source, weight, place = [
+                jnp.where(later, take(table[2 * i + 1], at), take(table[2 * i], at)) for i in range(3)
+            ]
+            sources_ref[octet, a] = source
+            weights_ref[octet, a] = jnp.where(valid, weight, 0.0)
+            places = [jnp.broadcast_to(place[i : i + 1], spread) for i in range(SUB)]
+            for delta, value in enumerate(regroup(places)):
                 places_ref[SUB * octet + delta, a] = value
-            for tile in range(tiles):
-                at = slice(SUB * tile, SUB * tile + SUB)
-                values = [
-                    jnp.take_along_axis(
-                        state_ref[a * SUB + sigma, at], index[sigma], axis=1, mode="promise_in_bounds"
-                    )
-                    * weight[sigma]
-                    for sigma in range(SUB)
-                ]
-                for delta, value in enumerate(regroup(values)):
-                    slots_ref[SUB * octet + delta, a, at] = value
-        return carry
-
-    lax.fori_loop(0, devices // SUB, gather, 0)
-
-    def scatter(target, carry):
-        groups = devices // SUB
-        value = jnp.concatenate([slots_ref[target, a] for a in range(groups)], axis=1)
+
+    def gather(octet, a):
+        sources, weights = sources_ref[octet, a].astype(jnp.int32), weights_ref[octet, a]
+        index = [jnp.broadcast_to(sources[i : i + 1], spread) for i in range(SUB)]
+        weight = [jnp.broadcast_to(weights[i : i + 1], spread) for i in range(SUB)]
+        for first in range(0, tiles, tiles // 2):
+            at = [slice(SUB * tile, SUB * tile + SUB) for tile in range(first, first + tiles // 2)]
+            values = [
+                [take(state_ref[a * SUB + i, rows_of], index[i]) * weight[i] for rows_of in at]
+                for i in range(SUB)
+            ]
+            for tile, rows_of in enumerate(at):
+                for delta, value in enumerate(regroup([value[tile] for value in values])):
+                    slots_ref[octet % 2][delta, a, rows_of] = value
+
+    block = lax.broadcasted_iota(jnp.int32, spread, 0).astype(jnp.float32)
+
+    def scatter(octet, delta):
+        target = SUB * octet + delta
+        slots = slots_ref[octet % 2]
+        value = jnp.concatenate([slots[delta, a] for a in range(groups)], axis=1)
         parts = jnp.concatenate(split3(value), axis=0)
         place = [places_ref[target, a] for a in range(groups)]
-        block = lax.broadcasted_iota(jnp.int32, (SUB, LANES), 0).astype(jnp.float32)
-        hot = jnp.concatenate(
+        hot = [
             [
-                jnp.concatenate(
-                    [
-                        jnp.where(place[a] == block + float(SUB * tile), 1.0, 0.0)
-                        for tile in range(LANES // SUB)
-                    ],
-                    axis=0,
-                )
-                for a in range(groups)
-            ],
-            axis=1,
-        ).astype(jnp.bfloat16)
+                jnp.where(place[a] == block + float(SUB * tile), 1.0, 0.0)
+                for tile in range(LANES // SUB)
+            ]
+            for a in range(groups)
+        ]
+        hot = jnp.concatenate([jnp.concatenate(column, axis=0) for column in hot], axis=1)
         total = lax.dot_general(
-            parts, hot, (((1,), (1,)), ((), ())), preferred_element_type=jnp.float32
+            parts,
+            hot.astype(jnp.bfloat16),
+            (((1,), (1,)), ((), ())),
+            preferred_element_type=jnp.float32,
         )
-        keep = jnp.broadcast_to(state_ref[target, rows + 12 : rows + 13], (rows, LANES))
+        keep = jnp.broadcast_to(late_ref[target, table_row + 7 : table_row + 8], (rows, LANES))
         stay = keep * state_ref[target, 0:rows]
         out_ref[target] = stay + total[0:rows] + total[rows : 2 * rows] + total[2 * rows : 3 * rows]
-        return carry
-
-    lax.fori_loop(0, devices, scatter, 0)
+
+    lax.fori_loop(0, groups, lambda a, carry: (gather(0, a), carry)[1], 0)
+    for octet in range(groups):
+
+        def step(a, carry):
+            if octet + 1 < groups:
+                gather(octet + 1, a)
+            for i in range(SUB // groups):
+                scatter(octet, SUB // groups * a + i)
+            return carry
+
+        lax.fori_loop(0, groups, step, 0, unroll=True)
 
 
 def unpack_kernel(sums_ref, out_ref):
@@ -415,15 +446,12 @@
     return [pl.BlockSpec(memory_space=pltpu.VMEM)] * count
 
 
-def call(kernel, name, outs, inputs, scratch=(), cycles=0):
-    specs = [
-        pl.BlockSpec(memory_space=pltpu.SMEM if value.size == 1 else pltpu.VMEM) for value in inputs
-    ]
+def call(kernel, name, outs, inputs, scratch=()):
     shapes = [jax.ShapeDtypeStruct(shape, jnp.float32) for shape in outs]
     return pl.pallas_call(
         kernel,
         out_shape=shapes if len(shapes) > 1 else shapes[0],
-        in_specs=specs,
+        in_specs=whole(len(inputs)),
         out_specs=whole(len(shapes)) if len(shapes) > 1 else whole(1)[0],
         scratch_shapes=[pltpu.VMEM(shape, jnp.float32) for shape in scratch],
         name=name,
@@ -452,9 +480,13 @@
     fields = 3 * materials
     rows = fields * QUAD
     plane = (2, rows_x, rows_y)
-    sums, rim = call(
-        sums_kernel, "sums", [plane, (16, rows_y)], (frac, density, energy, node_shift, node_speed)
-    )
+    early, sums, rim = call(
+        early_kernel,
+        "early",
+        [(devices, 2 * materials * QUAD, LANES), plane, (16, rows_y)],
+        (frac, density, energy, node_shift, node_speed),
+    )
+    early = exchange(early)
     above = shifted(rim, "zx", -1)
     below = above if lax.axis_size("zx") == 2 else shifted(rim, "zx", 1)
     tall = (rows_x + SUB, LANES)
@@ -466,28 +498,30 @@
     )
     right = shifted(first, "zy", -1)
     left = shifted(last, "zy", 1)
-    me = (lax.axis_index("zx") * lax.axis_size("zy") + lax.axis_index("zy")).astype(jnp.int32)
     tables = call(
         table_kernel,
         "tables",
-        [(16, LANES)],
-        (me.reshape(1, 1), dest_tile[0, 0], src_block[0], dest_block[0], crossing[0], keep[0]),
-    )
-    raw = call(pack_kernel, "pack", [(devices, rows, LANES)], (frac, density, energy))
-    speed_after, shift_after, state = call(
+        [(SUB, LANES)],
+        (dest_tile[0, 0], src_block[0], dest_block[0], crossing[0], keep[0]),
+    )
+    speed_after, shift_after, late = call(
         lagrange_kernel,
         "lagrange",
-        [plane, plane, (devices, rows + 2 * SUB, LANES)],
-        (extended, right, left, raw, tables),
-    )
-    state = exchange(state)
+        [plane, plane, (devices, (materials + 2) * QUAD + SUB, LANES)],
+        (extended, right, left, frac, density, energy, tables),
+    )
+    early, late = lax.optimization_barrier((early, late))
+    late = exchange(late)
     groups = devices // SUB
     totals = call(
         crossing_kernel,
         "crossings",
         [(devices, rows, LANES)],
-        (state,),
-        scratch=[(devices, groups, rows, LANES), (devices, groups, SUB, LANES)],
+        (early, late),
+        scratch=[(devices, rows, LANES)]
+        + [(SUB, groups, rows, LANES)] * 2
+        + [(devices, groups, SUB, LANES)]
+        + [(groups, groups, SUB, LANES)] * 2,
     )
     totals = exchange(totals)
     remapped = call(unpack_kernel, "unpack", [(fields, rows_x, rows_y)], (totals,))

time: 134 us -> 120 us (0.90)
  blocking collectives: 91.2 us -> 69.8 us
  Pallas kernels: 31.3 us -> 21.6 us
  waiting for transfers between devices: 2.49 us -> 11.4 us
  starting transfers between devices: 6.32 us -> 13.8 us
    all_to_all x2, blocking collectives: 91.2 us -> 69.8 us  [exchange(): return lax.all_to_all(value, ('zx', 'zy'), 0, 0, tiled=True)]
    pallas_call x7 -> x6, Pallas kernels: 31.3 us -> 21.6 us  [call(): pl.pallas_call(kernel, out_shape=shapes if len(shapes) > 1 else shapes[0]...]
    ppermute x3, waiting for transfers between devices: 2.49 us -> 11.4 us  [shifted(): lax.ppermute(value, axis, [(i, (i + by) % peers) for i in range(peers)])]
    all_to_all x0 -> x1, starting transfers between devices: none -> 7.3 us  [exchange(): return lax.all_to_all(value, ('zx', 'zy'), 0, 0, tiled=True)]
  transfers between devices with their start and end apart: 3 -> 4, of which waited for: 2 -> 3; matrix products, arithmetic and copies ran while one was open for 1% -> 1% of each run, Pallas kernels for 4% -> 6%
where the time goes in v3:
time: 120 us; the launch traced here: 119 us
  blocking collectives  69.8 us (58%)
  Pallas kernels  21.6 us (18%)
  starting transfers between devices  13.8 us (12%)
  waiting for transfers between devices  11.4 us (10%)
  local copies, waits for them, and re-layouts  2.01 us (2%)
    all_to_all x2, blocking collectives, exchange(): return lax.all_to_all(value, ('zx', 'zy'), 0, 0, tiled=True)  69.8 us
    pallas_call x6, Pallas kernels, call(): pl.pallas_call(kernel, out_shape=shapes if len(shapes) > 1 else shapes[0]...  21.6 us
    ppermute x3, waiting for transfers between devices, shifted(): lax.ppermute(value, axis, [(i, (i + by) % peers) for i in range(peers)])  11.4 us
    all_to_all x1, starting transfers between devices, exchange(): return lax.all_to_all(value, ('zx', 'zy'), 0, 0, tiled=True)  7.3 us
    ppermute x3, starting transfers between devices, shifted(): lax.ppermute(value, axis, [(i, (i + by) % peers) for i in range(peers)])  6.5 us
  transfers between devices with their start and end apart: 4, of which 3 were waited for; matrix products, arithmetic and copies ran while one was open for 1% of the time, Pallas kernels for 6%

profile of v3, /device:TPU:0, one launch (start us, length us, event | category | flops | bytes accessed | tf_op | source)
XLA Modules:
  0.0 119.2 jit_solution(3378764366176864363)
XLA Ops:
  0.6 2.8 %early.1 = (f32[32,64,128]{2,1,0:T(8,128)}, f32[2,64,256]{2,1,0:T(8,128)}, f32[16,256]{1,0:T(8,128)}) custom-call(f32[8,64,256]{2,1,0:T(8,128)} %frac_ref.3, f32[8,64,256]{2,1,0:T(8,128)} %density_ref.3, f32[8,64,256]{2,1,0:T(8,128)} %energy_ref.3, f32[2,64,256]{2,1,0:T(8,128)} %shift_ref.3, f32[2,64,256]{2,1,0:T(8,128)} %speed_ref.3), custom_call_target="tpu_custom_call" | custom-call | tf_op jit(solution)/shard_map/early/pallas_call | solution.py:451
  3.4 0.0 copy-start.5
  3.4 0.0 copy-start.4
  3.4 7.3 %all-to-all-start = ((f32[32,64,128]{2,1,0:T(8,128)}), f32[32,64,128]{2,1,0:T(8,128)S(1)}, u32[]{:S(2)}, u32[]{:S(2)}) async-start(f32[32,64,128]{2,1,0:T(8,128)} %get-tuple-element.14), calls=%async_computation | async-start | bytes 2097152 | tf_op jit(solution)/shard_map/all_to_all | solution.py:462
  10.7 0.0 copy-done.5
  10.7 1.8 %collective-permute-start = (f32[16,256]{1,0:T(8,128)S(1)}, f32[16,256]{1,0:T(8,128)S(1)}, u32[]{:S(2)}, u32[]{:S(2)}) collective-permute-start(f32[16,256]{1,0:T(8,128)S(1)} %copy-done.5), channel_id=1, source_target_pairs={{0,16},{16,0},{1,17},{17,1},{2,18},{18,2},{3,19},{19,3},{4,20},{20... | collective-permute-start | bytes 49160 | tf_op jit(solution)/shard_map/ppermute | solution.py:15
  12.5 6.3 %collective-permute-done.above_ref.below_ref = f32[16,256]{1,0:T(8,128)S(1)} collective-permute-done((f32[16,256]{1,0:T(8,128)S(1)}, f32[16,256]{1,0:T(8,128)S(1)}, u32[]{:S(2)}, u32[]{:S(2)}) %collective-permute-start) | collective-permute-done | bytes 16416 | tf_op jit(solution)/shard_map/ppermute | solution.py:15
  18.8 0.0 copy-start.1
  18.8 0.6 copy-done.1
  19.4 1.9 %rows.1 = (f32[6,72,256]{2,1,0:T(8,128)}, f32[72,128]{1,0:T(8,128)}, f32[72,128]{1,0:T(8,128)}) custom-call(f32[2,64,256]{2,1,0:T(8,128)} %shift_ref.3, f32[2,64,256]{2,1,0:T(8,128)} %speed_ref.3, f32[2,64,256]{2,1,0:T(8,128)} %get-tuple-element.15.sums_ref, f32[16,256]{1,0:T(8,128)} %copy-done.1, f32[16,256]{1,0:T(8,128)} %copy-done.1), custom_call_target="tpu_custom_call" | custom-call | tf_op jit(solution)/shard_map/rows/pallas_call | solution.py:451
  21.3 4.7 %collective-permute-start.1 = (f32[72,128]{1,0:T(8,128)}, f32[72,128]{1,0:T(8,128)S(1)}, u32[]{:S(2)}, u32[]{:S(2)}) collective-permute-start(f32[72,128]{1,0:T(8,128)} %get-tuple-element.18), channel_id=1, source_target_pairs={{0,15},{1,0},{2,1},{3,2},{4,3},{5,4},{6,5},{7,6},{8,7},{9,8},{10,9... | collective-permute-start | bytes 110600 | tf_op jit(solution)/shard_map/ppermute | solution.py:15
  26.0 0.0 collective-permute-start.2
  26.0 0.0 copy-done.4
  26.0 0.8 copy.13.target_ref
  26.8 1.9 %tables.1.tables_ref = f32[8,128]{1,0:T(8,128)} custom-call(s32[256,1]{1,0:T(8,128)} %copy.13.target_ref, s32[1,256]{1,0:T(1,128)} %bitcast.8, s32[1,256]{1,0:T(1,128)} %bitcast.9, f32[1,256]{1,0:T(1,128)} %bitcast.10, f32[1,128]{1,0:T(1,128)} %bitcast.11), custom_call_target="tpu_custom_call" | custom-call | tf_op jit(solution)/shard_map/tables/pallas_call | solution.py:451
  28.7 0.4 collective-permute-done.1.right_ref
  29.0 0.0 copy-start.2
  29.0 4.7 %collective-permute-done.2.left_ref = f32[72,128]{1,0:T(8,128)S(1)} collective-permute-done((f32[72,128]{1,0:T(8,128)}, f32[72,128]{1,0:T(8,128)S(1)}, u32[]{:S(2)}, u32[]{:S(2)}) %collective-permute-start.2) | collective-permute-done | bytes 36896 | tf_op jit(solution)/shard_map/ppermute | solution.py:15
  33.7 0.0 copy-start.3
  33.7 0.0 copy-done.2
  33.7 0.6 copy-done.3
  34.3 3.8 %lagrange.1 = (f32[2,64,256]{2,1,0:T(8,128)}, f32[2,64,256]{2,1,0:T(8,128)}, f32[32,48,128]{2,1,0:T(8,128)}) custom-call(f32[6,72,256]{2,1,0:T(8,128)} %get-tuple-element.17.rows_ref, f32[72,128]{1,0:T(8,128)} %copy-done.2, f32[72,128]{1,0:T(8,128)} %copy-done.3, f32[8,64,256]{2,1,0:T(8,128)} %frac_ref.3, f32[8,64,256]{2,1,0:T(8,128)} %density_ref.3, ...), custom_call_target="tpu_custom_call" | custom-call | tf_op jit(solution)/shard_map/lagrange/pallas_call | solution.py:451
  38.1 0.0 all-to-all-done.early_ref
  38.1 0.0 copy-start
  38.1 27.9 %all_to_all.15.late_ref = f32[32,48,128]{2,1,0:T(8,128)} all-to-all(f32[32,48,128]{2,1,0:T(8,128)} %get-tuple-element.22), channel_id=1, replica_groups=mesh['zx'=2,'zy'=16] {'zx','zy'}, dimensions={0} | all-to-all | bytes 1572864 | tf_op jit(solution)/shard_map/all_to_all | solution.py:462
  66.1 0.0 copy-done
  66.1 8.3 %crossings.1 = f32[32,96,128]{2,1,0:T(8,128)} custom-call(f32[32,64,128]{2,1,0:T(8,128)} %copy-done, f32[32,48,128]{2,1,0:T(8,128)} %all_to_all.15.late_ref), custom_call_target="tpu_custom_call" | custom-call | tf_op jit(solution)/shard_map/crossings/pallas_call | solution.py:451
  74.3 41.8 %all_to_all.16.sums_ref = f32[32,96,128]{2,1,0:T(8,128)} all-to-all(f32[32,96,128]{2,1,0:T(8,128)} %crossings.1), channel_id=1, replica_groups=mesh['zx'=2,'zy'=16] {'zx','zy'}, dimensions={0} | all-to-all | bytes 3145728 | tf_op jit(solution)/shard_map/all_to_all | solution.py:462
  116.2 3.0 %unpack.1 = f32[24,64,256]{2,1,0:T(8,128)} custom-call(f32[32,96,128]{2,1,0:T(8,128)} %all_to_all.16.sums_ref), custom_call_target="tpu_custom_call" | custom-call | tf_op jit(solution)/shard_map/unpack/pallas_call | solution.py:451
Async XLA Ops:
  3.4 7.3 %copy-start.5 = (f32[16,256]{1,0:T(8,128)S(1)}, f32[16,256]{1,0:T(8,128)}, u32[]{:S(2)}) copy-start(f32[16,256]{1,0:T(8,128)} %get-tuple-element.16) | copy-start | bytes 49156
  3.4 22.6 %copy-start.4 = (s32[1,1,256,1]{2,3,1,0:T(1,128)S(1)}, s32[1,1,256,1]{2,3,1,0:T(1,128)}, u32[]{:S(2)}) copy-start(s32[1,1,256,1]{2,3,1,0:T(1,128)} %param.15) | copy-start | bytes 3076
  3.4 34.7 %all-to-all-start = ((f32[32,64,128]{2,1,0:T(8,128)}), f32[32,64,128]{2,1,0:T(8,128)S(1)}, u32[]{:S(2)}, u32[]{:S(2)}) async-start(f32[32,64,128]{2,1,0:T(8,128)} %get-tuple-element.14), calls=%async_computation | async-start | bytes 2097152 | tf_op jit(solution)/shard_map/all_to_all | solution.py:462
  10.7 8.1 %collective-permute-start = (f32[16,256]{1,0:T(8,128)S(1)}, f32[16,256]{1,0:T(8,128)S(1)}, u32[]{:S(2)}, u32[]{:S(2)}) collective-permute-start(f32[16,256]{1,0:T(8,128)S(1)} %copy-done.5), channel_id=1, source_target_pairs={{0,16},{16,0},{1,17},{17,1},{2,18},{18,2},{3,19},{19,3},{4,20},{20... | collective-permute-start | bytes 49160 | tf_op jit(solution)/shard_map/ppermute | solution.py:15
  18.8 0.6 copy-start.1
  21.3 7.7 %collective-permute-start.1 = (f32[72,128]{1,0:T(8,128)}, f32[72,128]{1,0:T(8,128)S(1)}, u32[]{:S(2)}, u32[]{:S(2)}) collective-permute-start(f32[72,128]{1,0:T(8,128)} %get-tuple-element.18), channel_id=1, source_target_pairs={{0,15},{1,0},{2,1},{3,2},{4,3},{5,4},{6,5},{7,6},{8,7},{9,8},{10,9... | collective-permute-start | bytes 110600 | tf_op jit(solution)/shard_map/ppermute | solution.py:15
  26.0 7.8 %collective-permute-start.2 = (f32[72,128]{1,0:T(8,128)}, f32[72,128]{1,0:T(8,128)S(1)}, u32[]{:S(2)}, u32[]{:S(2)}) collective-permute-start(f32[72,128]{1,0:T(8,128)} %get-tuple-element.19), channel_id=1, source_target_pairs={{0,1},{1,2},{2,3},{3,4},{4,5},{5,6},{6,7},{7,8},{8,9},{9,10},{10,1... | collective-permute-start | bytes 110600 | tf_op jit(solution)/shard_map/ppermute | solution.py:15
  29.0 4.7 %copy-start.2 = (f32[72,128]{1,0:T(8,128)}, f32[72,128]{1,0:T(8,128)S(1)}, u32[]{:S(2)}) copy-start(f32[72,128]{1,0:T(8,128)S(1)} %collective-permute-done.1.right_ref) | copy-start | bytes 110596
  33.7 0.6 copy-start.3
  38.1 27.9 %copy-start = (f32[32,64,128]{2,1,0:T(8,128)}, f32[32,64,128]{2,1,0:T(8,128)S(1)}, u32[]{:S(2)}) copy-start(f32[32,64,128]{2,1,0:T(8,128)S(1)} %all-to-all-done.early_ref) | copy-start | bytes 3145732

commit v4 on v3

--- a/solution.py
+++ b/solution.py
@@ -144,11 +144,11 @@
 
 
 def table_kernel(target_ref, source_ref, place_ref, weight_ref, keep_ref, out_ref):
-    entries = target_ref.shape[0]
-    column = target_ref[...].astype(jnp.float32)
+    entries = target_ref.shape[1]
+    row = target_ref[...].astype(jnp.float32)
     down = lax.broadcasted_iota(jnp.int32, (entries, entries), 0)
     across = lax.broadcasted_iota(jnp.int32, (entries, entries), 1)
-    row = jnp.sum(jnp.where(down == across, column, 0.0), axis=0, keepdims=True)
+    column = jnp.sum(jnp.where(down == across, row, 0.0), axis=1, keepdims=True)
     earlier = (row < column) | ((row == column) & (across < down))
     order = jnp.sum(jnp.where(earlier, 1.0, 0.0), axis=1, keepdims=True)
     hot = jnp.where(across.astype(jnp.float32) == order, 1.0, 0.0)
@@ -201,50 +201,100 @@
     for field in range(2):
         for at, ref in ((0, shift_ref), (4, speed_ref)):
             rim_ref[at + 2 * field : at + 2 * field + 2, :] = ref[field, 0:2, :]
-            rim_ref[10 + at // 2 + field : 11 + at // 2 + field, :] = ref[field, last : last + 1, :]
+            for copy in range(2):
+                row = 16 + at + 2 * field + copy
+                rim_ref[row : row + 1, :] = ref[field, last : last + 1, :]
     for field, value in enumerate((mass, pressure)):
         rim_ref[8 + field : 9 + field, :] = value[0:1]
-        rim_ref[14 + field : 15 + field, :] = value[last : last + 1]
+        rim_ref[24 + field : 25 + field, :] = value[last : last + 1]
     store_pairs([frac_ref[material] for material in range(materials)] + held, out_ref, 0)
 
 
-def rows_kernel(shift_ref, speed_ref, sums_ref, above_ref, below_ref, out_ref, first_ref, last_ref):
+def columns_kernel(shift_ref, speed_ref, sums_ref, out_ref):
     height, width = shift_ref.shape[1:]
+    lane = lax.broadcasted_iota(jnp.int32, (height, LANES), 1)
+    wanted = jnp.zeros((height, LANES), jnp.float32)
     for field in range(6):
-        value = (shift_ref, speed_ref, sums_ref)[field // 2][field % 2]
-        out_ref[field, 1 : height + 1, :] = value
-        out_ref[field, 0:1, :] = below_ref[10 + field : 11 + field, :]
-        if field < 4:
-            out_ref[field, height + 1 : height + 3, :] = above_ref[2 * field : 2 * field + 2, :]
-        else:
-            for row in (1, 2):
-                out_ref[field, height + row : height + row + 1, :] = above_ref[4 + field : 5 + field, :]
-        out_ref[field, height + 3 : height + 8, :] = jnp.zeros((5, width), jnp.float32)
-        whole_column = out_ref[field]
-        if field < 4:
-            first_ref[:, 2 * field : 2 * field + 2] = whole_column[:, 0:2]
-        else:
-            first_ref[:, 4 + field : 5 + field] = whole_column[:, 0:1]
-        last_ref[:, field : field + 1] = whole_column[:, width - 1 : width]
+        ref = (shift_ref, speed_ref, sums_ref)[field // 2]
+        first = ref[field % 2, :, :LANES]
+        last = ref[field % 2, :, width - LANES :]
+        row = 2 * field if field < 4 else 4 + field
+        for column in range(2 if field < 4 else 1):
+            moved = pltpu.roll(first, row, 1) if row else first
+            wanted = jnp.where(lane == row + column, moved, wanted)
+        wanted = jnp.where(lane == 16 + row, pltpu.roll(last, 17 + row, 1), wanted)
+    wanted = jnp.concatenate([wanted, jnp.zeros((LANES - height, LANES), jnp.float32)], axis=0)
+    out_ref[...] = wanted.T[0 : out_ref.shape[0]]
+
+
+def corners_kernel(columns_ref, above_ref, below_ref, first_ref, last_ref):
+    height, width = 64, above_ref.shape[1]
+    shape = (16, LANES)
+    lane = lax.broadcasted_iota(jnp.int32, shape, 1)
+    row = lax.broadcasted_iota(jnp.int32, shape, 0)
+    second = (row % 2 == 1) & (row < 8)
+
+    def column(ref, base, at):
+        return jnp.broadcast_to(ref[base : base + 16, at : at + 1], shape)
+
+    def up(value):
+        return pltpu.roll(value, 15, 0)
+
+    def down(value):
+        return pltpu.roll(value, 1, 0)
+
+    left, right = column(above_ref, 0, 0), column(above_ref, 0, 1)
+    value = columns_ref[0:16]
+    value = jnp.where(lane == height, jnp.where(second, down(right), left), value)
+    value = jnp.where(lane == height + 1, jnp.where(second, right, up(left)), value)
+    under = jnp.where(second, column(below_ref, 16, 1), column(below_ref, 16, 0))
+    first_ref[...] = jnp.where(lane == LANES - 1, under, value)
+    end = column(above_ref, 0, width - 1)
+    value = jnp.where(lane == height, end, columns_ref[16:32])
+    value = jnp.where(lane == height + 1, up(end), value)
+    last_ref[...] = jnp.where(lane == LANES - 1, column(below_ref, 16, width - 1), value)
 
 
 def lagrange_kernel(
-    rows_ref, right_ref, left_ref, frac_ref, density_ref, energy_ref, tables_ref,
-    speed_ref, shift_ref, out_ref,
+    now_shift_ref,
+    now_speed_ref,
+    sums_ref,
+    above_ref,
+    below_ref,
+    right_ref,
+    left_ref,
+    frac_ref,
+    density_ref,
+    energy_ref,
+    tables_ref,
+    speed_ref,
+    shift_ref,
+    out_ref,
 ):
-    height, width = rows_ref.shape[1] - SUB, rows_ref.shape[2]
+    height, width = sums_ref.shape[1:]
     shape = (height + SUB, width + LANES)
     lane = lax.broadcasted_iota(jnp.int32, shape, 1)
-    right, left = right_ref[...], left_ref[...]
+    line = lax.broadcasted_iota(jnp.int32, (shape[0], width), 0)
+    sides = [pltpu.roll(ref[...], 1, 1) for ref in (right_ref, left_ref)]
+    sides.append(jnp.zeros((LANES - 32, LANES), jnp.float32))
+    sides = jnp.concatenate(sides, axis=0).T[0 : shape[0]]
 
     def extend(field):
-        value = jnp.concatenate([rows_ref[field], jnp.zeros((shape[0], LANES), jnp.float32)], axis=1)
+        value = (now_shift_ref, now_speed_ref, sums_ref)[field // 2][field % 2]
+        value = jnp.concatenate([value, jnp.zeros((SUB, width), jnp.float32)], axis=0)
+        value = pltpu.roll(value, 1, 0)
+        at = 2 * field if field < 4 else 4 + field
+        value = jnp.where(line == 0, below_ref[16 + at : 17 + at, :], value)
+        value = jnp.where(line == height + 1, above_ref[at : at + 1, :], value)
+        if field < 4:
+            value = jnp.where(line == height + 2, above_ref[at + 1 : at + 2, :], value)
+        value = jnp.concatenate([value, jnp.zeros((shape[0], LANES), jnp.float32)], axis=1)
         value = pltpu.roll(value, 1, 1)
-        value = jnp.where(lane == 0, left[:, field : field + 1], value)
+        value = jnp.where(lane == 0, sides[:, 16 + at : 17 + at], value)
+        value = jnp.where(lane == width + 1, sides[:, at : at + 1], value)
         if field < 4:
-            value = jnp.where(lane == width + 1, right[:, 2 * field : 2 * field + 1], value)
-            return jnp.where(lane == width + 2, right[:, 2 * field + 1 : 2 * field + 2], value)
-        return jnp.where(lane == width + 1, right[:, 4 + field : 5 + field], value)
+            value = jnp.where(lane == width + 2, sides[:, at + 1 : at + 2], value)
+        return value
 
     def next_row(value):
         return pltpu.roll(value, shape[0] - 1, 0)
@@ -426,9 +476,14 @@
         lax.fori_loop(0, groups, step, 0, unroll=True)
 
 
-def unpack_kernel(sums_ref, out_ref):
+UNPACK_PARTS = 4
+
+
+def unpack_kernel(sums_ref, out_ref, rows_ref, sems):
     low = lower_half((SUB, LANES))
     half = LANES // 2
+    fields = out_ref.shape[0] // UNPACK_PARTS
+    copies = []
     for pair in range(sums_ref.shape[1] // SUB):
         at = slice(SUB * pair, SUB * pair + SUB)
         first, second = [], []
@@ -438,16 +493,44 @@
             second.append(odd)
         for field, tiles in ((2 * pair, first), (2 * pair + 1, second)):
             blocks = jnp.concatenate(tiles, axis=0).T
-            out_ref[field, :, :LANES] = blocks[:half]
-            out_ref[field, :, LANES:] = blocks[half:]
+            rows_ref[field, :, :LANES] = blocks[:half]
+            rows_ref[field, :, LANES:] = blocks[half:]
+        if (2 * pair + 2) % fields == 0:
+            part = pl.ds(2 * pair + 2 - fields, fields)
+            sem = sems.at[len(copies)]
+            copies.append(pltpu.make_async_copy(rows_ref.at[part], out_ref.at[part], sem))
+            copies[-1].start()
+    for copy in copies:
+        copy.wait()
+
+
+def unpack(sums, shape):
+    return pl.pallas_call(
+        unpack_kernel,
+        out_shape=jax.ShapeDtypeStruct(shape, jnp.float32),
+        in_specs=whole(1),
+        out_specs=pl.BlockSpec(memory_space=pl.ANY),
+        scratch_shapes=[pltpu.VMEM(shape, jnp.float32), pltpu.SemaphoreType.DMA((UNPACK_PARTS,))],
+        name="unpack",
+    )(near(sums))
 
 
 def whole(count):
     return [pl.BlockSpec(memory_space=pltpu.VMEM)] * count
 
 
-def call(kernel, name, outs, inputs, scratch=()):
-    shapes = [jax.ShapeDtypeStruct(shape, jnp.float32) for shape in outs]
+def near(value):
+    return pltpu.with_memory_space_constraint(value, pltpu.VMEM)
+
+
+def call(kernel, name, outs, inputs, scratch=(), near_ins=(), near_outs=()):
+    inputs = [
+        near(value) if i in near_ins else value for i, value in enumerate(inputs)
+    ]
+    shapes = [
+        pltpu.VMEM(shape, jnp.float32) if i in near_outs else jax.ShapeDtypeStruct(shape, jnp.float32)
+        for i, shape in enumerate(outs)
+    ]
     return pl.pallas_call(
         kernel,
         out_shape=shapes if len(shapes) > 1 else shapes[0],
@@ -483,32 +566,31 @@
     early, sums, rim = call(
         early_kernel,
         "early",
-        [(devices, 2 * materials * QUAD, LANES), plane, (16, rows_y)],
+        [(devices, 2 * materials * QUAD, LANES), plane, (32, rows_y)],
         (frac, density, energy, node_shift, node_speed),
-    )
-    early = exchange(early)
+        near_outs=(0, 1, 2),
+    )
+    early = near(exchange(early))
     above = shifted(rim, "zx", -1)
     below = above if lax.axis_size("zx") == 2 else shifted(rim, "zx", 1)
-    tall = (rows_x + SUB, LANES)
-    extended, first, last = call(
-        rows_kernel,
-        "rows",
-        [(6, rows_x + SUB, rows_y), tall, tall],
-        (node_shift, node_speed, sums, above, below),
-    )
+    columns = call(columns_kernel, "columns", [(32, LANES)], (node_shift, node_speed, sums), near_ins=(2,), near_outs=(0,))
+    first, last = call(corners_kernel, "corners", [(16, LANES)] * 2, (columns, above, below), near_ins=(0, 1, 2), near_outs=(0, 1))
     right = shifted(first, "zy", -1)
     left = shifted(last, "zy", 1)
     tables = call(
         table_kernel,
         "tables",
         [(SUB, LANES)],
-        (dest_tile[0, 0], src_block[0], dest_block[0], crossing[0], keep[0]),
+        (dest_tile.reshape(1, -1), src_block[0], dest_block[0], crossing[0], keep[0]),
+        near_outs=(0,),
     )
     speed_after, shift_after, late = call(
         lagrange_kernel,
         "lagrange",
         [plane, plane, (devices, (materials + 2) * QUAD + SUB, LANES)],
-        (extended, right, left, frac, density, energy, tables),
+        (node_shift, node_speed, sums, above, below, right, left, frac, density, energy, tables),
+        near_ins=(2, 3, 4, 5, 6, 7, 8, 9, 10),
+        near_outs=(2,),
     )
     early, late = lax.optimization_barrier((early, late))
     late = exchange(late)
@@ -522,9 +604,11 @@
         + [(SUB, groups, rows, LANES)] * 2
         + [(devices, groups, SUB, LANES)]
         + [(groups, groups, SUB, LANES)] * 2,
+        near_ins=(1,),
+        near_outs=(0,),
     )
     totals = exchange(totals)
-    remapped = call(unpack_kernel, "unpack", [(fields, rows_x, rows_y)], (totals,))
+    remapped = unpack(totals, (fields, rows_x, rows_y))
     return (remapped.reshape(3, materials, rows_x, rows_y), speed_after, shift_after)
 
 

time: 120 us -> 114 us (0.950)
  Pallas kernels: 21.6 us -> 16.2 us
  waiting for transfers between devices: 11.4 us -> 14.6 us
  blocking collectives: 69.8 us -> 67.6 us
    pallas_call x6, Pallas kernels: 21.6 us -> 14.9 us  [call(): pl.pallas_call(kernel, out_shape=shapes if len(shapes) > 1 else shapes[0]...]
    ppermute x3, waiting for transfers between devices: 11.4 us -> 13.7 us  [shifted(): lax.ppermute(value, axis, [(i, (i + by) % peers) for i in range(peers)])]
    all_to_all x2, blocking collectives: 69.8 us -> 67.6 us  [exchange(): return lax.all_to_all(value, ('zx', 'zy'), 0, 0, tiled=True)]
    pallas_call x0 -> x1, Pallas kernels: none -> 1.34 us  [unpack(): pl.pallas_call(unpack_kernel, out_shape=jax.ShapeDtypeStruct(shape, jnp.f...]
  transfers between devices with their start and end apart: 4 -> 4, of which waited for: 3 -> 4; matrix products, arithmetic and copies ran while one was open for 1% -> 0% of each run, Pallas kernels for 6% -> 5%
where the time goes in v4:
time: 114 us
  blocking collectives  67.6 us (59%)
  Pallas kernels  16.2 us (14%)
  waiting for transfers between devices  14.6 us (13%)
  starting transfers between devices  13.8 us (12%)
    all_to_all x2, blocking collectives, exchange(): return lax.all_to_all(value, ('zx', 'zy'), 0, 0, tiled=True)  67.6 us
    pallas_call x6, Pallas kernels, call(): pl.pallas_call(kernel, out_shape=shapes if len(shapes) > 1 else shapes[0]...  14.9 us
    ppermute x3, waiting for transfers between devices, shifted(): lax.ppermute(value, axis, [(i, (i + by) % peers) for i in range(peers)])  13.7 us
    all_to_all x1, starting transfers between devices, exchange(): return lax.all_to_all(value, ('zx', 'zy'), 0, 0, tiled=True)  7.43 us
    ppermute x3, starting transfers between devices, shifted(): lax.ppermute(value, axis, [(i, (i + by) % peers) for i in range(peers)])  6.33 us
  transfers between devices with their start and end apart: 4, of which 4 were waited for; matrix products, arithmetic and copies ran while one was open for 0% of the time, Pallas kernels for 5%

profile of v4, /device:TPU:0, one launch (start us, length us, event | category | flops | bytes accessed | tf_op | source)
XLA Modules:
  0.0 113.8 jit_solution(2412129434566741203)
XLA Ops:
  0.6 2.8 %early.1 = (f32[32,64,128]{2,1,0:T(8,128)}, f32[2,64,256]{2,1,0:T(8,128)S(1)}, f32[32,256]{1,0:T(8,128)S(1)}) custom-call(f32[8,64,256]{2,1,0:T(8,128)} %frac_ref.3, f32[8,64,256]{2,1,0:T(8,128)} %density_ref.3, f32[8,64,256]{2,1,0:T(8,128)} %energy_ref.3, f32[2,64,256]{2,1,0:T(8,128)} %now_shift_ref.1, f32[2,64,256]{2,1,0:T(8,128)} %now_speed_ref.1), custom_call_target="tpu_custom_call" | custom-call | tf_op jit(solution)/shard_map/early/pallas_call | solution.py:534
  3.4 0.0 copy-start
  3.4 0.0 copy-start.1
  3.4 0.0 copy-start.2
  3.4 7.4 %all-to-all-start = ((f32[32,64,128]{2,1,0:T(8,128)}), f32[32,64,128]{2,1,0:T(8,128)}, u32[]{:S(2)}, u32[]{:S(2)}) async-start(f32[32,64,128]{2,1,0:T(8,128)} %get-tuple-element.13), calls=%async_computation | async-start | bytes 2097152 | tf_op jit(solution)/shard_map/all_to_all | solution.py:545
  10.8 1.8 %collective-permute-start = (f32[32,256]{1,0:T(8,128)S(1)}, f32[32,256]{1,0:T(8,128)S(1)}, u32[]{:S(2)}, u32[]{:S(2)}) collective-permute-start(f32[32,256]{1,0:T(8,128)S(1)} %get-tuple-element.15), channel_id=1, source_target_pairs={{0,16},{16,0},{1,17},{17,1},{2,18},{18,2},{3,19},{19,3},{4,20},{20... | collective-permute-start | bytes 98312 | tf_op jit(solution)/shard_map/ppermute | solution.py:15
  12.6 1.2 %columns.1.columns_ref = f32[32,128]{1,0:T(8,128)S(1)} custom-call(f32[2,64,256]{2,1,0:T(8,128)} %now_shift_ref.1, f32[2,64,256]{2,1,0:T(8,128)} %now_speed_ref.1, f32[2,64,256]{2,1,0:T(8,128)S(1)} %get-tuple-element.14.sums_ref), custom_call_target="tpu_custom_call" | custom-call | tf_op jit(solution)/shard_map/columns/pallas_call | solution.py:534
  13.8 6.0 %collective-permute-done.above_ref.below_ref = f32[32,256]{1,0:T(8,128)S(1)} collective-permute-done((f32[32,256]{1,0:T(8,128)S(1)}, f32[32,256]{1,0:T(8,128)S(1)}, u32[]{:S(2)}, u32[]{:S(2)}) %collective-permute-start) | collective-permute-done | bytes 32800 | tf_op jit(solution)/shard_map/ppermute | solution.py:15
  19.7 0.1 corners.1
  19.8 4.6 %collective-permute-start.1 = (f32[16,128]{1,0:T(8,128)S(1)}, f32[16,128]{1,0:T(8,128)S(1)}, u32[]{:S(2)}, u32[]{:S(2)}) collective-permute-start(f32[16,128]{1,0:T(8,128)S(1)} %get-tuple-element.16), channel_id=1, source_target_pairs={{0,15},{1,0},{2,1},{3,2},{4,3},{5,4},{6,5},{7,6},{8,7},{9,8},{10,9... | collective-permute-start | bytes 24584 | tf_op jit(solution)/shard_map/ppermute | solution.py:15
  24.4 0.0 collective-permute-start.2
  24.4 1.0 tables.1.tables_ref
  25.4 3.2 %collective-permute-done.1.right_ref = f32[16,128]{1,0:T(8,128)S(1)} collective-permute-done((f32[16,128]{1,0:T(8,128)S(1)}, f32[16,128]{1,0:T(8,128)S(1)}, u32[]{:S(2)}, u32[]{:S(2)}) %collective-permute-start.1) | collective-permute-done | bytes 8224 | tf_op jit(solution)/shard_map/ppermute | solution.py:15
  28.6 4.5 %collective-permute-done.2.left_ref = f32[16,128]{1,0:T(8,128)S(1)} collective-permute-done((f32[16,128]{1,0:T(8,128)S(1)}, f32[16,128]{1,0:T(8,128)S(1)}, u32[]{:S(2)}, u32[]{:S(2)}) %collective-permute-start.2) | collective-permute-done | bytes 8224 | tf_op jit(solution)/shard_map/ppermute | solution.py:15
  33.1 0.0 copy-done
  33.1 0.0 copy-done.1
  33.1 0.0 copy-done.2
  33.1 3.0 %lagrange.1 = (f32[2,64,256]{2,1,0:T(8,128)}, f32[2,64,256]{2,1,0:T(8,128)}, f32[32,48,128]{2,1,0:T(8,128)S(1)}) custom-call(f32[2,64,256]{2,1,0:T(8,128)} %now_shift_ref.1, f32[2,64,256]{2,1,0:T(8,128)} %now_speed_ref.1, f32[2,64,256]{2,1,0:T(8,128)S(1)} %get-tuple-element.14.sums_ref, f32[32,256]{1,0:T(8,128)S(1)} %collective-permute-done.above_ref.below_ref, ...), custom_call_target="tpu_custom_call" | custom-call | tf_op jit(solution)/shard_map/lagrange/pallas_call | solution.py:534
  36.1 0.0 copy-start.3
  36.1 0.9 copy-done.3
  37.0 0.9 all-to-all-done.early_ref
  38.0 27.2 %all_to_all.15.late_ref = f32[32,48,128]{2,1,0:T(8,128)S(1)} all-to-all(f32[32,48,128]{2,1,0:T(8,128)} %copy-done.3), channel_id=1, replica_groups=mesh['zx'=2,'zy'=16] {'zx','zy'}, dimensions={0} | all-to-all | bytes 1572864 | tf_op jit(solution)/shard_map/all_to_all | solution.py:545
  65.2 6.9 %crossings.1 = f32[32,96,128]{2,1,0:T(8,128)S(1)} custom-call(f32[32,64,128]{2,1,0:T(8,128)} %all-to-all-done.early_ref, f32[32,48,128]{2,1,0:T(8,128)S(1)} %all_to_all.15.late_ref), custom_call_target="tpu_custom_call" | custom-call | tf_op jit(solution)/shard_map/crossings/pallas_call | solution.py:534
  72.1 40.4 %all_to_all.16.sums_ref = f32[32,96,128]{2,1,0:T(8,128)S(1)} all-to-all(f32[32,96,128]{2,1,0:T(8,128)S(1)} %crossings.1), channel_id=1, replica_groups=mesh['zx'=2,'zy'=16] {'zx','zy'}, dimensions={0} | all-to-all | bytes 3145728 | tf_op jit(solution)/shard_map/all_to_all | solution.py:545
  112.4 1.3 %unpack.1 = f32[24,64,256]{2,1,0:T(8,128)} custom-call(f32[32,96,128]{2,1,0:T(8,128)S(1)} %all_to_all.16.sums_ref), custom_call_target="tpu_custom_call" | custom-call | tf_op jit(solution)/shard_map/unpack/pallas_call | solution.py:508
Async XLA Ops:
  3.4 29.7 %copy-start = (f32[8,64,256]{2,1,0:T(8,128)S(1)}, f32[8,64,256]{2,1,0:T(8,128)}, u32[]{:S(2)}) copy-start(f32[8,64,256]{2,1,0:T(8,128)} %frac_ref.3) | copy-start | bytes 1572868
  3.4 29.7 %copy-start.1 = (f32[8,64,256]{2,1,0:T(8,128)S(1)}, f32[8,64,256]{2,1,0:T(8,128)}, u32[]{:S(2)}) copy-start(f32[8,64,256]{2,1,0:T(8,128)} %density_ref.3) | copy-start | bytes 1572868
  3.4 29.7 %copy-start.2 = (f32[8,64,256]{2,1,0:T(8,128)S(1)}, f32[8,64,256]{2,1,0:T(8,128)}, u32[]{:S(2)}) copy-start(f32[8,64,256]{2,1,0:T(8,128)} %energy_ref.3) | copy-start | bytes 1572868
  3.4 34.6 %all-to-all-start = ((f32[32,64,128]{2,1,0:T(8,128)}), f32[32,64,128]{2,1,0:T(8,128)}, u32[]{:S(2)}, u32[]{:S(2)}) async-start(f32[32,64,128]{2,1,0:T(8,128)} %get-tuple-element.13), calls=%async_computation | async-start | bytes 2097152 | tf_op jit(solution)/shard_map/all_to_all | solution.py:545
  10.8 8.9 %collective-permute-start = (f32[32,256]{1,0:T(8,128)S(1)}, f32[32,256]{1,0:T(8,128)S(1)}, u32[]{:S(2)}, u32[]{:S(2)}) collective-permute-start(f32[32,256]{1,0:T(8,128)S(1)} %get-tuple-element.15), channel_id=1, source_target_pairs={{0,16},{16,0},{1,17},{17,1},{2,18},{18,2},{3,19},{19,3},{4,20},{20... | collective-permute-start | bytes 98312 | tf_op jit(solution)/shard_map/ppermute | solution.py:15
  19.8 8.8 %collective-permute-start.1 = (f32[16,128]{1,0:T(8,128)S(1)}, f32[16,128]{1,0:T(8,128)S(1)}, u32[]{:S(2)}, u32[]{:S(2)}) collective-permute-start(f32[16,128]{1,0:T(8,128)S(1)} %get-tuple-element.16), channel_id=1, source_target_pairs={{0,15},{1,0},{2,1},{3,2},{4,3},{5,4},{6,5},{7,6},{8,7},{9,8},{10,9... | collective-permute-start | bytes 24584 | tf_op jit(solution)/shard_map/ppermute | solution.py:15
  24.4 8.8 %collective-permute-start.2 = (f32[16,128]{1,0:T(8,128)S(1)}, f32[16,128]{1,0:T(8,128)S(1)}, u32[]{:S(2)}, u32[]{:S(2)}) collective-permute-start(f32[16,128]{1,0:T(8,128)S(1)} %get-tuple-element.17), channel_id=1, source_target_pairs={{0,1},{1,2},{2,3},{3,4},{4,5},{5,6},{6,7},{7,8},{8,9},{9,10},{10,1... | collective-permute-start | bytes 24584 | tf_op jit(solution)/shard_map/ppermute | solution.py:15
  36.1 0.9 copy-start.3

commit v5 on v4

--- a/solution.py
+++ b/solution.py
@@ -364,7 +364,16 @@
 
 
 def crossing_kernel(
-    early_ref, late_ref, out_ref, state_ref, even_ref, odd_ref, places_ref, sources_ref, weights_ref
+    early_hbm,
+    late_ref,
+    out_ref,
+    state_ref,
+    even_ref,
+    odd_ref,
+    places_ref,
+    sources_ref,
+    weights_ref,
+    sems,
 ):
     devices, rows = state_ref.shape[0], state_ref.shape[1]
     table_row = late_ref.shape[1] - SUB
@@ -372,6 +381,12 @@
     groups = devices // SUB
     capacity = LANES // SUB
     slots_ref = (even_ref, odd_ref)
+    copies = []
+    for i in range(WORKER_PARTS):
+        part = pl.ds(devices // WORKER_PARTS * i, devices // WORKER_PARTS)
+        target = state_ref.at[part, pl.ds(0, early_hbm.shape[1])]
+        copies.append(pltpu.make_async_copy(early_hbm.at[part], target, sems.at[i]))
+        copies[-1].start()
     spread = (SUB, LANES)
     lane = lax.broadcasted_iota(jnp.int32, spread, 1)
     source_of = lax.broadcasted_iota(jnp.int32, spread, 0)
@@ -391,21 +406,6 @@
             ]
         return values
 
-    low = lower_half(spread)
-    third = rows // 3
-
-    def conserve(source, carry):
-        areas = late_ref[source, third : third + SUB]
-        swapped = pltpu.roll(areas, QUAD, 0)
-        area, after = jnp.where(low, areas, swapped), jnp.where(low, swapped, areas)
-        for tile in range(tiles // 3):
-            at = [slice(SUB * tile + third * g, SUB * tile + third * g + SUB) for g in range(3)]
-            state_ref[source, at[0]] = early_ref[source, at[0]] * after
-            state_ref[source, at[1]] = early_ref[source, at[1]] * area
-            state_ref[source, at[2]] = late_ref[source, at[0]]
-        return carry
-
-    lax.fori_loop(0, devices, conserve, 0, unroll=4)
     for a in range(groups):
         table = [late_ref[a * SUB : a * SUB + SUB, table_row + i, :] for i in range(7)]
         starts = table[6].astype(jnp.int32)
@@ -422,6 +422,24 @@
             places = [jnp.broadcast_to(place[i : i + 1], spread) for i in range(SUB)]
             for delta, value in enumerate(regroup(places)):
                 places_ref[SUB * octet + delta, a] = value
+
+    low = lower_half(spread)
+    third = rows // 3
+
+    def conserve(source, carry):
+        areas = late_ref[source, third : third + SUB]
+        swapped = pltpu.roll(areas, QUAD, 0)
+        area, after = jnp.where(low, areas, swapped), jnp.where(low, swapped, areas)
+        for tile in range(tiles // 3):
+            at = [slice(SUB * tile + third * g, SUB * tile + third * g + SUB) for g in range(3)]
+            state_ref[source, at[0]] = state_ref[source, at[0]] * after
+            state_ref[source, at[1]] = state_ref[source, at[1]] * area
+            state_ref[source, at[2]] = late_ref[source, at[0]]
+        return carry
+
+    for copy in copies:
+        copy.wait()
+    lax.fori_loop(0, devices, conserve, 0, unroll=4)
 
     def gather(octet, a):
         sources, weights = sources_ref[octet, a].astype(jnp.int32), weights_ref[octet, a]
@@ -476,6 +494,7 @@
         lax.fori_loop(0, groups, step, 0, unroll=True)
 
 
+WORKER_PARTS = 4
 UNPACK_PARTS = 4
 
 
@@ -523,7 +542,7 @@
     return pltpu.with_memory_space_constraint(value, pltpu.VMEM)
 
 
-def call(kernel, name, outs, inputs, scratch=(), near_ins=(), near_outs=()):
+def call(kernel, name, outs, inputs, scratch=(), near_ins=(), near_outs=(), far_ins=(), sems=()):
     inputs = [
         near(value) if i in near_ins else value for i, value in enumerate(inputs)
     ]
@@ -534,9 +553,13 @@
     return pl.pallas_call(
         kernel,
         out_shape=shapes if len(shapes) > 1 else shapes[0],
-        in_specs=whole(len(inputs)),
+        in_specs=[
+            pl.BlockSpec(memory_space=pl.ANY if i in far_ins else pltpu.VMEM)
+            for i in range(len(inputs))
+        ],
         out_specs=whole(len(shapes)) if len(shapes) > 1 else whole(1)[0],
-        scratch_shapes=[pltpu.VMEM(shape, jnp.float32) for shape in scratch],
+        scratch_shapes=[pltpu.VMEM(shape, jnp.float32) for shape in scratch]
+        + [pltpu.SemaphoreType.DMA((count,)) for count in sems],
         name=name,
     )(*inputs)
 
@@ -570,7 +593,7 @@
         (frac, density, energy, node_shift, node_speed),
         near_outs=(0, 1, 2),
     )
-    early = near(exchange(early))
+    early = exchange(early)
     above = shifted(rim, "zx", -1)
     below = above if lax.axis_size("zx") == 2 else shifted(rim, "zx", 1)
     columns = call(columns_kernel, "columns", [(32, LANES)], (node_shift, node_speed, sums), near_ins=(2,), near_outs=(0,))
@@ -606,6 +629,8 @@
         + [(groups, groups, SUB, LANES)] * 2,
         near_ins=(1,),
         near_outs=(0,),
+        far_ins=(0,),
+        sems=(WORKER_PARTS,),
     )
     totals = exchange(totals)
     remapped = unpack(totals, (fields, rows_x, rows_y))

time: 114 us -> 112 us (0.982)
  blocking collectives: 67.6 us -> 66.4 us
    all_to_all x2, blocking collectives: 67.6 us -> 66.4 us  [exchange(): return lax.all_to_all(value, ('zx', 'zy'), 0, 0, tiled=True)]
where the time goes in v5:
time: 112 us
  blocking collectives  66.4 us (59%)
  Pallas kernels  15.6 us (14%)
  waiting for transfers between devices  15.5 us (14%)
  starting transfers between devices  13.8 us (12%)
    all_to_all x2, blocking collectives, exchange(): return lax.all_to_all(value, ('zx', 'zy'), 0, 0, tiled=True)  66.4 us
    pallas_call x6, Pallas kernels, call(): pl.pallas_call(kernel, out_shape=shapes if len(shapes) > 1 else shapes[0]...  14.3 us
    ppermute x3, waiting for transfers between devices, shifted(): lax.ppermute(value, axis, [(i, (i + by) % peers) for i in range(peers)])  13.7 us
    all_to_all x1, starting transfers between devices, exchange(): return lax.all_to_all(value, ('zx', 'zy'), 0, 0, tiled=True)  7.43 us
    ppermute x3, starting transfers between devices, shifted(): lax.ppermute(value, axis, [(i, (i + by) % peers) for i in range(peers)])  6.33 us
  transfers between devices with their start and end apart: 4, of which 4 were waited for; matrix products, arithmetic and copies ran while one was open for 0% of the time, Pallas kernels for 5%

profile of v5, /device:TPU:0, one launch (start us, length us, event | category | flops | bytes accessed | tf_op | source)
XLA Modules:
  0.0 112.0 jit_solution(10402213707788844430)
XLA Ops:
  0.6 2.8 %early.1 = (f32[32,64,128]{2,1,0:T(8,128)}, f32[2,64,256]{2,1,0:T(8,128)S(1)}, f32[32,256]{1,0:T(8,128)S(1)}) custom-call(f32[8,64,256]{2,1,0:T(8,128)} %frac_ref.3, f32[8,64,256]{2,1,0:T(8,128)} %density_ref.3, f32[8,64,256]{2,1,0:T(8,128)} %energy_ref.3, f32[2,64,256]{2,1,0:T(8,128)} %now_shift_ref.1, f32[2,64,256]{2,1,0:T(8,128)} %now_speed_ref.1), custom_call_target="tpu_custom_call" | custom-call | tf_op jit(solution)/shard_map/early/pallas_call | solution.py:553
  3.4 0.0 copy-start
  3.4 0.0 copy-start.1
  3.4 0.0 copy-start.2
  3.4 7.4 %all-to-all-start = ((f32[32,64,128]{2,1,0:T(8,128)}), f32[32,64,128]{2,1,0:T(8,128)}, u32[]{:S(2)}, u32[]{:S(2)}) async-start(f32[32,64,128]{2,1,0:T(8,128)} %get-tuple-element.13), calls=%async_computation | async-start | bytes 2097152 | tf_op jit(solution)/shard_map/all_to_all | solution.py:568
  10.8 1.8 %collective-permute-start = (f32[32,256]{1,0:T(8,128)S(1)}, f32[32,256]{1,0:T(8,128)S(1)}, u32[]{:S(2)}, u32[]{:S(2)}) collective-permute-start(f32[32,256]{1,0:T(8,128)S(1)} %get-tuple-element.15), channel_id=1, source_target_pairs={{0,16},{16,0},{1,17},{17,1},{2,18},{18,2},{3,19},{19,3},{4,20},{20... | collective-permute-start | bytes 98312 | tf_op jit(solution)/shard_map/ppermute | solution.py:15
  12.6 1.2 %columns.1.columns_ref = f32[32,128]{1,0:T(8,128)S(1)} custom-call(f32[2,64,256]{2,1,0:T(8,128)} %now_shift_ref.1, f32[2,64,256]{2,1,0:T(8,128)} %now_speed_ref.1, f32[2,64,256]{2,1,0:T(8,128)S(1)} %get-tuple-element.14.sums_ref), custom_call_target="tpu_custom_call" | custom-call | tf_op jit(solution)/shard_map/columns/pallas_call | solution.py:553
  13.8 6.0 %collective-permute-done.above_ref.below_ref = f32[32,256]{1,0:T(8,128)S(1)} collective-permute-done((f32[32,256]{1,0:T(8,128)S(1)}, f32[32,256]{1,0:T(8,128)S(1)}, u32[]{:S(2)}, u32[]{:S(2)}) %collective-permute-start) | collective-permute-done | bytes 32800 | tf_op jit(solution)/shard_map/ppermute | solution.py:15
  19.7 0.1 corners.1
  19.8 4.6 %collective-permute-start.1 = (f32[16,128]{1,0:T(8,128)S(1)}, f32[16,128]{1,0:T(8,128)S(1)}, u32[]{:S(2)}, u32[]{:S(2)}) collective-permute-start(f32[16,128]{1,0:T(8,128)S(1)} %get-tuple-element.16), channel_id=1, source_target_pairs={{0,15},{1,0},{2,1},{3,2},{4,3},{5,4},{6,5},{7,6},{8,7},{9,8},{10,9... | collective-permute-start | bytes 24584 | tf_op jit(solution)/shard_map/ppermute | solution.py:15
  24.4 0.0 collective-permute-start.2
  24.4 1.0 tables.1.tables_ref
  25.4 3.2 %collective-permute-done.1.right_ref = f32[16,128]{1,0:T(8,128)S(1)} collective-permute-done((f32[16,128]{1,0:T(8,128)S(1)}, f32[16,128]{1,0:T(8,128)S(1)}, u32[]{:S(2)}, u32[]{:S(2)}) %collective-permute-start.1) | collective-permute-done | bytes 8224 | tf_op jit(solution)/shard_map/ppermute | solution.py:15
  28.6 4.5 %collective-permute-done.2.left_ref = f32[16,128]{1,0:T(8,128)S(1)} collective-permute-done((f32[16,128]{1,0:T(8,128)S(1)}, f32[16,128]{1,0:T(8,128)S(1)}, u32[]{:S(2)}, u32[]{:S(2)}) %collective-permute-start.2) | collective-permute-done | bytes 8224 | tf_op jit(solution)/shard_map/ppermute | solution.py:15
  33.1 0.0 copy-done
  33.1 0.0 copy-done.1
  33.1 0.0 copy-done.2
  33.1 3.0 %lagrange.1 = (f32[2,64,256]{2,1,0:T(8,128)}, f32[2,64,256]{2,1,0:T(8,128)}, f32[32,48,128]{2,1,0:T(8,128)S(1)}) custom-call(f32[2,64,256]{2,1,0:T(8,128)} %now_shift_ref.1, f32[2,64,256]{2,1,0:T(8,128)} %now_speed_ref.1, f32[2,64,256]{2,1,0:T(8,128)S(1)} %get-tuple-element.14.sums_ref, f32[32,256]{1,0:T(8,128)S(1)} %collective-permute-done.above_ref.below_ref, ...), custom_call_target="tpu_custom_call" | custom-call | tf_op jit(solution)/shard_map/lagrange/pallas_call | solution.py:553
  36.1 1.9 %all-to-all-done.early_hbm = f32[32,64,128]{2,1,0:T(8,128)} async-done(((f32[32,64,128]{2,1,0:T(8,128)}), f32[32,64,128]{2,1,0:T(8,128)}, u32[]{:S(2)}, u32[]{:S(2)}) %all-to-all-start) | async-done | bytes 1048608 | tf_op jit(solution)/shard_map/all_to_all | solution.py:568
  38.0 26.1 %all_to_all.15.late_ref = f32[32,48,128]{2,1,0:T(8,128)S(1)} all-to-all(f32[32,48,128]{2,1,0:T(8,128)S(1)} %get-tuple-element.20), channel_id=1, replica_groups=mesh['zx'=2,'zy'=16] {'zx','zy'}, dimensions={0} | all-to-all | bytes 1572864 | tf_op jit(solution)/shard_map/all_to_all | solution.py:568
  64.0 6.2 %crossings.1 = f32[32,96,128]{2,1,0:T(8,128)S(1)} custom-call(f32[32,64,128]{2,1,0:T(8,128)} %all-to-all-done.early_hbm, f32[32,48,128]{2,1,0:T(8,128)S(1)} %all_to_all.15.late_ref), custom_call_target="tpu_custom_call" | custom-call | tf_op jit(solution)/shard_map/crossings/pallas_call | solution.py:553
  70.3 40.4 %all_to_all.16.sums_ref = f32[32,96,128]{2,1,0:T(8,128)S(1)} all-to-all(f32[32,96,128]{2,1,0:T(8,128)S(1)} %crossings.1), channel_id=1, replica_groups=mesh['zx'=2,'zy'=16] {'zx','zy'}, dimensions={0} | all-to-all | bytes 3145728 | tf_op jit(solution)/shard_map/all_to_all | solution.py:568
  110.7 1.3 %unpack.1 = f32[24,64,256]{2,1,0:T(8,128)} custom-call(f32[32,96,128]{2,1,0:T(8,128)S(1)} %all_to_all.16.sums_ref), custom_call_target="tpu_custom_call" | custom-call | tf_op jit(solution)/shard_map/unpack/pallas_call | solution.py:527
Async XLA Ops:
  3.4 29.7 %copy-start = (f32[8,64,256]{2,1,0:T(8,128)S(1)}, f32[8,64,256]{2,1,0:T(8,128)}, u32[]{:S(2)}) copy-start(f32[8,64,256]{2,1,0:T(8,128)} %frac_ref.3) | copy-start | bytes 1572868
  3.4 29.7 %copy-start.1 = (f32[8,64,256]{2,1,0:T(8,128)S(1)}, f32[8,64,256]{2,1,0:T(8,128)}, u32[]{:S(2)}) copy-start(f32[8,64,256]{2,1,0:T(8,128)} %density_ref.3) | copy-start | bytes 1572868
  3.4 29.7 %copy-start.2 = (f32[8,64,256]{2,1,0:T(8,128)S(1)}, f32[8,64,256]{2,1,0:T(8,128)}, u32[]{:S(2)}) copy-start(f32[8,64,256]{2,1,0:T(8,128)} %energy_ref.3) | copy-start | bytes 1572868
  3.4 34.6 %all-to-all-start = ((f32[32,64,128]{2,1,0:T(8,128)}), f32[32,64,128]{2,1,0:T(8,128)}, u32[]{:S(2)}, u32[]{:S(2)}) async-start(f32[32,64,128]{2,1,0:T(8,128)} %get-tuple-element.13), calls=%async_computation | async-start | bytes 2097152 | tf_op jit(solution)/shard_map/all_to_all | solution.py:568
  10.8 8.9 %collective-permute-start = (f32[32,256]{1,0:T(8,128)S(1)}, f32[32,256]{1,0:T(8,128)S(1)}, u32[]{:S(2)}, u32[]{:S(2)}) collective-permute-start(f32[32,256]{1,0:T(8,128)S(1)} %get-tuple-element.15), channel_id=1, source_target_pairs={{0,16},{16,0},{1,17},{17,1},{2,18},{18,2},{3,19},{19,3},{4,20},{20... | collective-permute-start | bytes 98312 | tf_op jit(solution)/shard_map/ppermute | solution.py:15
  19.8 8.8 %collective-permute-start.1 = (f32[16,128]{1,0:T(8,128)S(1)}, f32[16,128]{1,0:T(8,128)S(1)}, u32[]{:S(2)}, u32[]{:S(2)}) collective-permute-start(f32[16,128]{1,0:T(8,128)S(1)} %get-tuple-element.16), channel_id=1, source_target_pairs={{0,15},{1,0},{2,1},{3,2},{4,3},{5,4},{6,5},{7,6},{8,7},{9,8},{10,9... | collective-permute-start | bytes 24584 | tf_op jit(solution)/shard_map/ppermute | solution.py:15
  24.4 8.8 %collective-permute-start.2 = (f32[16,128]{1,0:T(8,128)S(1)}, f32[16,128]{1,0:T(8,128)S(1)}, u32[]{:S(2)}, u32[]{:S(2)}) collective-permute-start(f32[16,128]{1,0:T(8,128)S(1)} %get-tuple-element.17), channel_id=1, source_target_pairs={{0,1},{1,2},{2,3},{3,4},{4,5},{5,6},{6,7},{7,8},{8,9},{9,10},{10,1... | collective-permute-start | bytes 24584 | tf_op jit(solution)/shard_map/ppermute | solution.py:15

commit v6 on v4

--- a/solution.py
+++ b/solution.py
@@ -183,19 +183,15 @@
     return [float(gamma) for gamma in gammas - np.float32(1.0)]
 
 
-def early_kernel(
-    frac_ref, density_ref, energy_ref, shift_ref, speed_ref, out_ref, sums_ref, rim_ref
-):
+def sums_kernel(frac_ref, density_ref, energy_ref, shift_ref, speed_ref, sums_ref, rim_ref):
     materials = frac_ref.shape[0]
     stiff = stiffness(materials)
     mass = pressure = None
-    held = []
     for material in range(materials):
         part = frac_ref[material] * density_ref[material]
         force = part * energy_ref[material] * stiff[material]
         mass = part if mass is None else mass + part
         pressure = force if pressure is None else pressure + force
-        held.append(part)
     sums_ref[0], sums_ref[1] = mass, pressure
     last = mass.shape[0] - 1
     for field in range(2):
@@ -207,7 +203,6 @@
     for field, value in enumerate((mass, pressure)):
         rim_ref[8 + field : 9 + field, :] = value[0:1]
         rim_ref[24 + field : 25 + field, :] = value[last : last + 1]
-    store_pairs([frac_ref[material] for material in range(materials)] + held, out_ref, 0)
 
 
 def columns_kernel(shift_ref, speed_ref, sums_ref, out_ref):
@@ -353,21 +348,24 @@
     area, after, viscous = own(area), own(after), own(viscous)
     change = after - area
     materials = frac_ref.shape[0]
-    values = []
+    volumes, masses, energies = [], [], []
     for material, stiff in enumerate(stiffness(materials)):
         frac, density, energy = frac_ref[material], density_ref[material], energy_ref[material]
         force = stiff * density * energy + viscous
-        values.append(frac * density * area * energy - frac * force * change)
-    store_pairs(values + [area, after], out_ref, 0)
+        volumes.append(frac * after)
+        masses.append(frac * density * area)
+        energies.append(masses[-1] * energy - frac * force * change)
+    for third, values in enumerate((volumes, masses, energies)):
+        store_pairs(values, out_ref, third * materials * QUAD)
+    rows = 3 * materials * QUAD
     for piece in range(out_ref.shape[0]):
-        out_ref[piece, (materials + 2) * QUAD : (materials + 2) * QUAD + SUB] = tables_ref[...]
+        out_ref[piece, rows : rows + SUB] = tables_ref[...]
 
 
 def crossing_kernel(
-    early_ref, late_ref, out_ref, state_ref, even_ref, odd_ref, places_ref, sources_ref, weights_ref
+    state_ref, out_ref, even_ref, odd_ref, places_ref, sources_ref, weights_ref
 ):
-    devices, rows = state_ref.shape[0], state_ref.shape[1]
-    table_row = late_ref.shape[1] - SUB
+    devices, rows = out_ref.shape[0], out_ref.shape[1]
     tiles = rows // SUB
     groups = devices // SUB
     capacity = LANES // SUB
@@ -391,23 +389,8 @@
             ]
         return values
 
-    low = lower_half(spread)
-    third = rows // 3
-
-    def conserve(source, carry):
-        areas = late_ref[source, third : third + SUB]
-        swapped = pltpu.roll(areas, QUAD, 0)
-        area, after = jnp.where(low, areas, swapped), jnp.where(low, swapped, areas)
-        for tile in range(tiles // 3):
-            at = [slice(SUB * tile + third * g, SUB * tile + third * g + SUB) for g in range(3)]
-            state_ref[source, at[0]] = early_ref[source, at[0]] * after
-            state_ref[source, at[1]] = early_ref[source, at[1]] * area
-            state_ref[source, at[2]] = late_ref[source, at[0]]
-        return carry
-
-    lax.fori_loop(0, devices, conserve, 0, unroll=4)
     for a in range(groups):
-        table = [late_ref[a * SUB : a * SUB + SUB, table_row + i, :] for i in range(7)]
+        table = [state_ref[a * SUB : a * SUB + SUB, rows + i, :] for i in range(7)]
         starts = table[6].astype(jnp.int32)
         for octet in range(groups):
             target = SUB * octet + (piece ^ source_of)
@@ -459,7 +442,7 @@
             (((1,), (1,)), ((), ())),
             preferred_element_type=jnp.float32,
         )
-        keep = jnp.broadcast_to(late_ref[target, table_row + 7 : table_row + 8], (rows, LANES))
+        keep = jnp.broadcast_to(state_ref[target, rows + 7 : rows + 8], (rows, LANES))
         stay = keep * state_ref[target, 0:rows]
         out_ref[target] = stay + total[0:rows] + total[rows : 2 * rows] + total[2 * rows : 3 * rows]
 
@@ -563,14 +546,13 @@
     fields = 3 * materials
     rows = fields * QUAD
     plane = (2, rows_x, rows_y)
-    early, sums, rim = call(
-        early_kernel,
-        "early",
-        [(devices, 2 * materials * QUAD, LANES), plane, (32, rows_y)],
+    sums, rim = call(
+        sums_kernel,
+        "sums",
+        [plane, (32, rows_y)],
         (frac, density, energy, node_shift, node_speed),
-        near_outs=(0, 1, 2),
-    )
-    early = near(exchange(early))
+        near_outs=(0, 1),
+    )
     above = shifted(rim, "zx", -1)
     below = above if lax.axis_size("zx") == 2 else shifted(rim, "zx", 1)
     columns = call(columns_kernel, "columns", [(32, LANES)], (node_shift, node_speed, sums), near_ins=(2,), near_outs=(0,))
@@ -584,27 +566,27 @@
         (dest_tile.reshape(1, -1), src_block[0], dest_block[0], crossing[0], keep[0]),
         near_outs=(0,),
     )
-    speed_after, shift_after, late = call(
+    speed_after, shift_after, state = call(
         lagrange_kernel,
         "lagrange",
-        [plane, plane, (devices, (materials + 2) * QUAD + SUB, LANES)],
-        (node_shift, node_speed, sums, above, below, right, left, frac, density, energy, tables),
-        near_ins=(2, 3, 4, 5, 6, 7, 8, 9, 10),
+        [plane, plane, (devices, rows + SUB, LANES)],
+        (
+            node_shift, node_speed, sums, above, below, right, left, frac, density, energy, tables,
+        ),
+        near_ins=(2, 3, 4, 5, 6, 10),
         near_outs=(2,),
     )
-    early, late = lax.optimization_barrier((early, late))
-    late = exchange(late)
+    state = exchange(state)
     groups = devices // SUB
     totals = call(
         crossing_kernel,
         "crossings",
         [(devices, rows, LANES)],
-        (early, late),
-        scratch=[(devices, rows, LANES)]
-        + [(SUB, groups, rows, LANES)] * 2
+        (state,),
+        scratch=[(SUB, groups, rows, LANES)] * 2
         + [(devices, groups, SUB, LANES)]
         + [(groups, groups, SUB, LANES)] * 2,
-        near_ins=(1,),
+        near_ins=(0,),
         near_outs=(0,),
     )
     totals = exchange(totals)

time: 114 us -> 110 us (0.965)
  blocking collectives: 67.6 us -> 83.3 us
  waiting for transfers between devices: 14.6 us -> 5.43 us
  starting transfers between devices: 13.8 us -> 6.43 us
  Pallas kernels: 16.2 us -> 13.9 us
    all_to_all x2, blocking collectives: 67.6 us -> 83.3 us  [exchange(): return lax.all_to_all(value, ('zx', 'zy'), 0, 0, tiled=True)]
    ppermute x3, waiting for transfers between devices: 13.7 us -> 5.43 us  [shifted(): lax.ppermute(value, axis, [(i, (i + by) % peers) for i in range(peers)])]
    all_to_all x1 -> x0, starting transfers between devices: 7.43 us -> none  [exchange(): return lax.all_to_all(value, ('zx', 'zy'), 0, 0, tiled=True)]
    pallas_call x6, Pallas kernels: 14.9 us -> 12.6 us  [call(): pl.pallas_call(kernel, out_shape=shapes if len(shapes) > 1 else shapes[0]...]
  transfers between devices with their start and end apart: 4 -> 3, of which waited for: 4 -> 3; matrix products, arithmetic and copies ran while one was open for 0% -> 0% of each run, Pallas kernels for 5% -> 2%
where the time goes in v6:
time: 110 us
  blocking collectives  83.3 us (76%)
  Pallas kernels  13.9 us (13%)
  starting transfers between devices  6.43 us (6%)
  waiting for transfers between devices  5.43 us (5%)
    all_to_all x2, blocking collectives, exchange(): return lax.all_to_all(value, ('zx', 'zy'), 0, 0, tiled=True)  83.3 us
    pallas_call x6, Pallas kernels, call(): pl.pallas_call(kernel, out_shape=shapes if len(shapes) > 1 else shapes[0]...  12.6 us
    ppermute x3, starting transfers between devices, shifted(): lax.ppermute(value, axis, [(i, (i + by) % peers) for i in range(peers)])  6.43 us
    ppermute x3, waiting for transfers between devices, shifted(): lax.ppermute(value, axis, [(i, (i + by) % peers) for i in range(peers)])  5.43 us
  transfers between devices with their start and end apart: 3, of which 3 were waited for; matrix products, arithmetic and copies ran while one was open for 0% of the time, Pallas kernels for 2%

profile of v6, /device:TPU:0, one launch (start us, length us, event | category | flops | bytes accessed | tf_op | source)
XLA Modules:
  0.0 109.7 jit_solution(15531379146295630476)
XLA Ops:
  0.6 1.5 %sums.1 = (f32[2,64,256]{2,1,0:T(8,128)S(1)}, f32[32,256]{1,0:T(8,128)S(1)}) custom-call(f32[8,64,256]{2,1,0:T(8,128)} %frac_ref.3, f32[8,64,256]{2,1,0:T(8,128)} %density_ref.3, f32[8,64,256]{2,1,0:T(8,128)} %energy_ref.3, f32[2,64,256]{2,1,0:T(8,128)} %now_shift_ref.1, f32[2,64,256]{2,1,0:T(8,128)} %now_speed_ref.1), custom_call_target="tpu_custom_call" | custom-call | tf_op jit(solution)/shard_map/sums/pallas_call | solution.py:517
  2.2 3.0 %collective-permute-start = (f32[32,256]{1,0:T(8,128)S(1)}, f32[32,256]{1,0:T(8,128)S(1)}, u32[]{:S(2)}, u32[]{:S(2)}) collective-permute-start(f32[32,256]{1,0:T(8,128)S(1)} %get-tuple-element.11), channel_id=1, source_target_pairs={{0,16},{16,0},{1,17},{17,1},{2,18},{18,2},{3,19},{19,3},{4,20},{20... | collective-permute-start | bytes 98312 | tf_op jit(solution)/shard_map/ppermute | solution.py:15
  5.2 1.2 %columns.1.columns_ref = f32[32,128]{1,0:T(8,128)S(1)} custom-call(f32[2,64,256]{2,1,0:T(8,128)} %now_shift_ref.1, f32[2,64,256]{2,1,0:T(8,128)} %now_speed_ref.1, f32[2,64,256]{2,1,0:T(8,128)S(1)} %get-tuple-element.10.sums_ref), custom_call_target="tpu_custom_call" | custom-call | tf_op jit(solution)/shard_map/columns/pallas_call | solution.py:517
  6.4 0.7 collective-permute-done.above_ref.below_ref
  7.1 0.1 corners.1
  7.1 3.4 %collective-permute-start.1 = (f32[16,128]{1,0:T(8,128)S(1)}, f32[16,128]{1,0:T(8,128)S(1)}, u32[]{:S(2)}, u32[]{:S(2)}) collective-permute-start(f32[16,128]{1,0:T(8,128)S(1)} %get-tuple-element.12), channel_id=1, source_target_pairs={{0,15},{1,0},{2,1},{3,2},{4,3},{5,4},{6,5},{7,6},{8,7},{9,8},{10,9... | collective-permute-start | bytes 24584 | tf_op jit(solution)/shard_map/ppermute | solution.py:15
  10.6 0.0 collective-permute-start.2
  10.6 1.0 tables.1.tables_ref
  11.6 0.3 collective-permute-done.1.right_ref
  11.9 4.4 %collective-permute-done.2.left_ref = f32[16,128]{1,0:T(8,128)S(1)} collective-permute-done((f32[16,128]{1,0:T(8,128)S(1)}, f32[16,128]{1,0:T(8,128)S(1)}, u32[]{:S(2)}, u32[]{:S(2)}) %collective-permute-start.2) | collective-permute-done | bytes 8224 | tf_op jit(solution)/shard_map/ppermute | solution.py:15
  16.3 3.3 %lagrange.1 = (f32[2,64,256]{2,1,0:T(8,128)}, f32[2,64,256]{2,1,0:T(8,128)}, f32[32,104,128]{2,1,0:T(8,128)S(1)}) custom-call(f32[2,64,256]{2,1,0:T(8,128)} %now_shift_ref.1, f32[2,64,256]{2,1,0:T(8,128)} %now_speed_ref.1, f32[2,64,256]{2,1,0:T(8,128)S(1)} %get-tuple-element.10.sums_ref, f32[32,256]{1,0:T(8,128)S(1)} %collective-permute-done.above_ref.below_ref, ...), custom_call_target="tpu_custom_call" | custom-call | tf_op jit(solution)/shard_map/lagrange/pallas_call | solution.py:517
  19.6 42.9 %all_to_all.10.state_ref = f32[32,104,128]{2,1,0:T(8,128)S(1)} all-to-all(f32[32,104,128]{2,1,0:T(8,128)S(1)} %get-tuple-element.14), channel_id=1, replica_groups=mesh['zx'=2,'zy'=16] {'zx','zy'}, dimensions={0} | all-to-all | bytes 3407872 | tf_op jit(solution)/shard_map/all_to_all | solution.py:528
  62.5 5.5 %crossings.1 = f32[32,96,128]{2,1,0:T(8,128)S(1)} custom-call(f32[32,104,128]{2,1,0:T(8,128)S(1)} %all_to_all.10.state_ref), custom_call_target="tpu_custom_call" | custom-call | tf_op jit(solution)/shard_map/crossings/pallas_call | solution.py:517
  68.0 40.4 %all_to_all.11.sums_ref = f32[32,96,128]{2,1,0:T(8,128)S(1)} all-to-all(f32[32,96,128]{2,1,0:T(8,128)S(1)} %crossings.1), channel_id=1, replica_groups=mesh['zx'=2,'zy'=16] {'zx','zy'}, dimensions={0} | all-to-all | bytes 3145728 | tf_op jit(solution)/shard_map/all_to_all | solution.py:528
  108.4 1.3 %unpack.1 = f32[24,64,256]{2,1,0:T(8,128)} custom-call(f32[32,96,128]{2,1,0:T(8,128)S(1)} %all_to_all.11.sums_ref), custom_call_target="tpu_custom_call" | custom-call | tf_op jit(solution)/shard_map/unpack/pallas_call | solution.py:491
Async XLA Ops:
  2.2 4.9 %collective-permute-start = (f32[32,256]{1,0:T(8,128)S(1)}, f32[32,256]{1,0:T(8,128)S(1)}, u32[]{:S(2)}, u32[]{:S(2)}) collective-permute-start(f32[32,256]{1,0:T(8,128)S(1)} %get-tuple-element.11), channel_id=1, source_target_pairs={{0,16},{16,0},{1,17},{17,1},{2,18},{18,2},{3,19},{19,3},{4,20},{20... | collective-permute-start | bytes 98312 | tf_op jit(solution)/shard_map/ppermute | solution.py:15
  7.1 4.8 %collective-permute-start.1 = (f32[16,128]{1,0:T(8,128)S(1)}, f32[16,128]{1,0:T(8,128)S(1)}, u32[]{:S(2)}, u32[]{:S(2)}) collective-permute-start(f32[16,128]{1,0:T(8,128)S(1)} %get-tuple-element.12), channel_id=1, source_target_pairs={{0,15},{1,0},{2,1},{3,2},{4,3},{5,4},{6,5},{7,6},{8,7},{9,8},{10,9... | collective-permute-start | bytes 24584 | tf_op jit(solution)/shard_map/ppermute | solution.py:15
  10.6 5.8 %collective-permute-start.2 = (f32[16,128]{1,0:T(8,128)S(1)}, f32[16,128]{1,0:T(8,128)S(1)}, u32[]{:S(2)}, u32[]{:S(2)}) collective-permute-start(f32[16,128]{1,0:T(8,128)S(1)} %get-tuple-element.13), channel_id=1, source_target_pairs={{0,1},{1,2},{2,3},{3,4},{4,5},{5,6},{6,7},{7,8},{8,9},{9,10},{10,1... | collective-permute-start | bytes 24584 | tf_op jit(solution)/shard_map/ppermute | solution.py:15

commit v7 on v6

--- a/solution.py
+++ b/solution.py
@@ -183,7 +183,9 @@
     return [float(gamma) for gamma in gammas - np.float32(1.0)]
 
 
-def sums_kernel(frac_ref, density_ref, energy_ref, shift_ref, speed_ref, sums_ref, rim_ref):
+def sums_kernel(
+    frac_ref, density_ref, energy_ref, shift_ref, speed_ref, sums_ref, rim_ref, first_ref, last_ref
+):
     materials = frac_ref.shape[0]
     stiff = stiffness(materials)
     mass = pressure = None
@@ -203,61 +205,34 @@
     for field, value in enumerate((mass, pressure)):
         rim_ref[8 + field : 9 + field, :] = value[0:1]
         rim_ref[24 + field : 25 + field, :] = value[last : last + 1]
-
-
-def columns_kernel(shift_ref, speed_ref, sums_ref, out_ref):
-    height, width = shift_ref.shape[1:]
+    height, width = mass.shape
     lane = lax.broadcasted_iota(jnp.int32, (height, LANES), 1)
     wanted = jnp.zeros((height, LANES), jnp.float32)
-    for field in range(6):
-        ref = (shift_ref, speed_ref, sums_ref)[field // 2]
-        first = ref[field % 2, :, :LANES]
-        last = ref[field % 2, :, width - LANES :]
+    values = [shift_ref[0], shift_ref[1], speed_ref[0], speed_ref[1], mass, pressure]
+    for field, value in enumerate(values):
         row = 2 * field if field < 4 else 4 + field
-        for column in range(2 if field < 4 else 1):
-            moved = pltpu.roll(first, row, 1) if row else first
-            wanted = jnp.where(lane == row + column, moved, wanted)
-        wanted = jnp.where(lane == 16 + row, pltpu.roll(last, 17 + row, 1), wanted)
-    wanted = jnp.concatenate([wanted, jnp.zeros((LANES - height, LANES), jnp.float32)], axis=0)
-    out_ref[...] = wanted.T[0 : out_ref.shape[0]]
-
-
-def corners_kernel(columns_ref, above_ref, below_ref, first_ref, last_ref):
-    height, width = 64, above_ref.shape[1]
-    shape = (16, LANES)
-    lane = lax.broadcasted_iota(jnp.int32, shape, 1)
-    row = lax.broadcasted_iota(jnp.int32, shape, 0)
-    second = (row % 2 == 1) & (row < 8)
-
-    def column(ref, base, at):
-        return jnp.broadcast_to(ref[base : base + 16, at : at + 1], shape)
-
-    def up(value):
-        return pltpu.roll(value, 15, 0)
-
-    def down(value):
-        return pltpu.roll(value, 1, 0)
-
-    left, right = column(above_ref, 0, 0), column(above_ref, 0, 1)
-    value = columns_ref[0:16]
-    value = jnp.where(lane == height, jnp.where(second, down(right), left), value)
-    value = jnp.where(lane == height + 1, jnp.where(second, right, up(left)), value)
-    under = jnp.where(second, column(below_ref, 16, 1), column(below_ref, 16, 0))
-    first_ref[...] = jnp.where(lane == LANES - 1, under, value)
-    end = column(above_ref, 0, width - 1)
-    value = jnp.where(lane == height, end, columns_ref[16:32])
-    value = jnp.where(lane == height + 1, up(end), value)
-    last_ref[...] = jnp.where(lane == LANES - 1, column(below_ref, 16, width - 1), value)
+        moved = value[:, :LANES]
+        moved = pltpu.roll(moved, row, 1) if row else moved
+        ends = (lane == row) | (lane == row + 1) if field < 4 else lane == row
+        wanted = jnp.where(ends, moved, wanted)
+        moved = pltpu.roll(value[:, width - LANES :], 17 + row, 1)
+        wanted = jnp.where(lane == 16 + row, moved, wanted)
+    wanted = jnp.concatenate([wanted, jnp.zeros((LANES - height, LANES), jnp.float32)], axis=0).T
+    first_ref[...], last_ref[...] = wanted[0:16], wanted[16:32]
 
 
 def lagrange_kernel(
     now_shift_ref,
     now_speed_ref,
     sums_ref,
+    left_above_ref,
+    left_below_ref,
+    left_ref,
+    right_ref,
+    right_above_ref,
+    right_below_ref,
     above_ref,
     below_ref,
-    right_ref,
-    left_ref,
     frac_ref,
     density_ref,
     energy_ref,
@@ -270,7 +245,16 @@
     shape = (height + SUB, width + LANES)
     lane = lax.broadcasted_iota(jnp.int32, shape, 1)
     line = lax.broadcasted_iota(jnp.int32, (shape[0], width), 0)
-    sides = [pltpu.roll(ref[...], 1, 1) for ref in (right_ref, left_ref)]
+    side_lane = lax.broadcasted_iota(jnp.int32, (16, LANES), 1)
+    sides = []
+    for ref, above, below in (
+        (right_ref, right_above_ref, right_below_ref),
+        (left_ref, left_above_ref, left_below_ref),
+    ):
+        beyond = jnp.where(
+            side_lane < LANES - 1, pltpu.roll(above[...], height, 1), pltpu.roll(below[...], height, 1)
+        )
+        sides.append(pltpu.roll(jnp.where(side_lane < height, ref[...], beyond), 1, 1))
     sides.append(jnp.zeros((LANES - 32, LANES), jnp.float32))
     sides = jnp.concatenate(sides, axis=0).T[0 : shape[0]]
 
@@ -404,23 +388,25 @@
             weights_ref[octet, a] = jnp.where(valid, weight, 0.0)
             places = [jnp.broadcast_to(place[i : i + 1], spread) for i in range(SUB)]
             for delta, value in enumerate(regroup(places)):
-                places_ref[SUB * octet + delta, a] = value
+                twice = jnp.concatenate([value, value], axis=0)
+                places_ref[SUB * octet + delta, a] = twice.astype(jnp.bfloat16)
 
     def gather(octet, a):
         sources, weights = sources_ref[octet, a].astype(jnp.int32), weights_ref[octet, a]
         index = [jnp.broadcast_to(sources[i : i + 1], spread) for i in range(SUB)]
         weight = [jnp.broadcast_to(weights[i : i + 1], spread) for i in range(SUB)]
-        for first in range(0, tiles, tiles // 2):
-            at = [slice(SUB * tile, SUB * tile + SUB) for tile in range(first, first + tiles // 2)]
-            values = [
-                [take(state_ref[a * SUB + i, rows_of], index[i]) * weight[i] for rows_of in at]
-                for i in range(SUB)
-            ]
-            for tile, rows_of in enumerate(at):
-                for delta, value in enumerate(regroup([value[tile] for value in values])):
-                    slots_ref[octet % 2][delta, a, rows_of] = value
-
-    block = lax.broadcasted_iota(jnp.int32, spread, 0).astype(jnp.float32)
+        at = [slice(SUB * tile, SUB * tile + SUB) for tile in range(tiles)]
+        values = [
+            [take(state_ref[a * SUB + i, rows_of], index[i]) * weight[i] for rows_of in at]
+            for i in range(SUB)
+        ]
+        for tile, rows_of in enumerate(at):
+            for delta, value in enumerate(regroup([value[tile] for value in values])):
+                slots_ref[octet % 2][delta, a, rows_of] = value
+
+    packed = (2 * SUB, LANES)
+    block = lax.broadcasted_iota(jnp.int32, packed, 0).astype(jnp.float32).astype(jnp.bfloat16)
+    one, zero = jnp.ones(packed, jnp.bfloat16), jnp.zeros(packed, jnp.bfloat16)
 
     def scatter(octet, delta):
         target = SUB * octet + delta
@@ -430,15 +416,15 @@
         place = [places_ref[target, a] for a in range(groups)]
         hot = [
             [
-                jnp.where(place[a] == block + float(SUB * tile), 1.0, 0.0)
-                for tile in range(LANES // SUB)
+                jnp.where(place[a] == block + jnp.bfloat16(2 * SUB * tile), one, zero)
+                for tile in range(LANES // SUB // 2)
             ]
             for a in range(groups)
         ]
         hot = jnp.concatenate([jnp.concatenate(column, axis=0) for column in hot], axis=1)
         total = lax.dot_general(
             parts,
-            hot.astype(jnp.bfloat16),
+            hot,
             (((1,), (1,)), ((), ())),
             preferred_element_type=jnp.float32,
         )
@@ -519,13 +505,23 @@
         out_shape=shapes if len(shapes) > 1 else shapes[0],
         in_specs=whole(len(inputs)),
         out_specs=whole(len(shapes)) if len(shapes) > 1 else whole(1)[0],
-        scratch_shapes=[pltpu.VMEM(shape, jnp.float32) for shape in scratch],
+        scratch_shapes=scratch,
         name=name,
     )(*inputs)
 
 
 def exchange(value):
     return lax.all_to_all(value, ("zx", "zy"), 0, 0, tiled=True)
+
+
+def diagonal(value, by_x, by_y):
+    size_x, size_y = lax.axis_size("zx"), lax.axis_size("zy")
+    route = [
+        (a * size_y + b, (a + by_x) % size_x * size_y + (b + by_y) % size_y)
+        for a in range(size_x)
+        for b in range(size_y)
+    ]
+    return lax.ppermute(value, ("zx", "zy"), route)
 
 
 def local(*arguments):
@@ -546,19 +542,21 @@
     fields = 3 * materials
     rows = fields * QUAD
     plane = (2, rows_x, rows_y)
-    sums, rim = call(
+    sums, rim, first, last = call(
         sums_kernel,
         "sums",
-        [plane, (32, rows_y)],
+        [plane, (32, rows_y), (16, LANES), (16, LANES)],
         (frac, density, energy, node_shift, node_speed),
-        near_outs=(0, 1),
-    )
+        near_outs=(0, 1, 2, 3),
+    )
+    right_above, left_above = diagonal(first, -1, -1), diagonal(last, -1, 1)
+    right, left = shifted(first, "zy", -1), shifted(last, "zy", 1)
     above = shifted(rim, "zx", -1)
-    below = above if lax.axis_size("zx") == 2 else shifted(rim, "zx", 1)
-    columns = call(columns_kernel, "columns", [(32, LANES)], (node_shift, node_speed, sums), near_ins=(2,), near_outs=(0,))
-    first, last = call(corners_kernel, "corners", [(16, LANES)] * 2, (columns, above, below), near_ins=(0, 1, 2), near_outs=(0, 1))
-    right = shifted(first, "zy", -1)
-    left = shifted(last, "zy", 1)
+    if lax.axis_size("zx") == 2:
+        below, right_below, left_below = above, right_above, left_above
+    else:
+        below = shifted(rim, "zx", 1)
+        right_below, left_below = diagonal(first, 1, -1), diagonal(last, 1, 1)
     tables = call(
         table_kernel,
         "tables",
@@ -571,9 +569,23 @@
         "lagrange",
         [plane, plane, (devices, rows + SUB, LANES)],
         (
-            node_shift, node_speed, sums, above, below, right, left, frac, density, energy, tables,
+            node_shift,
+            node_speed,
+            sums,
+            left_above,
+            left_below,
+            left,
+            right,
+            right_above,
+            right_below,
+            above,
+            below,
+            frac,
+            density,
+            energy,
+            tables,
         ),
-        near_ins=(2, 3, 4, 5, 6, 10),
+        near_ins=(2, 3, 4, 5, 6, 7, 8, 9, 10, 14),
         near_outs=(2,),
     )
     state = exchange(state)
@@ -583,9 +595,9 @@
         "crossings",
         [(devices, rows, LANES)],
         (state,),
-        scratch=[(SUB, groups, rows, LANES)] * 2
-        + [(devices, groups, SUB, LANES)]
-        + [(groups, groups, SUB, LANES)] * 2,
+        scratch=[pltpu.VMEM((SUB, groups, rows, LANES), jnp.float32)] * 2
+        + [pltpu.VMEM((devices, groups, 2 * SUB, LANES), jnp.bfloat16)]
+        + [pltpu.VMEM((groups, groups, SUB, LANES), jnp.float32)] * 2,
         near_ins=(0,),
         near_outs=(0,),
     )

time: 110 us -> 109 us (level)
  waiting for transfers between devices: 5.43 us -> 0.3 us
  blocking collectives: 83.3 us -> 86.3 us
  starting transfers between devices: 6.43 us -> 9.13 us
  Pallas kernels: 13.9 us -> 12.4 us
    ppermute x0 -> x2, starting transfers between devices: none -> 5.34 us  [diagonal(): return lax.ppermute(value, ('zx', 'zy'), route)]
    ppermute x3, waiting for transfers between devices: 5.43 us -> 0.3 us  [shifted(): lax.ppermute(value, axis, [(i, (i + by) % peers) for i in range(peers)])]
    all_to_all x2, blocking collectives: 83.3 us -> 86.3 us  [exchange(): return lax.all_to_all(value, ('zx', 'zy'), 0, 0, tiled=True)]
    ppermute x3, starting transfers between devices: 6.43 us -> 3.79 us  [shifted(): lax.ppermute(value, axis, [(i, (i + by) % peers) for i in range(peers)])]
    pallas_call x6 -> x4, Pallas kernels: 12.6 us -> 11.1 us  [call(): pl.pallas_call(kernel, out_shape=shapes if len(shapes) > 1 else shapes[0]...]
  transfers between devices with their start and end apart: 3 -> 5, of which waited for: 3 -> 1; matrix products, arithmetic and copies ran while one was open for 0% -> 0% of each run, Pallas kernels for 2% -> 1%
where the time goes in v7:
time: 109 us
  blocking collectives  86.3 us (79%)
  Pallas kernels  12.4 us (11%)
  starting transfers between devices  9.13 us (8%)
    all_to_all x2, blocking collectives, exchange(): return lax.all_to_all(value, ('zx', 'zy'), 0, 0, tiled=True)  86.3 us
    pallas_call x4, Pallas kernels, call(): pl.pallas_call(kernel, out_shape=shapes if len(shapes) > 1 else shapes[0]...  11.1 us
    ppermute x2, starting transfers between devices, diagonal(): return lax.ppermute(value, ('zx', 'zy'), route)  5.34 us
    ppermute x3, starting transfers between devices, shifted(): lax.ppermute(value, axis, [(i, (i + by) % peers) for i in range(peers)])  3.79 us
  transfers between devices with their start and end apart: 5, of which 1 were waited for; matrix products, arithmetic and copies ran while one was open for 0% of the time, Pallas kernels for 1%

profile of v7, /device:TPU:0, one launch (start us, length us, event | category | flops | bytes accessed | tf_op | source)
XLA Modules:
  0.0 108.8 jit_solution(4285258231722776493)
XLA Ops:
  0.6 1.7 %sums.1 = (f32[2,64,256]{2,1,0:T(8,128)S(1)}, f32[32,256]{1,0:T(8,128)S(1)}, f32[16,128]{1,0:T(8,128)S(1)}, f32[16,128]{1,0:T(8,128)S(1)}) custom-call(f32[8,64,256]{2,1,0:T(8,128)} %frac_ref.3, f32[8,64,256]{2,1,0:T(8,128)} %density_ref.3, f32[8,64,256]{2,1,0:T(8,128)} %energy_ref.3, f32[2,64,256]{2,1,0:T(8,128)} %now_shift_ref.1, f32[2,64,256]{2,1,0:T(8,128)} %now_speed_ref.1), custom_call_target="tpu_custom_call" | custom-call | tf_op jit(solution)/shard_map/sums/pallas_call | solution.py:503
  2.3 2.9 %collective-permute-start.4 = (f32[32,256]{1,0:T(8,128)S(1)}, f32[32,256]{1,0:T(8,128)S(1)}, u32[]{:S(2)}, u32[]{:S(2)}) collective-permute-start(f32[32,256]{1,0:T(8,128)S(1)} %get-tuple-element.13), channel_id=1, source_target_pairs={{0,16},{16,0},{1,17},{17,1},{2,18},{18,2},{3,19},{19,3},{4,20},{20... | collective-permute-start | bytes 98312 | tf_op jit(solution)/shard_map/ppermute | solution.py:15
  5.2 0.0 collective-permute-start.1
  5.2 1.8 %collective-permute-start = (f32[16,128]{1,0:T(8,128)S(1)}, f32[16,128]{1,0:T(8,128)S(1)}, u32[]{:S(2)}, u32[]{:S(2)}) collective-permute-start(f32[16,128]{1,0:T(8,128)S(1)} %get-tuple-element.11), channel_id=1, source_target_pairs={{0,17},{1,18},{2,19},{3,20},{4,21},{5,22},{6,23},{7,24},{8,25},{9,... | collective-permute-start | bytes 24584 | tf_op jit(solution)/shard_map/ppermute | solution.py:524
  7.0 3.6 %collective-permute-start.3 = (f32[16,128]{1,0:T(8,128)S(1)}, f32[16,128]{1,0:T(8,128)S(1)}, u32[]{:S(2)}, u32[]{:S(2)}) collective-permute-start(f32[16,128]{1,0:T(8,128)S(1)} %get-tuple-element.12), channel_id=1, source_target_pairs={{0,31},{1,16},{2,17},{3,18},{4,19},{5,20},{6,21},{7,22},{8,23},{9,... | collective-permute-start | bytes 24584 | tf_op jit(solution)/shard_map/ppermute | solution.py:524
  10.6 0.8 collective-permute-start.2
  11.4 1.0 tables.1.tables_ref
  12.5 0.0 collective-permute-done.1.left_ref
  12.5 0.0 collective-permute-done.left_above_ref.left_below_ref
  12.5 0.0 collective-permute-done.3.right_above_ref.right_below_ref
  12.5 0.3 collective-permute-done.2.right_ref
  12.8 0.0 collective-permute-done.4.above_ref.below_ref
  12.8 3.3 %lagrange.1 = (f32[2,64,256]{2,1,0:T(8,128)}, f32[2,64,256]{2,1,0:T(8,128)}, f32[32,104,128]{2,1,0:T(8,128)S(1)}) custom-call(f32[2,64,256]{2,1,0:T(8,128)} %now_shift_ref.1, f32[2,64,256]{2,1,0:T(8,128)} %now_speed_ref.1, f32[2,64,256]{2,1,0:T(8,128)S(1)} %get-tuple-element.10.sums_ref, f32[16,128]{1,0:T(8,128)S(1)} %collective-permute-done.left_above_ref.left_below_ref, ...), custom_call_target="tpu_custom_call" | custom-call | tf_op jit(solution)/shard_map/lagrange/pallas_call | solution.py:503
  16.1 45.9 %all_to_all.10.state_ref = f32[32,104,128]{2,1,0:T(8,128)S(1)} all-to-all(f32[32,104,128]{2,1,0:T(8,128)S(1)} %get-tuple-element.14), channel_id=1, replica_groups=mesh['zx'=2,'zy'=16] {'zx','zy'}, dimensions={0} | all-to-all | bytes 3407872 | tf_op jit(solution)/shard_map/all_to_all | solution.py:514
  61.9 5.1 %crossings.1 = f32[32,96,128]{2,1,0:T(8,128)S(1)} custom-call(f32[32,104,128]{2,1,0:T(8,128)S(1)} %all_to_all.10.state_ref), custom_call_target="tpu_custom_call" | custom-call | tf_op jit(solution)/shard_map/crossings/pallas_call | solution.py:503
  67.0 40.4 %all_to_all.11.sums_ref = f32[32,96,128]{2,1,0:T(8,128)S(1)} all-to-all(f32[32,96,128]{2,1,0:T(8,128)S(1)} %crossings.1), channel_id=1, replica_groups=mesh['zx'=2,'zy'=16] {'zx','zy'}, dimensions={0} | all-to-all | bytes 3145728 | tf_op jit(solution)/shard_map/all_to_all | solution.py:514
  107.4 1.3 %unpack.1 = f32[24,64,256]{2,1,0:T(8,128)} custom-call(f32[32,96,128]{2,1,0:T(8,128)S(1)} %all_to_all.11.sums_ref), custom_call_target="tpu_custom_call" | custom-call | tf_op jit(solution)/shard_map/unpack/pallas_call | solution.py:477
Async XLA Ops:
  2.3 10.5 %collective-permute-start.4 = (f32[32,256]{1,0:T(8,128)S(1)}, f32[32,256]{1,0:T(8,128)S(1)}, u32[]{:S(2)}, u32[]{:S(2)}) collective-permute-start(f32[32,256]{1,0:T(8,128)S(1)} %get-tuple-element.13), channel_id=1, source_target_pairs={{0,16},{16,0},{1,17},{17,1},{2,18},{18,2},{3,19},{19,3},{4,20},{20... | collective-permute-start | bytes 98312 | tf_op jit(solution)/shard_map/ppermute | solution.py:15
  5.2 7.2 %collective-permute-start.1 = (f32[16,128]{1,0:T(8,128)S(1)}, f32[16,128]{1,0:T(8,128)S(1)}, u32[]{:S(2)}, u32[]{:S(2)}) collective-permute-start(f32[16,128]{1,0:T(8,128)S(1)} %get-tuple-element.11), channel_id=1, source_target_pairs={{0,1},{1,2},{2,3},{3,4},{4,5},{5,6},{6,7},{7,8},{8,9},{9,10},{10,1... | collective-permute-start | bytes 24584 | tf_op jit(solution)/shard_map/ppermute | solution.py:15
  5.2 7.2 %collective-permute-start = (f32[16,128]{1,0:T(8,128)S(1)}, f32[16,128]{1,0:T(8,128)S(1)}, u32[]{:S(2)}, u32[]{:S(2)}) collective-permute-start(f32[16,128]{1,0:T(8,128)S(1)} %get-tuple-element.11), channel_id=1, source_target_pairs={{0,17},{1,18},{2,19},{3,20},{4,21},{5,22},{6,23},{7,24},{8,25},{9,... | collective-permute-start | bytes 24584 | tf_op jit(solution)/shard_map/ppermute | solution.py:524
  7.0 5.5 %collective-permute-start.3 = (f32[16,128]{1,0:T(8,128)S(1)}, f32[16,128]{1,0:T(8,128)S(1)}, u32[]{:S(2)}, u32[]{:S(2)}) collective-permute-start(f32[16,128]{1,0:T(8,128)S(1)} %get-tuple-element.12), channel_id=1, source_target_pairs={{0,31},{1,16},{2,17},{3,18},{4,19},{5,20},{6,21},{7,22},{8,23},{9,... | collective-permute-start | bytes 24584 | tf_op jit(solution)/shard_map/ppermute | solution.py:524
  10.6 2.2 %collective-permute-start.2 = (f32[16,128]{1,0:T(8,128)S(1)}, f32[16,128]{1,0:T(8,128)S(1)}, u32[]{:S(2)}, u32[]{:S(2)}) collective-permute-start(f32[16,128]{1,0:T(8,128)S(1)} %get-tuple-element.12), channel_id=1, source_target_pairs={{0,15},{1,0},{2,1},{3,2},{4,3},{5,4},{6,5},{7,6},{8,7},{9,8},{10,9... | collective-permute-start | bytes 24584 | tf_op jit(solution)/shard_map/ppermute | solution.py:15

commit v8 on v7

--- a/solution.py
+++ b/solution.py
@@ -252,27 +252,25 @@
         (left_ref, left_above_ref, left_below_ref),
     ):
         beyond = jnp.where(
-            side_lane < LANES - 1, pltpu.roll(above[...], height, 1), pltpu.roll(below[...], height, 1)
+            side_lane < shape[0] - 1, pltpu.roll(above[...], height, 1), pltpu.roll(below[...], SUB, 1)
         )
-        sides.append(pltpu.roll(jnp.where(side_lane < height, ref[...], beyond), 1, 1))
+        sides.append(jnp.where(side_lane < height, ref[...], beyond))
     sides.append(jnp.zeros((LANES - 32, LANES), jnp.float32))
     sides = jnp.concatenate(sides, axis=0).T[0 : shape[0]]
 
     def extend(field):
         value = (now_shift_ref, now_speed_ref, sums_ref)[field // 2][field % 2]
         value = jnp.concatenate([value, jnp.zeros((SUB, width), jnp.float32)], axis=0)
-        value = pltpu.roll(value, 1, 0)
         at = 2 * field if field < 4 else 4 + field
-        value = jnp.where(line == 0, below_ref[16 + at : 17 + at, :], value)
-        value = jnp.where(line == height + 1, above_ref[at : at + 1, :], value)
+        value = jnp.where(line == shape[0] - 1, below_ref[16 + at : 17 + at, :], value)
+        value = jnp.where(line == height, above_ref[at : at + 1, :], value)
         if field < 4:
-            value = jnp.where(line == height + 2, above_ref[at + 1 : at + 2, :], value)
+            value = jnp.where(line == height + 1, above_ref[at + 1 : at + 2, :], value)
         value = jnp.concatenate([value, jnp.zeros((shape[0], LANES), jnp.float32)], axis=1)
-        value = pltpu.roll(value, 1, 1)
-        value = jnp.where(lane == 0, sides[:, 16 + at : 17 + at], value)
-        value = jnp.where(lane == width + 1, sides[:, at : at + 1], value)
+        value = jnp.where(lane == shape[1] - 1, sides[:, 16 + at : 17 + at], value)
+        value = jnp.where(lane == width, sides[:, at : at + 1], value)
         if field < 4:
-            value = jnp.where(lane == width + 2, sides[:, at + 1 : at + 2], value)
+            value = jnp.where(lane == width + 1, sides[:, at + 1 : at + 2], value)
         return value
 
     def next_row(value):
@@ -324,7 +322,7 @@
     after = 0.5 * (rise_x * cross_y - cross_x * rise_y)
 
     def own(value):
-        return next_column(next_row(value))[0:height, 0:width]
+        return value[0:height, 0:width]
 
     speed_ref[0], speed_ref[1] = own(speed_x), own(speed_y)
     shift_ref[0], shift_ref[1] = own(shift_x), own(shift_y)

time: 109 us -> 109 us (level)
  no operation moved by 1% of the time
where the time goes in v8:
time: 109 us
  blocking collectives  86.3 us (79%)
  Pallas kernels  12.2 us (11%)
  starting transfers between devices  9.13 us (8%)
    all_to_all x2, blocking collectives, exchange(): return lax.all_to_all(value, ('zx', 'zy'), 0, 0, tiled=True)  86.3 us
    pallas_call x4, Pallas kernels, call(): pl.pallas_call(kernel, out_shape=shapes if len(shapes) > 1 else shapes[0]...  10.8 us
    ppermute x2, starting transfers between devices, diagonal(): return lax.ppermute(value, ('zx', 'zy'), route)  5.34 us
    ppermute x3, starting transfers between devices, shifted(): lax.ppermute(value, axis, [(i, (i + by) % peers) for i in range(peers)])  3.79 us
  transfers between devices with their start and end apart: 5, of which 1 were waited for; matrix products, arithmetic and copies ran while one was open for 0% of the time, Pallas kernels for 1%

profile of v8, /device:TPU:0, one launch (start us, length us, event | category | flops | bytes accessed | tf_op | source)
XLA Modules:
  0.0 108.5 jit_solution(12027685971985438240)
XLA Ops:
  0.6 1.7 %sums.1 = (f32[2,64,256]{2,1,0:T(8,128)S(1)}, f32[32,256]{1,0:T(8,128)S(1)}, f32[16,128]{1,0:T(8,128)S(1)}, f32[16,128]{1,0:T(8,128)S(1)}) custom-call(f32[8,64,256]{2,1,0:T(8,128)} %frac_ref.3, f32[8,64,256]{2,1,0:T(8,128)} %density_ref.3, f32[8,64,256]{2,1,0:T(8,128)} %energy_ref.3, f32[2,64,256]{2,1,0:T(8,128)} %now_shift_ref.1, f32[2,64,256]{2,1,0:T(8,128)} %now_speed_ref.1), custom_call_target="tpu_custom_call" | custom-call | tf_op jit(solution)/shard_map/sums/pallas_call | solution.py:501
  2.3 2.9 %collective-permute-start.4 = (f32[32,256]{1,0:T(8,128)S(1)}, f32[32,256]{1,0:T(8,128)S(1)}, u32[]{:S(2)}, u32[]{:S(2)}) collective-permute-start(f32[32,256]{1,0:T(8,128)S(1)} %get-tuple-element.13), channel_id=1, source_target_pairs={{0,16},{16,0},{1,17},{17,1},{2,18},{18,2},{3,19},{19,3},{4,20},{20... | collective-permute-start | bytes 98312 | tf_op jit(solution)/shard_map/ppermute | solution.py:15
  5.2 0.0 collective-permute-start.1
  5.2 1.8 %collective-permute-start = (f32[16,128]{1,0:T(8,128)S(1)}, f32[16,128]{1,0:T(8,128)S(1)}, u32[]{:S(2)}, u32[]{:S(2)}) collective-permute-start(f32[16,128]{1,0:T(8,128)S(1)} %get-tuple-element.11), channel_id=1, source_target_pairs={{0,17},{1,18},{2,19},{3,20},{4,21},{5,22},{6,23},{7,24},{8,25},{9,... | collective-permute-start | bytes 24584 | tf_op jit(solution)/shard_map/ppermute | solution.py:522
  7.0 3.6 %collective-permute-start.3 = (f32[16,128]{1,0:T(8,128)S(1)}, f32[16,128]{1,0:T(8,128)S(1)}, u32[]{:S(2)}, u32[]{:S(2)}) collective-permute-start(f32[16,128]{1,0:T(8,128)S(1)} %get-tuple-element.12), channel_id=1, source_target_pairs={{0,31},{1,16},{2,17},{3,18},{4,19},{5,20},{6,21},{7,22},{8,23},{9,... | collective-permute-start | bytes 24584 | tf_op jit(solution)/shard_map/ppermute | solution.py:522
  10.6 0.8 collective-permute-start.2
  11.4 1.0 tables.1.tables_ref
  12.5 0.0 collective-permute-done.1.left_ref
  12.5 0.0 collective-permute-done.left_above_ref.left_below_ref
  12.5 0.0 collective-permute-done.3.right_above_ref.right_below_ref
  12.5 0.3 collective-permute-done.2.right_ref
  12.8 0.0 collective-permute-done.4.above_ref.below_ref
  12.8 3.0 %lagrange.1 = (f32[2,64,256]{2,1,0:T(8,128)}, f32[2,64,256]{2,1,0:T(8,128)}, f32[32,104,128]{2,1,0:T(8,128)S(1)}) custom-call(f32[2,64,256]{2,1,0:T(8,128)} %now_shift_ref.1, f32[2,64,256]{2,1,0:T(8,128)} %now_speed_ref.1, f32[2,64,256]{2,1,0:T(8,128)S(1)} %get-tuple-element.10.sums_ref, f32[16,128]{1,0:T(8,128)S(1)} %collective-permute-done.left_above_ref.left_below_ref, ...), custom_call_target="tpu_custom_call" | custom-call | tf_op jit(solution)/shard_map/lagrange/pallas_call | solution.py:501
  15.8 45.9 %all_to_all.10.state_ref = f32[32,104,128]{2,1,0:T(8,128)S(1)} all-to-all(f32[32,104,128]{2,1,0:T(8,128)S(1)} %get-tuple-element.14), channel_id=1, replica_groups=mesh['zx'=2,'zy'=16] {'zx','zy'}, dimensions={0} | all-to-all | bytes 3407872 | tf_op jit(solution)/shard_map/all_to_all | solution.py:512
  61.7 5.1 %crossings.1 = f32[32,96,128]{2,1,0:T(8,128)S(1)} custom-call(f32[32,104,128]{2,1,0:T(8,128)S(1)} %all_to_all.10.state_ref), custom_call_target="tpu_custom_call" | custom-call | tf_op jit(solution)/shard_map/crossings/pallas_call | solution.py:501
  66.8 40.4 %all_to_all.11.sums_ref = f32[32,96,128]{2,1,0:T(8,128)S(1)} all-to-all(f32[32,96,128]{2,1,0:T(8,128)S(1)} %crossings.1), channel_id=1, replica_groups=mesh['zx'=2,'zy'=16] {'zx','zy'}, dimensions={0} | all-to-all | bytes 3145728 | tf_op jit(solution)/shard_map/all_to_all | solution.py:512
  107.2 1.3 %unpack.1 = f32[24,64,256]{2,1,0:T(8,128)} custom-call(f32[32,96,128]{2,1,0:T(8,128)S(1)} %all_to_all.11.sums_ref), custom_call_target="tpu_custom_call" | custom-call | tf_op jit(solution)/shard_map/unpack/pallas_call | solution.py:475
Async XLA Ops:
  2.3 10.5 %collective-permute-start.4 = (f32[32,256]{1,0:T(8,128)S(1)}, f32[32,256]{1,0:T(8,128)S(1)}, u32[]{:S(2)}, u32[]{:S(2)}) collective-permute-start(f32[32,256]{1,0:T(8,128)S(1)} %get-tuple-element.13), channel_id=1, source_target_pairs={{0,16},{16,0},{1,17},{17,1},{2,18},{18,2},{3,19},{19,3},{4,20},{20... | collective-permute-start | bytes 98312 | tf_op jit(solution)/shard_map/ppermute | solution.py:15
  5.2 7.2 %collective-permute-start.1 = (f32[16,128]{1,0:T(8,128)S(1)}, f32[16,128]{1,0:T(8,128)S(1)}, u32[]{:S(2)}, u32[]{:S(2)}) collective-permute-start(f32[16,128]{1,0:T(8,128)S(1)} %get-tuple-element.11), channel_id=1, source_target_pairs={{0,1},{1,2},{2,3},{3,4},{4,5},{5,6},{6,7},{7,8},{8,9},{9,10},{10,1... | collective-permute-start | bytes 24584 | tf_op jit(solution)/shard_map/ppermute | solution.py:15
  5.2 7.2 %collective-permute-start = (f32[16,128]{1,0:T(8,128)S(1)}, f32[16,128]{1,0:T(8,128)S(1)}, u32[]{:S(2)}, u32[]{:S(2)}) collective-permute-start(f32[16,128]{1,0:T(8,128)S(1)} %get-tuple-element.11), channel_id=1, source_target_pairs={{0,17},{1,18},{2,19},{3,20},{4,21},{5,22},{6,23},{7,24},{8,25},{9,... | collective-permute-start | bytes 24584 | tf_op jit(solution)/shard_map/ppermute | solution.py:522
  7.0 5.5 %collective-permute-start.3 = (f32[16,128]{1,0:T(8,128)S(1)}, f32[16,128]{1,0:T(8,128)S(1)}, u32[]{:S(2)}, u32[]{:S(2)}) collective-permute-start(f32[16,128]{1,0:T(8,128)S(1)} %get-tuple-element.12), channel_id=1, source_target_pairs={{0,31},{1,16},{2,17},{3,18},{4,19},{5,20},{6,21},{7,22},{8,23},{9,... | collective-permute-start | bytes 24584 | tf_op jit(solution)/shard_map/ppermute | solution.py:522
  10.6 2.2 %collective-permute-start.2 = (f32[16,128]{1,0:T(8,128)S(1)}, f32[16,128]{1,0:T(8,128)S(1)}, u32[]{:S(2)}, u32[]{:S(2)}) collective-permute-start(f32[16,128]{1,0:T(8,128)S(1)} %get-tuple-element.12), channel_id=1, source_target_pairs={{0,15},{1,0},{2,1},{3,2},{4,3},{5,4},{6,5},{7,6},{8,7},{9,8},{10,9... | collective-permute-start | bytes 24584 | tf_op jit(solution)/shard_map/ppermute | solution.py:15

commit v9 on v8

--- a/solution.py
+++ b/solution.py
@@ -243,8 +243,8 @@
 ):
     height, width = sums_ref.shape[1:]
     shape = (height + SUB, width + LANES)
-    lane = lax.broadcasted_iota(jnp.int32, shape, 1)
-    line = lax.broadcasted_iota(jnp.int32, (shape[0], width), 0)
+    lane = lax.broadcasted_iota(jnp.int32, (shape[0], LANES), 1)
+    line = lax.broadcasted_iota(jnp.int32, (SUB, width), 0)
     side_lane = lax.broadcasted_iota(jnp.int32, (16, LANES), 1)
     sides = []
     for ref, above, below in (
@@ -260,17 +260,15 @@
 
     def extend(field):
         value = (now_shift_ref, now_speed_ref, sums_ref)[field // 2][field % 2]
-        value = jnp.concatenate([value, jnp.zeros((SUB, width), jnp.float32)], axis=0)
         at = 2 * field if field < 4 else 4 + field
-        value = jnp.where(line == shape[0] - 1, below_ref[16 + at : 17 + at, :], value)
-        value = jnp.where(line == height, above_ref[at : at + 1, :], value)
+        edge = jnp.where(line == SUB - 1, below_ref[16 + at : 17 + at, :], above_ref[at : at + 1, :])
         if field < 4:
-            value = jnp.where(line == height + 1, above_ref[at + 1 : at + 2, :], value)
-        value = jnp.concatenate([value, jnp.zeros((shape[0], LANES), jnp.float32)], axis=1)
-        value = jnp.where(lane == shape[1] - 1, sides[:, 16 + at : 17 + at], value)
-        value = jnp.where(lane == width, sides[:, at : at + 1], value)
+            edge = jnp.where(line == 1, above_ref[at + 1 : at + 2, :], edge)
+        value = jnp.concatenate([value, edge], axis=0)
+        edge = jnp.where(lane == LANES - 1, sides[:, 16 + at : 17 + at], sides[:, at : at + 1])
         if field < 4:
-            value = jnp.where(lane == width + 1, sides[:, at + 1 : at + 2], value)
+            edge = jnp.where(lane == 1, sides[:, at + 1 : at + 2], edge)
+        value = jnp.concatenate([value, edge], axis=1)
         return value
 
     def next_row(value):

time: 109 us -> 109 us (level)
  no operation moved by 1% of the time
where the time goes in v9:
time: 109 us
  blocking collectives  86.2 us (79%)
  Pallas kernels  12.2 us (11%)
  starting transfers between devices  9.13 us (8%)
    all_to_all x2, blocking collectives, exchange(): return lax.all_to_all(value, ('zx', 'zy'), 0, 0, tiled=True)  86.2 us
    pallas_call x4, Pallas kernels, call(): pl.pallas_call(kernel, out_shape=shapes if len(shapes) > 1 else shapes[0]...  10.8 us
    ppermute x2, starting transfers between devices, diagonal(): return lax.ppermute(value, ('zx', 'zy'), route)  5.34 us
    ppermute x3, starting transfers between devices, shifted(): lax.ppermute(value, axis, [(i, (i + by) % peers) for i in range(peers)])  3.79 us
  transfers between devices with their start and end apart: 5, of which 1 were waited for; matrix products, arithmetic and copies ran while one was open for 0% of the time, Pallas kernels for 1%

profile of v9, /device:TPU:0, one launch (start us, length us, event | category | flops | bytes accessed | tf_op | source)
XLA Modules:
  0.0 108.5 jit_solution(15780019880520152130)
XLA Ops:
  0.6 1.7 %sums.1 = (f32[2,64,256]{2,1,0:T(8,128)S(1)}, f32[32,256]{1,0:T(8,128)S(1)}, f32[16,128]{1,0:T(8,128)S(1)}, f32[16,128]{1,0:T(8,128)S(1)}) custom-call(f32[8,64,256]{2,1,0:T(8,128)} %frac_ref.3, f32[8,64,256]{2,1,0:T(8,128)} %density_ref.3, f32[8,64,256]{2,1,0:T(8,128)} %energy_ref.3, f32[2,64,256]{2,1,0:T(8,128)} %now_shift_ref.1, f32[2,64,256]{2,1,0:T(8,128)} %now_speed_ref.1), custom_call_target="tpu_custom_call" | custom-call | tf_op jit(solution)/shard_map/sums/pallas_call | solution.py:499
  2.3 2.9 %collective-permute-start.4 = (f32[32,256]{1,0:T(8,128)S(1)}, f32[32,256]{1,0:T(8,128)S(1)}, u32[]{:S(2)}, u32[]{:S(2)}) collective-permute-start(f32[32,256]{1,0:T(8,128)S(1)} %get-tuple-element.13), channel_id=1, source_target_pairs={{0,16},{16,0},{1,17},{17,1},{2,18},{18,2},{3,19},{19,3},{4,20},{20... | collective-permute-start | bytes 98312 | tf_op jit(solution)/shard_map/ppermute | solution.py:15
  5.2 0.0 collective-permute-start.1
  5.2 1.8 %collective-permute-start = (f32[16,128]{1,0:T(8,128)S(1)}, f32[16,128]{1,0:T(8,128)S(1)}, u32[]{:S(2)}, u32[]{:S(2)}) collective-permute-start(f32[16,128]{1,0:T(8,128)S(1)} %get-tuple-element.11), channel_id=1, source_target_pairs={{0,17},{1,18},{2,19},{3,20},{4,21},{5,22},{6,23},{7,24},{8,25},{9,... | collective-permute-start | bytes 24584 | tf_op jit(solution)/shard_map/ppermute | solution.py:520
  7.0 3.6 %collective-permute-start.3 = (f32[16,128]{1,0:T(8,128)S(1)}, f32[16,128]{1,0:T(8,128)S(1)}, u32[]{:S(2)}, u32[]{:S(2)}) collective-permute-start(f32[16,128]{1,0:T(8,128)S(1)} %get-tuple-element.12), channel_id=1, source_target_pairs={{0,31},{1,16},{2,17},{3,18},{4,19},{5,20},{6,21},{7,22},{8,23},{9,... | collective-permute-start | bytes 24584 | tf_op jit(solution)/shard_map/ppermute | solution.py:520
  10.6 0.8 collective-permute-start.2
  11.4 1.0 tables.1.tables_ref
  12.5 0.0 collective-permute-done.1.left_ref
  12.5 0.0 collective-permute-done.left_above_ref.left_below_ref
  12.5 0.0 collective-permute-done.3.right_above_ref.right_below_ref
  12.5 0.3 collective-permute-done.2.right_ref
  12.8 0.0 collective-permute-done.4.above_ref.below_ref
  12.8 3.0 %lagrange.1 = (f32[2,64,256]{2,1,0:T(8,128)}, f32[2,64,256]{2,1,0:T(8,128)}, f32[32,104,128]{2,1,0:T(8,128)S(1)}) custom-call(f32[2,64,256]{2,1,0:T(8,128)} %now_shift_ref.1, f32[2,64,256]{2,1,0:T(8,128)} %now_speed_ref.1, f32[2,64,256]{2,1,0:T(8,128)S(1)} %get-tuple-element.10.sums_ref, f32[16,128]{1,0:T(8,128)S(1)} %collective-permute-done.left_above_ref.left_below_ref, ...), custom_call_target="tpu_custom_call" | custom-call | tf_op jit(solution)/shard_map/lagrange/pallas_call | solution.py:499
  15.8 45.9 %all_to_all.10.state_ref = f32[32,104,128]{2,1,0:T(8,128)S(1)} all-to-all(f32[32,104,128]{2,1,0:T(8,128)S(1)} %get-tuple-element.14), channel_id=1, replica_groups=mesh['zx'=2,'zy'=16] {'zx','zy'}, dimensions={0} | all-to-all | bytes 3407872 | tf_op jit(solution)/shard_map/all_to_all | solution.py:510
  61.7 5.1 %crossings.1 = f32[32,96,128]{2,1,0:T(8,128)S(1)} custom-call(f32[32,104,128]{2,1,0:T(8,128)S(1)} %all_to_all.10.state_ref), custom_call_target="tpu_custom_call" | custom-call | tf_op jit(solution)/shard_map/crossings/pallas_call | solution.py:499
  66.8 40.4 %all_to_all.11.sums_ref = f32[32,96,128]{2,1,0:T(8,128)S(1)} all-to-all(f32[32,96,128]{2,1,0:T(8,128)S(1)} %crossings.1), channel_id=1, replica_groups=mesh['zx'=2,'zy'=16] {'zx','zy'}, dimensions={0} | all-to-all | bytes 3145728 | tf_op jit(solution)/shard_map/all_to_all | solution.py:510
  107.2 1.3 %unpack.1 = f32[24,64,256]{2,1,0:T(8,128)} custom-call(f32[32,96,128]{2,1,0:T(8,128)S(1)} %all_to_all.11.sums_ref), custom_call_target="tpu_custom_call" | custom-call | tf_op jit(solution)/shard_map/unpack/pallas_call | solution.py:473
Async XLA Ops:
  2.3 10.5 %collective-permute-start.4 = (f32[32,256]{1,0:T(8,128)S(1)}, f32[32,256]{1,0:T(8,128)S(1)}, u32[]{:S(2)}, u32[]{:S(2)}) collective-permute-start(f32[32,256]{1,0:T(8,128)S(1)} %get-tuple-element.13), channel_id=1, source_target_pairs={{0,16},{16,0},{1,17},{17,1},{2,18},{18,2},{3,19},{19,3},{4,20},{20... | collective-permute-start | bytes 98312 | tf_op jit(solution)/shard_map/ppermute | solution.py:15
  5.2 7.2 %collective-permute-start.1 = (f32[16,128]{1,0:T(8,128)S(1)}, f32[16,128]{1,0:T(8,128)S(1)}, u32[]{:S(2)}, u32[]{:S(2)}) collective-permute-start(f32[16,128]{1,0:T(8,128)S(1)} %get-tuple-element.11), channel_id=1, source_target_pairs={{0,1},{1,2},{2,3},{3,4},{4,5},{5,6},{6,7},{7,8},{8,9},{9,10},{10,1... | collective-permute-start | bytes 24584 | tf_op jit(solution)/shard_map/ppermute | solution.py:15
  5.2 7.2 %collective-permute-start = (f32[16,128]{1,0:T(8,128)S(1)}, f32[16,128]{1,0:T(8,128)S(1)}, u32[]{:S(2)}, u32[]{:S(2)}) collective-permute-start(f32[16,128]{1,0:T(8,128)S(1)} %get-tuple-element.11), channel_id=1, source_target_pairs={{0,17},{1,18},{2,19},{3,20},{4,21},{5,22},{6,23},{7,24},{8,25},{9,... | collective-permute-start | bytes 24584 | tf_op jit(solution)/shard_map/ppermute | solution.py:520
  7.0 5.5 %collective-permute-start.3 = (f32[16,128]{1,0:T(8,128)S(1)}, f32[16,128]{1,0:T(8,128)S(1)}, u32[]{:S(2)}, u32[]{:S(2)}) collective-permute-start(f32[16,128]{1,0:T(8,128)S(1)} %get-tuple-element.12), channel_id=1, source_target_pairs={{0,31},{1,16},{2,17},{3,18},{4,19},{5,20},{6,21},{7,22},{8,23},{9,... | collective-permute-start | bytes 24584 | tf_op jit(solution)/shard_map/ppermute | solution.py:520
  10.6 2.2 %collective-permute-start.2 = (f32[16,128]{1,0:T(8,128)S(1)}, f32[16,128]{1,0:T(8,128)S(1)}, u32[]{:S(2)}, u32[]{:S(2)}) collective-permute-start(f32[16,128]{1,0:T(8,128)S(1)} %get-tuple-element.12), channel_id=1, source_target_pairs={{0,15},{1,0},{2,1},{3,2},{4,3},{5,4},{6,5},{7,6},{8,7},{9,8},{10,9... | collective-permute-start | bytes 24584 | tf_op jit(solution)/shard_map/ppermute | solution.py:15
